TPU v7x, 256 devices: a whole 4x4x8 slice. The times are simulated.
256 devices in a mesh: row: 4 (over y), col: 16 (over x, z_hi), rep: 4 (over z_lo, core).
Axes of the slice: x: 4, y: 4, z: 8 (z_hi: 4, z_lo: 2; z = z_hi * 2 + z_lo), core: 2. Of those that a mesh axis runs over, the one named last changes fastest.
Arguments:
- a_weights: bfloat16 [4, 4096, 2048], P('rep', 'row', 'col'), may hold values from 0 to 10000, as said below
- a_flags: int32 [4, 32, 16], P('rep', 'row', 'col'), may hold values 0 or 1
- b_weights: bfloat16 [4, 2048, 32768], P('rep', 'row', 'col'), may hold values from 0 to 10000, as said below
- b_flags: int32 [4, 16, 256], P('rep', 'row', 'col'), may hold values 0 or 1
- out_flags: int32 [32, 256], P('row', ('col', 'rep')), may hold values 0 or 1
Outputs:
- two_hop: bfloat16 [4096, 32768], P('row', ('col', 'rep'))
Inputs may be any that keep to these rules, and one draw needn't show every extreme that they name: `a_weights`: positive edge weights. `b_weights`: positive edge weights.
All inputs are finite; a program needn't handle non-finite values. No bound on the sum of `a_flags` or of `b_flags` or of `out_flags` on one device may be relied on, other than what follows from the above.
Results may differ from a plain program's by a relative error of at most 0.012.
Values may be sent and summed in bfloat16 or wider, within the bound.
No kernel may reach another device: no remote copies, remote signals or barrier semaphores. Data moves between devices by JAX's collectives and lax.ppermute only.
A program may use at most 64 MiB of HBM per device.

v0:
```python
import jax
import jax.numpy as jnp
from jax import lax
from jax.sharding import PartitionSpec as P


def expand(flags, width):
    return jnp.repeat(jnp.repeat(flags, width, axis=-2), width, axis=-1)


def shards(a_weights, a_flags, b_weights, b_flags, out_flags):
    width = a_weights.shape[1] // a_flags.shape[1]
    a_masked = a_weights * expand(a_flags, width).astype(jnp.bfloat16)
    b_masked = b_weights * expand(b_flags, width).astype(jnp.bfloat16)
    deg_a = 1.0 + lax.psum(jnp.sum(a_masked, axis=(0, 2), dtype=jnp.float32), ("col", "rep"))
    walk_local = (a_masked.astype(jnp.float32) / deg_a[None, :, None]).astype(jnp.bfloat16)
    walk_a = lax.all_gather(walk_local, "col", axis=2, tiled=True)
    deg_b = 1.0 + lax.psum(jnp.sum(b_masked, axis=2, dtype=jnp.float32), "col")
    walk_b = (b_masked.astype(jnp.float32) / deg_b[:, :, None]).astype(jnp.bfloat16)
    left_rows = walk_a[0]
    partial_sum = jnp.dot(
        left_rows,
        lax.all_gather(walk_b, "row", axis=1, tiled=True)[0],
        preferred_element_type=jnp.float32,
    )
    summed = lax.psum_scatter(
        partial_sum.astype(jnp.bfloat16), "rep", scatter_dimension=1, tiled=True
    ).astype(jnp.float32)
    factor = jnp.float32(b_weights.shape[2] * lax.axis_size("col"))
    return (factor * summed * expand(out_flags, width).astype(jnp.float32)).astype(jnp.bfloat16)


def solution(mesh):
    return jax.shard_map(
        shards,
        mesh=mesh,
        in_specs=(
            P("rep", "row", "col"),
            P("rep", "row", "col"),
            P("rep", "row", "col"),
            P("rep", "row", "col"),
            P("row", ("col", "rep")),
        ),
        out_specs=P("row", ("col", "rep")),
        check_vma=False,
    )
```

profile of v0, /device:TPU:1, one launch (start us, length us, event | category | flops | bytes accessed | tf_op | source)
XLA Modules:
  0.0 379.0 jit_solution(2328880365797852931)
XLA Ops:
  6.5 0.0 all-gather.3.cloned.1.call-start
  6.5 0.7 convert_bitcast_fusion.1
  7.2 0.1 broadcast_bitcast_fusion
  7.3 1.3 convert_reduce_fusion.1
  8.6 128.0 %psum.14 = f32[1024]{0:T(1024)S(1)} all-reduce(f32[1024]{0:T(1024)S(1)} %convert_reduce_fusion.1), channel_id=1, replica_groups=mesh['row'=4,'col'=16,'rep'=4] {'col','rep'}, use_global_device_ids=true, to_apply=%region_1.0 | all-reduce | flops 1024 | bytes 8192 | tf_op jit(solution)/shard_map/psum | solution.py:15
  136.6 2.0 fusion.10
  138.6 0.0 all-gather.3.cloned.1.call-update
  138.6 0.0 all-gather.5.cloned.1.call-start
  138.7 0.7 convert_bitcast_fusion
  139.4 2.3 broadcast_in_dim.20
  141.7 2.8 convert_element_type.80
  144.5 2.2 convert_reduce_fusion
  146.7 33.6 %psum.15 = f32[1,512]{1,0:T(1,128)S(1)} all-reduce(f32[1,512]{1,0:T(1,128)S(1)} %bitcast.29), channel_id=1, replica_groups=mesh['row'=4,'col'=16,'rep'=4] {'col'}, use_global_device_ids=true, to_apply=%region_3.0 | all-reduce | flops 512 | bytes 4096 | tf_op jit(solution)/shard_map/psum | solution.py:18
  180.3 3.9 %fusion.2 = bf16[1,512,2048]{2,1,0:T(8,128)(2,1)} fusion(f32[512]{0:T(512)S(1)} %bitcast.28, bf16[1,512,2048]{2,1,0:T(8,128)(2,1)} %param.7, bf16[1,512,2048]{2,1,0:T(8,128)(2,1)S(1)} %convert_element_type.80), kind=kLoop, calls=%fused_computation.4 | loop fusion | flops 4194304 | bytes 6293504 | tf_op jit(solution)/shard_map/convert_element_type | solution.py:19
  184.2 0.0 all-gather.5.cloned.1.call-update
  184.2 0.0 reduce-scatter.2.cloned.1.call-start
  184.3 36.4 %all-gather.3.cloned.1.call-done = bf16[1,1024,2048]{2,1,0:T(8,128)(2,1)} async-done(((bf16[1,1024,128]{2,1,0:T(8,128)(2,1)}), bf16[1,1024,2048]{2,1,0:T(8,128)(2,1)}) %all-gather.3.cloned.1.call-update) | async-done | bytes 4194320 | tf_op jit(solution)/shard_map/all_gather | solution.py:17
  220.6 86.0 %all-gather.5.cloned.1.call-done = bf16[1,2048,2048]{2,1,0:T(8,128)(2,1)} async-done(((bf16[1,512,2048]{2,1,0:T(8,128)(2,1)}), bf16[1,2048,2048]{2,1,0:T(8,128)(2,1)}) %all-gather.5.cloned.1.call-update) | async-done | bytes 8388624 | tf_op jit(solution)/shard_map/all_gather | solution.py:23
  306.6 13.8 %fusion.4 = bf16[1024,2048]{1,0:T(8,128)(2,1)} fusion(bf16[1,2048,2048]{2,1,0:T(8,128)(2,1)} %all-gather.5.cloned.1.call-done, bf16[1,1024,2048]{2,1,0:T(8,128)(2,1)} %all-gather.3.cloned.1.call-done), kind=kOutput, calls=%fused_computation.6 | convolution fusion | flops 8592031744 | bytes 16777216 | tf_op jit(solution)/shard_map/dot_general | solution.py:21
  320.4 0.0 copy-start.1
  320.4 0.0 reduce-scatter.2.cloned.1.call-update
  320.4 0.7 copy-done.1
  321.1 0.1 copy.6
  321.2 48.7 %reduce-scatter.2.cloned.1.call-done = bf16[1024,512]{1,0:T(8,128)(2,1)} async-done(((bf16[1024,2048]{1,0:T(8,128)(2,1)}), bf16[1024,512]{1,0:T(8,128)(2,1)}) %reduce-scatter.2.cloned.1.call-update) | async-done | bytes 1048592 | tf_op jit(solution)/shard_map/reduce_scatter | solution.py:26
  369.8 0.0 copy-start
  369.9 1.2 broadcast_in_dim.22
  371.1 0.0 copy-done
  371.1 1.4 fusion.9
  (5 shorter events, 0.1 us)
Async XLA Ops:
  6.5 214.1 %all-gather.3.cloned.1.call-start = ((), (), s32[]{:S(2)}) async-start(), calls=%async_computation.1 | async-start | bytes 4456448 | tf_op jit(solution)/shard_map/all_gather | solution.py:17
  138.6 168.0 %all-gather.5.cloned.1.call-start = ((), (), s32[]{:S(2)}) async-start(), calls=%async_computation.2 | async-start | bytes 10485760 | tf_op jit(solution)/shard_map/all_gather | solution.py:23
  184.2 185.6 %reduce-scatter.2.cloned.1.call-start = ((), (), s32[]{:S(2)}) async-start(), calls=%async_computation.3 | async-start | bytes 5242880 | tf_op jit(solution)/shard_map/reduce_scatter | solution.py:26
  320.4 0.7 copy-start.1
  369.8 1.3 copy-start
Sparse Core Ops, SparseCore 0:
  138.7 81.8 all-gather.2
  222.4 84.1 all-gather.4
  320.6 49.2 reduce-scatter.1
where the time goes:
time: 379 us
  waiting for transfers between devices  171 us (45%)
  blocking collectives  162 us (43%)
  matrix products  13.8 us (4%)
  between operations  13.1 us (3%)
  other arithmetic  12.1 us (3%)
  local copies, waits for them, and re-layouts  7.21 us (2%)
    psum x1, blocking collectives, shards(): lax.psum(jnp.sum(a_masked, axis=(0, 2), dtype=jnp.float32), ('col', 'rep'))  128 us
    all_gather x1, waiting for transfers between devices, shards(): lax.all_gather(walk_b, 'row', axis=1, tiled=True)[0]  86 us
    reduce_scatter x1, waiting for transfers between devices, shards(): lax.psum_scatter(partial_sum.astype(jnp.bfloat16), 'rep', scatter_dimensi...  48.7 us
    all_gather x1, waiting for transfers between devices, shards(): walk_a = lax.all_gather(walk_local, 'col', axis=2, tiled=True)  36.4 us
    psum x1, blocking collectives, shards(): deg_b = 1.0 + lax.psum(jnp.sum(b_masked, axis=2, dtype=jnp.float32), 'col')  33.6 us
    dot_general x1, matrix products, shards(): jnp.dot(left_rows, lax.all_gather(walk_b, 'row', axis=1, tiled=True)[0],...  13.8 us
  transfers between devices with their start and end apart: 3, of which 3 were waited for; matrix products, arithmetic and copies ran while one was open for 3% of the time, Pallas kernels for 0%

commit v1 on v0

v1 whole, which is shorter than its diff:
```python
import functools

import jax
import jax.numpy as jnp
from jax import lax
from jax.experimental import pallas as pl
from jax.experimental.pallas import tpu as pltpu
from jax.sharding import PartitionSpec as P

TILE = 128
F32, BF16 = jnp.float32, jnp.bfloat16
TURN = (1, -1, 1, -1)
ROWS = {h: [(4 * y + r, 4 * ((y + h * TURN[r]) % 4) + r) for y in range(4) for r in range(4)] for h in (1, 2, 3)}
ALONG_X = [
    (16 * x + 4 * z + r, 16 * ((x + TURN[r]) % 4) + 4 * z + r)
    for x in range(4) for z in range(4) for r in range(4)
]
ALONG_Z = [
    (16 * x + 4 * z + r, 16 * x + 4 * ((z + TURN[r]) % 4) + r)
    for x in range(4) for z in range(4) for r in range(4)
]
SWAP = {k: [(i, i ^ k) for i in range(4)] for k in (1, 2)}
COLS = {k: [(i, i ^ k) for i in range(16)] for k in (1, 2, 4, 8)}


def prep_kernel(rep_ref, flags_ref, b_ref, o_ref, *, chunk):
    p = pl.program_id(0)
    q = (p >> 1) | ((p & 1) << 1)
    column = (rep_ref[0] ^ q) * 4 + chunk
    for k in range(4):
        rows = pl.ds(TILE * k, TILE)
        on = flags_ref[k, column] != 0
        o_ref[rows, :] = jnp.where(on, b_ref[rows, :], jnp.zeros((TILE, TILE), BF16))


def prep(rep, flags, b, chunk):
    def source(p, rep_ref, flags_ref):
        q = (p >> 1) | ((p & 1) << 1)
        return 0, (rep_ref[0] ^ q) * 4 + chunk

    return pl.pallas_call(
        functools.partial(prep_kernel, chunk=chunk),
        grid_spec=pltpu.PrefetchScalarGridSpec(
            num_scalar_prefetch=2,
            grid=(4,),
            in_specs=[pl.BlockSpec((512, TILE), source)],
            out_specs=pl.BlockSpec((512, TILE), lambda p, rep_ref, flags_ref: (0, p)),
        ),
        out_shape=jax.ShapeDtypeStruct((512, 512), BF16),
        cost_estimate=pl.CostEstimate(flops=0, bytes_accessed=1 << 20, transcendentals=0),
    )(rep, flags, b)


def assemble_kernel(place_ref, scale_ref, *refs):
    pieces, o_ref = refs[:8], refs[8]
    for g in range(4):
        t = (g - place_ref[0]) & 3
        for j in range(4):
            z = (place_ref[1] - j * place_ref[2]) & 3
            piece = pieces[2 * g + j // 2][:, TILE * (j % 2):TILE * (j % 2 + 1)]
            scale = scale_ref[t, pl.ds(z, 1), :]
            o_ref[t, z] = (piece.astype(F32) * scale).astype(BF16)


def assemble(place, scale, pieces):
    return pl.pallas_call(
        assemble_kernel,
        grid_spec=pltpu.PrefetchScalarGridSpec(
            num_scalar_prefetch=1,
            grid=(4,),
            in_specs=[pl.BlockSpec((4, 4, TILE), lambda i, t: (0, 0, 0))]
            + [pl.BlockSpec((256, 256), lambda i, t: (i, 0))] * 8,
            out_specs=pl.BlockSpec((4, 4, 256, TILE), lambda i, t: (0, 0, i, 0)),
        ),
        out_shape=jax.ShapeDtypeStruct((4, 4, 1024, TILE), BF16),
        cost_estimate=pl.CostEstimate(flops=1 << 21, bytes_accessed=8 << 20, transcendentals=0),
    )(place, scale, *pieces)


def product_kernel(a_ref, *refs):
    hops, (k0_ref, k2_ref, s_ref) = refs[:4], refs[4:]
    total = jnp.zeros((256, 512), F32)
    for h in range(4):
        left = jnp.concatenate([a_ref[h, z] for z in range(4)], 1)
        total += jnp.dot(left, hops[h][...], preferred_element_type=F32)
    k0_ref[...] = total[:, :128]
    k2_ref[...] = total[:, 128:256]
    s_ref[...] = total[:, 256:].astype(BF16)


def product(a, hops):
    return pl.pallas_call(
        product_kernel,
        grid=(4,),
        in_specs=[pl.BlockSpec((4, 4, 256, TILE), lambda i: (0, 0, i, 0))]
        + [pl.BlockSpec((512, 512), lambda i: (0, 0))] * 4,
        out_specs=[
            pl.BlockSpec((256, 128), lambda i: (i, 0)),
            pl.BlockSpec((256, 128), lambda i: (i, 0)),
            pl.BlockSpec((256, 256), lambda i: (i, 0)),
        ],
        out_shape=[
            jax.ShapeDtypeStruct((1024, 128), F32),
            jax.ShapeDtypeStruct((1024, 128), F32),
            jax.ShapeDtypeStruct((1024, 256), BF16),
        ],
        compiler_params=pltpu.CompilerParams(vmem_limit_bytes=32 << 20),
        cost_estimate=pl.CostEstimate(flops=2 * 1024 * 2048 * 512, bytes_accessed=8 << 20, transcendentals=0),
    )(a, *hops)


def after(value, *others):
    return lax.optimization_barrier((value, *others))[0]


def shards(a_weights, a_flags, b_weights, b_flags, out_flags):
    rep = lax.axis_index("rep").astype(jnp.int32)
    row = lax.axis_index("row").astype(jnp.int32)
    col = lax.axis_index("col").astype(jnp.int32)
    x, z, turn = col >> 2, col & 3, 1 - 2 * (rep & 1)
    b, bf = b_weights[0], b_flags[0]
    chunks = [prep(rep[None], bf, b, c) for c in range(4)]
    a = a_weights[0] * jnp.repeat(a_flags[0, :, 0], TILE).astype(BF16)[:, None]

    hops = [[v] for v in chunks]
    for c in range(4):
        if c >= 2:
            hops[c][0] = after(hops[c][0], hops[c - 2][3])
        for h in range(3):
            hops[c].append(lax.ppermute(hops[c][h], ("row", "rep"), ROWS[1]))
        hops[c][0] = chunks[c]

    along_z = [a]
    for h in range(3):
        along_z.append(lax.ppermute(along_z[h], ("col", "rep"), ALONG_Z))
    near = [jnp.concatenate(along_z[:2], 1)]
    far = [jnp.concatenate(along_z[2:], 1)]
    for h in range(3):
        near.append(lax.ppermute(near[h], ("col", "rep"), ALONG_X))
        far.append(lax.ppermute(far[h], ("col", "rep"), ALONG_X))
    pieces = [v for pair in zip(near, far) for v in pair]

    a_sum = jnp.sum(a, axis=1, dtype=F32)
    b_sum = sum(jnp.sum(v, axis=1, dtype=F32) for v in chunks)
    sums = jnp.concatenate([a_sum, b_sum])
    for k in (1, 2, 4, 8):
        sums = sums + lax.ppermute(sums, "col", COLS[k])
    walk_b = 1.0 / (1.0 + sums[1024:])
    scale = jnp.stack([walk_b] + [lax.ppermute(walk_b, ("row", "rep"), ROWS[h]) for h in (1, 2, 3)], 0)
    deg_a = sums[:1024]
    for k in (1, 2):
        deg_a = deg_a + lax.ppermute(deg_a, "rep", SWAP[k])
    row_scale = (jnp.float32(TILE * 256) / (1.0 + deg_a))[:, None]

    place = jnp.stack([(x - row) * turn, z, turn])
    full = assemble(place, scale.reshape(4, 4, TILE), pieces)

    done = []
    for c in range(4):
        k0, k2, send = product(full, hops[c])
        got = lax.ppermute(send, "rep", SWAP[1])
        onward = (k2 + got[:, 128:].astype(F32)).astype(BF16)
        last = lax.ppermute(onward, "rep", SWAP[2])
        total = k0 + got[:, :128].astype(F32) + last.astype(F32)
        on = jnp.repeat(out_flags[:, c], TILE).astype(F32)[:, None]
        done.append((row_scale * total * on).astype(BF16))
    return jnp.concatenate(done, 1)


def solution(mesh):
    return jax.shard_map(
        shards,
        mesh=mesh,
        in_specs=(
            P("rep", "row", "col"),
            P("rep", "row", "col"),
            P("rep", "row", "col"),
            P("rep", "row", "col"),
            P("row", ("col", "rep")),
        ),
        out_specs=P("row", ("col", "rep")),
        check_vma=False,
    )
```

time: 379 us -> 166 us (0.44)
  blocking collectives: 162 us -> 0 us
  waiting for transfers between devices: 171 us -> 45.7 us
  starting transfers between devices: 0.09 us -> 68.1 us
  Pallas kernels: 0 us -> 37.7 us
  matrix products: 13.8 us -> 0 us
  between operations: 13.1 us -> 0.22 us
  other arithmetic: 12.1 us -> 6.38 us
    psum x2 -> x0, blocking collectives: 162 us -> none  [the longest x1 128 us: shards(): lax.psum(jnp.sum(a_masked, axis=(0, 2), dtype=jnp.float32), ('col', 'rep'))]
    all_gather x2 -> x0, waiting for transfers between devices: 122 us -> none  [the longest x1 86 us: shards(): lax.all_gather(walk_b, 'row', axis=1, tiled=True)[0]]
    ppermute x0 -> x38, starting transfers between devices: none -> 68.1 us  [the longest x3 16.5 us: shards(): along_z.append(lax.ppermute(along_z[h], ('col', 'rep'), ALONG_Z))]
    reduce_scatter x1 -> x0, waiting for transfers between devices: 48.7 us -> none  [shards(): lax.psum_scatter(partial_sum.astype(jnp.bfloat16), 'rep', scatter_dimensi...]
    ppermute x0 -> x38, waiting for transfers between devices: none -> 45.7 us  [the longest x4 20.8 us: shards(): last = lax.ppermute(onward, 'rep', SWAP[2])]
    pallas_call x0 -> x9, Pallas kernels: none -> 37.7 us  [the longest x4 16.1 us: product(): pl.pallas_call(product_kernel, grid=(4,), in_specs=[pl.BlockSpec((4, 4, 2...]
    dot_general x1 -> x0, matrix products: 13.8 us -> none  [shards(): jnp.dot(left_rows, lax.all_gather(walk_b, 'row', axis=1, tiled=True)[0],...]
    convert_element_type x6 -> x7, other arithmetic: 8.61 us -> 1.18 us  [the longest x1 0.95 us: shards(): done.append((row_scale * total * on).astype(BF16))]
  transfers between devices with their start and end apart: 3 -> 38, of which waited for: 3 -> 14; matrix products, arithmetic and copies ran while one was open for 3% -> 3% of each run, Pallas kernels for 0% -> 20%
where the time goes in v1:
time: 166 us; the launch traced here: 164 us
  starting transfers between devices  68.1 us (41%)
  waiting for transfers between devices  45.7 us (28%)
  Pallas kernels  37.7 us (23%)
  other arithmetic  6.38 us (4%)
  local copies, waits for them, and re-layouts  6.02 us (4%)
    ppermute x4, waiting for transfers between devices, shards(): last = lax.ppermute(onward, 'rep', SWAP[2])  20.8 us
    ppermute x3, starting transfers between devices, shards(): along_z.append(lax.ppermute(along_z[h], ('col', 'rep'), ALONG_Z))  16.5 us
    pallas_call x4, Pallas kernels, product(): pl.pallas_call(product_kernel, grid=(4,), in_specs=[pl.BlockSpec((4, 4, 2...  16.1 us
    pallas_call x4, Pallas kernels, prep(): pl.pallas_call(functools.partial(prep_kernel, chunk=chunk), grid_spec=plt...  15.9 us
    ppermute x2, starting transfers between devices, shards(): deg_a = deg_a + lax.ppermute(deg_a, 'rep', SWAP[k])  9.38 us
    ppermute x3, starting transfers between devices, shards(): lax.ppermute(walk_b, ('row', 'rep'), ROWS[h])  9.15 us
    ppermute x4, waiting for transfers between devices, shards(): sums = sums + lax.ppermute(sums, 'col', COLS[k])  8.76 us
    ppermute x12, starting transfers between devices, shards(): hops[c].append(lax.ppermute(hops[c][h], ('row', 'rep'), ROWS[1]))  8.62 us
  transfers between devices with their start and end apart: 38, of which 14 were waited for; matrix products, arithmetic and copies ran while one was open for 3% of the time, Pallas kernels for 20%

profile of v1, /device:TPU:1, one launch (start us, length us, event | category | flops | bytes accessed | tf_op | source)
XLA Modules:
  0.0 164.1 jit_solution(4996440263843381450)
XLA Ops:
  0.0 4.1 %shard_map.55.refs_0_ = bf16[512,512]{1,0:T(8,128)(2,1)} custom-call(s32[1]{0:T(128)} %bitcast.3.rep_ref, s32[4,16]{1,0:T(4,128)} %bitcast.38, bf16[512,2048]{1,0:T(8,128)(2,1)} %bitcast.34), custom_call_target="tpu_custom_call" | custom-call | bytes 1048576 | tf_op jit(solution)/shard_map/pallas_call | solution.py:41
  4.1 3.6 %collective-permute-start.18 = (bf16[512,512]{1,0:T(8,128)(2,1)}, bf16[512,512]{1,0:T(8,128)(2,1)S(1)}, u32[]{:S(2)}, u32[]{:S(2)}) collective-permute-start(bf16[512,512]{1,0:T(8,128)(2,1)} %shard_map.55.refs_0_), channel_id=1, source_target_pairs={{0,64},{1,193},{2,66},{3,195},{64,128},{65,1},{66,130},{67,3},{128... | collective-permute-start | bytes 1572872 | tf_op jit(solution)/shard_map/ppermute | solution.py:130
  8.1 6.1 %collective-permute-start.9 = (bf16[1024,128]{1,0:T(8,128)(2,1)S(1)}, bf16[1024,128]{1,0:T(8,128)(2,1)}, u32[]{:S(2)}, u32[]{:S(2)}) collective-permute-start(bf16[1024,128]{1,0:T(8,128)(2,1)S(1)} %get-tuple-element.34), channel_id=1, source_target_pairs={{0,4},{1,13},{2,6},{3,15},{4,8},{5,1},{6,10},{7,3},{8,12},{9,5},{1... | collective-permute-start | bytes 786440 | tf_op jit(solution)/shard_map/ppermute | solution.py:135
  14.2 3.9 %shard_map.56.refs_0_ = bf16[512,512]{1,0:T(8,128)(2,1)} custom-call(s32[1]{0:T(128)} %bitcast.3.rep_ref, s32[4,16]{1,0:T(4,128)} %bitcast.39, bf16[512,2048]{1,0:T(8,128)(2,1)} %bitcast.35), custom_call_target="tpu_custom_call" | custom-call | bytes 1048576 | tf_op jit(solution)/shard_map/pallas_call | solution.py:41
  18.7 3.9 %shard_map.58.refs_0_ = bf16[512,512]{1,0:T(8,128)(2,1)} custom-call(s32[1]{0:T(128)} %bitcast.3.rep_ref, s32[4,16]{1,0:T(4,128)} %bitcast.40, bf16[512,2048]{1,0:T(8,128)(2,1)} %bitcast.36), custom_call_target="tpu_custom_call" | custom-call | bytes 1048576 | tf_op jit(solution)/shard_map/pallas_call | solution.py:41
  22.6 4.0 %shard_map.57.refs_0_ = bf16[512,512]{1,0:T(8,128)(2,1)} custom-call(s32[1]{0:T(128)} %bitcast.3.rep_ref, s32[4,16]{1,0:T(4,128)} %bitcast.41, bf16[512,2048]{1,0:T(8,128)(2,1)} %bitcast.37), custom_call_target="tpu_custom_call" | custom-call | bytes 1048576 | tf_op jit(solution)/shard_map/pallas_call | solution.py:41
  26.7 4.7 %collective-permute-start.10 = (bf16[1024,128]{1,0:T(8,128)(2,1)}, bf16[1024,128]{1,0:T(8,128)(2,1)S(1)}, u32[]{:S(2)}, u32[]{:S(2)}) collective-permute-start(bf16[1024,128]{1,0:T(8,128)(2,1)} %collective-permute-done.9), channel_id=1, source_target_pairs={{0,4},{1,13},{2,6},{3,15},{4,8},{5,1},{6,10},{7,3},{8,12},{9,5},{1... | collective-permute-start | bytes 786440 | tf_op jit(solution)/shard_map/ppermute | solution.py:135
  31.6 1.3 convert_reduce_fusion
  32.9 3.1 %collective-permute-done.10 = bf16[1024,128]{1,0:T(8,128)(2,1)S(1)} collective-permute-done((bf16[1024,128]{1,0:T(8,128)(2,1)}, bf16[1024,128]{1,0:T(8,128)(2,1)S(1)}, u32[]{:S(2)}, u32[]{:S(2)}) %collective-permute-start.10) | collective-permute-done | bytes 262176 | tf_op jit(solution)/shard_map/ppermute | solution.py:135
  36.0 5.7 %collective-permute-start.11 = (bf16[1024,128]{1,0:T(8,128)(2,1)S(1)}, bf16[1024,128]{1,0:T(8,128)(2,1)S(1)}, u32[]{:S(2)}, u32[]{:S(2)}) collective-permute-start(bf16[1024,128]{1,0:T(8,128)(2,1)S(1)} %collective-permute-done.10), channel_id=1, source_target_pairs={{0,4},{1,13},{2,6},{3,15},{4,8},{5,1},{6,10},{7,3},{8,12},{9,5},{1... | collective-permute-start | bytes 786440 | tf_op jit(solution)/shard_map/ppermute | solution.py:135
  41.9 1.0 pad_maximum_fusion.1.refs_0_
  42.9 2.6 %collective-permute-start.12 = (bf16[1024,256]{1,0:T(8,128)(2,1)S(1)}, bf16[1024,256]{1,0:T(8,128)(2,1)}, u32[]{:S(2)}, u32[]{:S(2)}) collective-permute-start(bf16[1024,256]{1,0:T(8,128)(2,1)S(1)} %pad_maximum_fusion.1.refs_0_), channel_id=1, source_target_pairs={{0,16},{1,49},{2,18},{3,51},{4,20},{5,53},{6,22},{7,55},{8,24},{9,... | collective-permute-start | bytes 1572872 | tf_op jit(solution)/shard_map/ppermute | solution.py:139
  45.5 2.3 %collective-permute-done.11 = bf16[1024,128]{1,0:T(8,128)(2,1)S(1)} collective-permute-done((bf16[1024,128]{1,0:T(8,128)(2,1)S(1)}, bf16[1024,128]{1,0:T(8,128)(2,1)S(1)}, u32[]{:S(2)}, u32[]{:S(2)}) %collective-permute-start.11) | collective-permute-done | bytes 262176 | tf_op jit(solution)/shard_map/ppermute | solution.py:135
  47.8 2.6 %collective-permute-start.13 = (bf16[1024,256]{1,0:T(8,128)(2,1)S(1)}, bf16[1024,256]{1,0:T(8,128)(2,1)}, u32[]{:S(2)}, u32[]{:S(2)}) collective-permute-start(bf16[1024,256]{1,0:T(8,128)(2,1)S(1)} %constant_dynamic-update-slice_fusion.refs_1_), channel_id=1, source_target_pairs={{0,16},{1,49},{2,18},{3,51},{4,20},{5,53},{6,22},{7,55},{8,24},{9,... | collective-permute-start | bytes 1572872 | tf_op jit(solution)/shard_map/ppermute | solution.py:140
  50.4 1.0 collective-permute-start.25
  51.4 0.8 copy-done.5
  52.6 3.2 %collective-permute-done.20.refs_3_ = bf16[512,512]{1,0:T(8,128)(2,1)S(1)} collective-permute-done((bf16[512,512]{1,0:T(8,128)(2,1)}, bf16[512,512]{1,0:T(8,128)(2,1)S(1)}, u32[]{:S(2)}, u32[]{:S(2)}) %collective-permute-start.20) | collective-permute-done | bytes 524320 | tf_op jit(solution)/shard_map/ppermute | solution.py:130
  56.6 1.2 collective-permute-start.28
  57.8 1.1 collective-permute-start.1
  58.9 5.4 %collective-permute-done.1 = f32[1536]{0:T(1024)S(1)} collective-permute-done((f32[1536]{0:T(1024)S(1)}, f32[1536]{0:T(1024)S(1)}, u32[]{:S(2)}, u32[]{:S(2)}) %collective-permute-start.1) | collective-permute-done | bytes 6176 | tf_op jit(solution)/shard_map/ppermute | solution.py:147
  65.1 1.7 %collective-permute-done.2 = f32[1536]{0:T(1024)S(1)} collective-permute-done((f32[1536]{0:T(1024)S(1)}, f32[1536]{0:T(1024)S(1)}, u32[]{:S(2)}, u32[]{:S(2)}) %collective-permute-start.2) | collective-permute-done | bytes 6176 | tf_op jit(solution)/shard_map/ppermute | solution.py:147
  66.8 2.3 %collective-permute-start.3 = (f32[1536]{0:T(1024)S(1)}, f32[1536]{0:T(1024)S(1)}, u32[]{:S(2)}, u32[]{:S(2)}) collective-permute-start(f32[1536]{0:T(1024)S(1)} %add.80), channel_id=1, source_target_pairs={{0,32},{4,36},{8,40},{12,44},{16,48},{20,52},{24,56},{28,60},{32,0... | collective-permute-start | bytes 18440 | tf_op jit(solution)/shard_map/ppermute | solution.py:147
  69.2 1.7 %collective-permute-done.3 = f32[1536]{0:T(1024)S(1)} collective-permute-done((f32[1536]{0:T(1024)S(1)}, f32[1536]{0:T(1024)S(1)}, u32[]{:S(2)}, u32[]{:S(2)}) %collective-permute-start.3) | collective-permute-done | bytes 6176 | tf_op jit(solution)/shard_map/ppermute | solution.py:147
  70.9 2.1 %collective-permute-start.14 = (bf16[1024,256]{1,0:T(8,128)(2,1)}, bf16[1024,256]{1,0:T(8,128)(2,1)}, u32[]{:S(2)}, u32[]{:S(2)}) collective-permute-start(bf16[1024,256]{1,0:T(8,128)(2,1)} %collective-permute-done.12.refs_2_), channel_id=1, source_target_pairs={{0,16},{1,49},{2,18},{3,51},{4,20},{5,53},{6,22},{7,55},{8,24},{9,... | collective-permute-start | bytes 1572872 | tf_op jit(solution)/shard_map/ppermute | solution.py:139
  74.7 1.1 collective-permute-start.8
  75.8 1.6 collective-permute-start.29
  77.5 1.3 collective-permute-done.8
  79.8 2.9 %collective-permute-done.7 = f32[512]{0:T(512)S(1)} collective-permute-done((f32[512]{0:T(512)S(1)}, f32[512]{0:T(512)S(1)}, u32[]{:S(2)}, u32[]{:S(2)}) %collective-permute-start.7) | collective-permute-done | bytes 2080 | tf_op jit(solution)/shard_map/ppermute | solution.py:149
  82.7 7.7 %collective-permute-start.6 = (f32[512]{0:T(512)S(1)}, f32[512]{0:T(512)S(1)}, u32[]{:S(2)}, u32[]{:S(2)}) collective-permute-start(f32[512]{0:T(512)S(1)} %fusion), channel_id=1, source_target_pairs={{0,64},{1,193},{2,66},{3,195},{64,128},{65,1},{66,130},{67,3},{128... | collective-permute-start | bytes 6152 | tf_op jit(solution)/shard_map/ppermute | solution.py:149
  91.3 7.0 %collective-permute-start.4 = (f32[1024]{0:T(1024)S(1)}, f32[1024]{0:T(1024)S(1)}, u32[]{:S(2)}, u32[]{:S(2)}) collective-permute-start(f32[1024]{0:T(1024)S(1)} %slice.62), channel_id=1, source_target_pairs={{0,1},{1,0},{2,3},{3,2},{4,5},{5,4},{6,7},{7,6},{8,9},{9,8},{10,11... | collective-permute-start | bytes 12296 | tf_op jit(solution)/shard_map/ppermute | solution.py:152
  99.2 2.3 %collective-permute-start.5 = (f32[1024]{0:T(1024)S(1)}, f32[1024]{0:T(1024)S(1)}, u32[]{:S(2)}, u32[]{:S(2)}) collective-permute-start(f32[1024]{0:T(1024)S(1)} %slice_add_fusion.1), channel_id=1, source_target_pairs={{0,2},{1,3},{2,0},{3,1},{4,6},{5,7},{6,4},{7,5},{8,10},{9,11},{10,... | collective-permute-start | bytes 12296 | tf_op jit(solution)/shard_map/ppermute | solution.py:152
  101.5 3.1 %collective-permute-done.17.refs_7_ = bf16[1024,256]{1,0:T(8,128)(2,1)} collective-permute-done((bf16[1024,256]{1,0:T(8,128)(2,1)}, bf16[1024,256]{1,0:T(8,128)(2,1)}, u32[]{:S(2)}, u32[]{:S(2)}) %collective-permute-start.17) | collective-permute-done | bytes 524320 | tf_op jit(solution)/shard_map/ppermute | solution.py:140
  104.6 5.7 %shard_map.59.a_ref = bf16[4,4,1024,128]{3,2,1,0:T(8,128)(2,1)} custom-call(s32[3]{0:T(128)} %pad_add_fusion.place_ref, f32[4,4,128]{2,1,0:T(4,128)} %pad_maximum_fusion.3.scale_ref, bf16[1024,256]{1,0:T(8,128)(2,1)} %copy-done.11, bf16[1024,256]{1,0:T(8,128)(2,1)} %copy-done.12, bf16[1024,256]{1,0:T(8,128)(2,1)} %collective-permute-done.12.refs_2_, ...), custom_call_target="tpu_custom_call" | custom-call | flops 2097152 | bytes 8388608 | tf_op jit(solution)/shard_map/pallas_call | solution.py:66
  110.4 2.2 %copy-done = bf16[4,4,1024,128]{3,2,1,0:T(8,128)(2,1)S(1)} copy-done((bf16[4,4,1024,128]{3,2,1,0:T(8,128)(2,1)S(1)}, bf16[4,4,1024,128]{3,2,1,0:T(8,128)(2,1)}, u32[]{:S(2)}) %copy-start) | copy-done | bytes 4194328
  112.6 1.0 copy-done.8
  113.6 4.2 %shard_map.60 = (f32[1024,128]{1,0:T(8,128)S(1)}, f32[1024,128]{1,0:T(8,128)S(1)}, bf16[1024,256]{1,0:T(8,128)(2,1)S(1)}) custom-call(bf16[4,4,1024,128]{3,2,1,0:T(8,128)(2,1)S(1)} %copy-done, bf16[512,512]{1,0:T(8,128)(2,1)S(1)} %copy-done.2, bf16[512,512]{1,0:T(8,128)(2,1)S(1)} %collective-permute-done.18.refs_1_, ...), custom_call_target="tpu_custom_call" | custom-call | flops 2147483648 | bytes 8388608 | tf_op jit(solution)/shard_map/pallas_call | solution.py:92
  117.8 7.1 %collective-permute-start.21 = (bf16[1024,256]{1,0:T(8,128)(2,1)S(1)}, bf16[1024,256]{1,0:T(8,128)(2,1)S(1)}, u32[]{:S(2)}, u32[]{:S(2)}) collective-permute-start(bf16[1024,256]{1,0:T(8,128)(2,1)S(1)} %get-tuple-element.20), channel_id=1, source_target_pairs={{0,1},{1,0},{2,3},{3,2},{4,5},{5,4},{6,7},{7,6},{8,9},{9,8},{10,11... | collective-permute-start | bytes 1572872 | tf_op jit(solution)/shard_map/ppermute | solution.py:161
  124.9 3.1 %shard_map.61 = (f32[1024,128]{1,0:T(8,128)S(1)}, f32[1024,128]{1,0:T(8,128)S(1)}, bf16[1024,256]{1,0:T(8,128)(2,1)S(1)}) custom-call(bf16[4,4,1024,128]{3,2,1,0:T(8,128)(2,1)S(1)} %copy-done, bf16[512,512]{1,0:T(8,128)(2,1)S(1)} %copy-done.4, bf16[512,512]{1,0:T(8,128)(2,1)S(1)} %collective-permute-done.23.refs_1_, bf16[512,512]{1,0:T(8,128)(2,1)S(1)} %copy-done.6, ...), custom_call_target="tpu_custom_call" | custom-call | flops 2147483648 | bytes 8388608 | tf_op jit(solution)/shard_map/pallas_call | solution.py:92
  128.2 4.5 %shard_map.62 = (f32[1024,128]{1,0:T(8,128)S(1)}, f32[1024,128]{1,0:T(8,128)S(1)}, bf16[1024,256]{1,0:T(8,128)(2,1)S(1)}) custom-call(bf16[4,4,1024,128]{3,2,1,0:T(8,128)(2,1)S(1)} %copy-done, bf16[512,512]{1,0:T(8,128)(2,1)S(1)} %copy-done.3, bf16[512,512]{1,0:T(8,128)(2,1)} %collective-permute-done.28.refs_1_, ...), custom_call_target="tpu_custom_call" | custom-call | flops 2147483648 | bytes 8388608 | tf_op jit(solution)/shard_map/pallas_call | solution.py:92
  133.2 4.3 %shard_map.63 = (f32[1024,128]{1,0:T(8,128)S(1)}, f32[1024,128]{1,0:T(8,128)S(1)}, bf16[1024,256]{1,0:T(8,128)(2,1)S(1)}) custom-call(bf16[4,4,1024,128]{3,2,1,0:T(8,128)(2,1)S(1)} %copy-done, bf16[512,512]{1,0:T(8,128)(2,1)S(1)} %copy-done.1, bf16[512,512]{1,0:T(8,128)(2,1)} %collective-permute-done.33.refs_1_, ...), custom_call_target="tpu_custom_call" | custom-call | flops 2147483648 | bytes 8388608 | tf_op jit(solution)/shard_map/pallas_call | solution.py:92
  137.7 0.9 collective-permute-start.22
  139.5 0.9 collective-permute-start.32
  141.2 3.9 %collective-permute-done.22 = bf16[1024,128]{1,0:T(8,128)(2,1)S(1)} collective-permute-done((bf16[1024,128]{1,0:T(8,128)(2,1)S(1)}, bf16[1024,128]{1,0:T(8,128)(2,1)S(1)}, u32[]{:S(2)}, u32[]{:S(2)}) %collective-permute-start.22) | collective-permute-done | bytes 262176 | tf_op jit(solution)/shard_map/ppermute | solution.py:163
  145.2 5.6 %collective-permute-done.27 = bf16[1024,128]{1,0:T(8,128)(2,1)S(1)} collective-permute-done((bf16[1024,128]{1,0:T(8,128)(2,1)S(1)}, bf16[1024,128]{1,0:T(8,128)(2,1)S(1)}, u32[]{:S(2)}, u32[]{:S(2)}) %collective-permute-start.27) | collective-permute-done | bytes 262176 | tf_op jit(solution)/shard_map/ppermute | solution.py:163
  150.8 5.6 %collective-permute-done.32 = bf16[1024,128]{1,0:T(8,128)(2,1)S(1)} collective-permute-done((bf16[1024,128]{1,0:T(8,128)(2,1)S(1)}, bf16[1024,128]{1,0:T(8,128)(2,1)S(1)}, u32[]{:S(2)}, u32[]{:S(2)}) %collective-permute-start.32) | collective-permute-done | bytes 262176 | tf_op jit(solution)/shard_map/ppermute | solution.py:163
  156.4 5.6 %collective-permute-done.37 = bf16[1024,128]{1,0:T(8,128)(2,1)S(1)} collective-permute-done((bf16[1024,128]{1,0:T(8,128)(2,1)S(1)}, bf16[1024,128]{1,0:T(8,128)(2,1)S(1)}, u32[]{:S(2)}, u32[]{:S(2)}) %collective-permute-start.37) | collective-permute-done | bytes 262176 | tf_op jit(solution)/shard_map/ppermute | solution.py:163
  162.0 1.0 multiply_convert_fusion.3
  163.0 1.1 pad_maximum_fusion
  (99 shorter events, 10.8 us)
Async XLA Ops:
  0.0 7.7 %copy-start.13 = (bf16[1,1024,128]{2,1,0:T(8,128)(2,1)S(1)}, bf16[1,1024,128]{2,1,0:T(8,128)(2,1)}, u32[]{:S(2)}) copy-start(bf16[1,1024,128]{2,1,0:T(8,128)(2,1)} %param.5) | copy-start | bytes 786436
  4.1 14.5 %collective-permute-start.18 = (bf16[512,512]{1,0:T(8,128)(2,1)}, bf16[512,512]{1,0:T(8,128)(2,1)S(1)}, u32[]{:S(2)}, u32[]{:S(2)}) collective-permute-start(bf16[512,512]{1,0:T(8,128)(2,1)} %shard_map.55.refs_0_), channel_id=1, source_target_pairs={{0,64},{1,193},{2,66},{3,195},{64,128},{65,1},{66,130},{67,3},{128... | collective-permute-start | bytes 1572872 | tf_op jit(solution)/shard_map/ppermute | solution.py:130
  8.1 18.6 %collective-permute-start.9 = (bf16[1024,128]{1,0:T(8,128)(2,1)S(1)}, bf16[1024,128]{1,0:T(8,128)(2,1)}, u32[]{:S(2)}, u32[]{:S(2)}) collective-permute-start(bf16[1024,128]{1,0:T(8,128)(2,1)S(1)} %get-tuple-element.34), channel_id=1, source_target_pairs={{0,4},{1,13},{2,6},{3,15},{4,8},{5,1},{6,10},{7,3},{8,12},{9,5},{1... | collective-permute-start | bytes 786440 | tf_op jit(solution)/shard_map/ppermute | solution.py:135
  18.1 13.3 %copy-start.2 = (bf16[512,512]{1,0:T(8,128)(2,1)S(1)}, bf16[512,512]{1,0:T(8,128)(2,1)}, u32[]{:S(2)}) copy-start(bf16[512,512]{1,0:T(8,128)(2,1)} %shard_map.55.refs_0_) | copy-start | bytes 1572868
  18.1 13.3 %copy-start.4 = (bf16[512,512]{1,0:T(8,128)(2,1)S(1)}, bf16[512,512]{1,0:T(8,128)(2,1)}, u32[]{:S(2)}) copy-start(bf16[512,512]{1,0:T(8,128)(2,1)} %shard_map.56.refs_0_) | copy-start | bytes 1572868
  18.1 23.6 %collective-permute-start.23 = (bf16[512,512]{1,0:T(8,128)(2,1)}, bf16[512,512]{1,0:T(8,128)(2,1)S(1)}, u32[]{:S(2)}, u32[]{:S(2)}) collective-permute-start(bf16[512,512]{1,0:T(8,128)(2,1)} %shard_map.56.refs_0_), channel_id=1, source_target_pairs={{0,64},{1,193},{2,66},{3,195},{64,128},{65,1},{66,130},{67,3},{128... | collective-permute-start | bytes 1572872 | tf_op jit(solution)/shard_map/ppermute | solution.py:130
  18.6 23.2 %collective-permute-start.19 = (bf16[512,512]{1,0:T(8,128)(2,1)S(1)}, bf16[512,512]{1,0:T(8,128)(2,1)}, u32[]{:S(2)}, u32[]{:S(2)}) collective-permute-start(bf16[512,512]{1,0:T(8,128)(2,1)S(1)} %collective-permute-done.18.refs_1_), channel_id=1, source_target_pairs={{0,64},{1,193},{2,66},{3,195},{64,128},{65,1},{66,130},{67,3},{128... | collective-permute-start | bytes 1572872 | tf_op jit(solution)/shard_map/ppermute | solution.py:130
  22.6 9.0 %copy-start.1 = (bf16[512,512]{1,0:T(8,128)(2,1)S(1)}, bf16[512,512]{1,0:T(8,128)(2,1)}, u32[]{:S(2)}) copy-start(bf16[512,512]{1,0:T(8,128)(2,1)} %shard_map.58.refs_0_) | copy-start | bytes 1572868
  26.7 29.9 %copy-start.3 = (bf16[512,512]{1,0:T(8,128)(2,1)S(1)}, bf16[512,512]{1,0:T(8,128)(2,1)}, u32[]{:S(2)}) copy-start(bf16[512,512]{1,0:T(8,128)(2,1)} %shard_map.57.refs_0_) | copy-start | bytes 1572868
  26.7 42.5 %copy-start.14 = (s32[8,4]{0,1:T(4,128)S(1)}, s32[8,4]{0,1:T(4,128)}, u32[]{:S(2)}) copy-start(s32[8,4]{0,1:T(4,128)} %param.9) | copy-start | bytes 388
  26.7 9.3 %collective-permute-start.10 = (bf16[1024,128]{1,0:T(8,128)(2,1)}, bf16[1024,128]{1,0:T(8,128)(2,1)S(1)}, u32[]{:S(2)}, u32[]{:S(2)}) collective-permute-start(bf16[1024,128]{1,0:T(8,128)(2,1)} %collective-permute-done.9), channel_id=1, source_target_pairs={{0,4},{1,13},{2,6},{3,15},{4,8},{5,1},{6,10},{7,3},{8,12},{9,5},{1... | collective-permute-start | bytes 786440 | tf_op jit(solution)/shard_map/ppermute | solution.py:135
  36.0 11.8 %collective-permute-start.11 = (bf16[1024,128]{1,0:T(8,128)(2,1)S(1)}, bf16[1024,128]{1,0:T(8,128)(2,1)S(1)}, u32[]{:S(2)}, u32[]{:S(2)}) collective-permute-start(bf16[1024,128]{1,0:T(8,128)(2,1)S(1)} %collective-permute-done.10), channel_id=1, source_target_pairs={{0,4},{1,13},{2,6},{3,15},{4,8},{5,1},{6,10},{7,3},{8,12},{9,5},{1... | collective-permute-start | bytes 786440 | tf_op jit(solution)/shard_map/ppermute | solution.py:135
  41.7 8.6 %collective-permute-start.24 = (bf16[512,512]{1,0:T(8,128)(2,1)S(1)}, bf16[512,512]{1,0:T(8,128)(2,1)S(1)}, u32[]{:S(2)}, u32[]{:S(2)}) collective-permute-start(bf16[512,512]{1,0:T(8,128)(2,1)S(1)} %collective-permute-done.23.refs_1_), channel_id=1, source_target_pairs={{0,64},{1,193},{2,66},{3,195},{64,128},{65,1},{66,130},{67,3},{128... | collective-permute-start | bytes 1572872 | tf_op jit(solution)/shard_map/ppermute | solution.py:130
  41.8 14.0 %collective-permute-start.20 = (bf16[512,512]{1,0:T(8,128)(2,1)}, bf16[512,512]{1,0:T(8,128)(2,1)S(1)}, u32[]{:S(2)}, u32[]{:S(2)}) collective-permute-start(bf16[512,512]{1,0:T(8,128)(2,1)} %collective-permute-done.19.refs_2_), channel_id=1, source_target_pairs={{0,64},{1,193},{2,66},{3,195},{64,128},{65,1},{66,130},{67,3},{128... | collective-permute-start | bytes 1572872 | tf_op jit(solution)/shard_map/ppermute | solution.py:130
  42.9 32.9 %copy-start.11 = (bf16[1024,256]{1,0:T(8,128)(2,1)}, bf16[1024,256]{1,0:T(8,128)(2,1)S(1)}, u32[]{:S(2)}) copy-start(bf16[1024,256]{1,0:T(8,128)(2,1)S(1)} %pad_maximum_fusion.1.refs_0_) | copy-start | bytes 1572868
  42.9 28.0 %collective-permute-start.12 = (bf16[1024,256]{1,0:T(8,128)(2,1)S(1)}, bf16[1024,256]{1,0:T(8,128)(2,1)}, u32[]{:S(2)}, u32[]{:S(2)}) collective-permute-start(bf16[1024,256]{1,0:T(8,128)(2,1)S(1)} %pad_maximum_fusion.1.refs_0_), channel_id=1, source_target_pairs={{0,16},{1,49},{2,18},{3,51},{4,20},{5,53},{6,22},{7,55},{8,24},{9,... | collective-permute-start | bytes 1572872 | tf_op jit(solution)/shard_map/ppermute | solution.py:139
  47.8 29.6 %copy-start.12 = (bf16[1024,256]{1,0:T(8,128)(2,1)}, bf16[1024,256]{1,0:T(8,128)(2,1)S(1)}, u32[]{:S(2)}) copy-start(bf16[1024,256]{1,0:T(8,128)(2,1)S(1)} %constant_dynamic-update-slice_fusion.refs_1_) | copy-start | bytes 1572868
  47.8 25.1 %collective-permute-start.13 = (bf16[1024,256]{1,0:T(8,128)(2,1)S(1)}, bf16[1024,256]{1,0:T(8,128)(2,1)}, u32[]{:S(2)}, u32[]{:S(2)}) collective-permute-start(bf16[1024,256]{1,0:T(8,128)(2,1)S(1)} %constant_dynamic-update-slice_fusion.refs_1_), channel_id=1, source_target_pairs={{0,16},{1,49},{2,18},{3,51},{4,20},{5,53},{6,22},{7,55},{8,24},{9,... | collective-permute-start | bytes 1572872 | tf_op jit(solution)/shard_map/ppermute | solution.py:140
  50.4 23.1 %collective-permute-start.25 = (bf16[512,512]{1,0:T(8,128)(2,1)S(1)}, bf16[512,512]{1,0:T(8,128)(2,1)S(1)}, u32[]{:S(2)}, u32[]{:S(2)}) collective-permute-start(bf16[512,512]{1,0:T(8,128)(2,1)S(1)} %collective-permute-done.24.refs_2_), channel_id=1, source_target_pairs={{0,64},{1,193},{2,66},{3,195},{64,128},{65,1},{66,130},{67,3},{128... | collective-permute-start | bytes 1572872 | tf_op jit(solution)/shard_map/ppermute | solution.py:130
  52.2 5.6 %collective-permute-start = (f32[1536]{0:T(1024)S(1)}, f32[1536]{0:T(1024)S(1)}, u32[]{:S(2)}, u32[]{:S(2)}) collective-permute-start(f32[1536]{0:T(1024)S(1)} %pad_maximum_fusion.2), channel_id=1, source_target_pairs={{0,4},{4,0},{8,12},{12,8},{16,20},{20,16},{24,28},{28,24},{32,36},... | collective-permute-start | bytes 18440 | tf_op jit(solution)/shard_map/ppermute | solution.py:147
  56.6 19.2 %collective-permute-start.28 = (bf16[512,512]{1,0:T(8,128)(2,1)S(1)}, bf16[512,512]{1,0:T(8,128)(2,1)}, u32[]{:S(2)}, u32[]{:S(2)}) collective-permute-start(bf16[512,512]{1,0:T(8,128)(2,1)S(1)} %copy-done.3), channel_id=1, source_target_pairs={{0,64},{1,193},{2,66},{3,195},{64,128},{65,1},{66,130},{67,3},{128... | collective-permute-start | bytes 1572872 | tf_op jit(solution)/shard_map/ppermute | solution.py:130
  57.8 6.5 %collective-permute-start.1 = (f32[1536]{0:T(1024)S(1)}, f32[1536]{0:T(1024)S(1)}, u32[]{:S(2)}, u32[]{:S(2)}) collective-permute-start(f32[1536]{0:T(1024)S(1)} %fusion.1), channel_id=1, source_target_pairs={{0,8},{4,12},{8,0},{12,4},{16,24},{20,28},{24,16},{28,20},{32,40},... | collective-permute-start | bytes 18440 | tf_op jit(solution)/shard_map/ppermute | solution.py:147
  64.3 2.5 %collective-permute-start.2 = (f32[1536]{0:T(1024)S(1)}, f32[1536]{0:T(1024)S(1)}, u32[]{:S(2)}, u32[]{:S(2)}) collective-permute-start(f32[1536]{0:T(1024)S(1)} %add.79), channel_id=1, source_target_pairs={{0,16},{4,20},{8,24},{12,28},{16,0},{20,4},{24,8},{28,12},{32,48},... | collective-permute-start | bytes 18440 | tf_op jit(solution)/shard_map/ppermute | solution.py:147
  66.8 4.0 %collective-permute-start.3 = (f32[1536]{0:T(1024)S(1)}, f32[1536]{0:T(1024)S(1)}, u32[]{:S(2)}, u32[]{:S(2)}) collective-permute-start(f32[1536]{0:T(1024)S(1)} %add.80), channel_id=1, source_target_pairs={{0,32},{4,36},{8,40},{12,44},{16,48},{20,52},{24,56},{28,60},{32,0... | collective-permute-start | bytes 18440 | tf_op jit(solution)/shard_map/ppermute | solution.py:147
  70.9 19.5 %collective-permute-start.14 = (bf16[1024,256]{1,0:T(8,128)(2,1)}, bf16[1024,256]{1,0:T(8,128)(2,1)}, u32[]{:S(2)}, u32[]{:S(2)}) collective-permute-start(bf16[1024,256]{1,0:T(8,128)(2,1)} %collective-permute-done.12.refs_2_), channel_id=1, source_target_pairs={{0,16},{1,49},{2,18},{3,51},{4,20},{5,53},{6,22},{7,55},{8,24},{9,... | collective-permute-start | bytes 1572872 | tf_op jit(solution)/shard_map/ppermute | solution.py:139
  72.9 17.7 %collective-permute-start.15 = (bf16[1024,256]{1,0:T(8,128)(2,1)}, bf16[1024,256]{1,0:T(8,128)(2,1)}, u32[]{:S(2)}, u32[]{:S(2)}) collective-permute-start(bf16[1024,256]{1,0:T(8,128)(2,1)} %collective-permute-done.13.refs_3_), channel_id=1, source_target_pairs={{0,16},{1,49},{2,18},{3,51},{4,20},{5,53},{6,22},{7,55},{8,24},{9,... | collective-permute-start | bytes 1572872 | tf_op jit(solution)/shard_map/ppermute | solution.py:140
  74.3 17.0 %collective-permute-start.33 = (bf16[512,512]{1,0:T(8,128)(2,1)S(1)}, bf16[512,512]{1,0:T(8,128)(2,1)}, u32[]{:S(2)}, u32[]{:S(2)}) collective-permute-start(bf16[512,512]{1,0:T(8,128)(2,1)S(1)} %copy-done.1), channel_id=1, source_target_pairs={{0,64},{1,193},{2,66},{3,195},{64,128},{65,1},{66,130},{67,3},{128... | collective-permute-start | bytes 1572872 | tf_op jit(solution)/shard_map/ppermute | solution.py:130
  74.7 4.1 %collective-permute-start.8 = (f32[512]{0:T(512)S(1)}, f32[512]{0:T(512)S(1)}, u32[]{:S(2)}, u32[]{:S(2)}) collective-permute-start(f32[512]{0:T(512)S(1)} %fusion), channel_id=1, source_target_pairs={{0,192},{1,65},{2,194},{3,67},{64,0},{65,129},{66,2},{67,131},{128... | collective-permute-start | bytes 6152 | tf_op jit(solution)/shard_map/ppermute | solution.py:149
  75.8 23.2 %collective-permute-start.29 = (bf16[512,512]{1,0:T(8,128)(2,1)}, bf16[512,512]{1,0:T(8,128)(2,1)}, u32[]{:S(2)}, u32[]{:S(2)}) collective-permute-start(bf16[512,512]{1,0:T(8,128)(2,1)} %collective-permute-done.28.refs_1_), channel_id=1, source_target_pairs={{0,64},{1,193},{2,66},{3,195},{64,128},{65,1},{66,130},{67,3},{128... | collective-permute-start | bytes 1572872 | tf_op jit(solution)/shard_map/ppermute | solution.py:130
  78.7 4.0 %collective-permute-start.7 = (f32[512]{0:T(512)S(1)}, f32[512]{0:T(512)S(1)}, u32[]{:S(2)}, u32[]{:S(2)}) collective-permute-start(f32[512]{0:T(512)S(1)} %fusion), channel_id=1, source_target_pairs={{0,128},{1,129},{2,130},{3,131},{64,192},{65,193},{66,194},{67,195... | collective-permute-start | bytes 6152 | tf_op jit(solution)/shard_map/ppermute | solution.py:149
  82.7 8.6 %collective-permute-start.6 = (f32[512]{0:T(512)S(1)}, f32[512]{0:T(512)S(1)}, u32[]{:S(2)}, u32[]{:S(2)}) collective-permute-start(f32[512]{0:T(512)S(1)} %fusion), channel_id=1, source_target_pairs={{0,64},{1,193},{2,66},{3,195},{64,128},{65,1},{66,130},{67,3},{128... | collective-permute-start | bytes 6152 | tf_op jit(solution)/shard_map/ppermute | solution.py:149
  90.4 11.2 %collective-permute-start.16 = (bf16[1024,256]{1,0:T(8,128)(2,1)}, bf16[1024,256]{1,0:T(8,128)(2,1)}, u32[]{:S(2)}, u32[]{:S(2)}) collective-permute-start(bf16[1024,256]{1,0:T(8,128)(2,1)} %collective-permute-done.14.refs_4_), channel_id=1, source_target_pairs={{0,16},{1,49},{2,18},{3,51},{4,20},{5,53},{6,22},{7,55},{8,24},{9,... | collective-permute-start | bytes 1572872 | tf_op jit(solution)/shard_map/ppermute | solution.py:139
  90.6 14.0 %collective-permute-start.17 = (bf16[1024,256]{1,0:T(8,128)(2,1)}, bf16[1024,256]{1,0:T(8,128)(2,1)}, u32[]{:S(2)}, u32[]{:S(2)}) collective-permute-start(bf16[1024,256]{1,0:T(8,128)(2,1)} %collective-permute-done.15.refs_5_), channel_id=1, source_target_pairs={{0,16},{1,49},{2,18},{3,51},{4,20},{5,53},{6,22},{7,55},{8,24},{9,... | collective-permute-start | bytes 1572872 | tf_op jit(solution)/shard_map/ppermute | solution.py:140
  91.3 19.0 %collective-permute-start.34 = (bf16[512,512]{1,0:T(8,128)(2,1)}, bf16[512,512]{1,0:T(8,128)(2,1)}, u32[]{:S(2)}, u32[]{:S(2)}) collective-permute-start(bf16[512,512]{1,0:T(8,128)(2,1)} %collective-permute-done.33.refs_1_), channel_id=1, source_target_pairs={{0,64},{1,193},{2,66},{3,195},{64,128},{65,1},{66,130},{67,3},{128... | collective-permute-start | bytes 1572872 | tf_op jit(solution)/shard_map/ppermute | solution.py:130
  91.3 7.9 %collective-permute-start.4 = (f32[1024]{0:T(1024)S(1)}, f32[1024]{0:T(1024)S(1)}, u32[]{:S(2)}, u32[]{:S(2)}) collective-permute-start(f32[1024]{0:T(1024)S(1)} %slice.62), channel_id=1, source_target_pairs={{0,1},{1,0},{2,3},{3,2},{4,5},{5,4},{6,7},{7,6},{8,9},{9,8},{10,11... | collective-permute-start | bytes 12296 | tf_op jit(solution)/shard_map/ppermute | solution.py:152
  99.0 29.2 %collective-permute-start.30 = (bf16[512,512]{1,0:T(8,128)(2,1)}, bf16[512,512]{1,0:T(8,128)(2,1)}, u32[]{:S(2)}, u32[]{:S(2)}) collective-permute-start(bf16[512,512]{1,0:T(8,128)(2,1)} %collective-permute-done.29.refs_2_), channel_id=1, source_target_pairs={{0,64},{1,193},{2,66},{3,195},{64,128},{65,1},{66,130},{67,3},{128... | collective-permute-start | bytes 1572872 | tf_op jit(solution)/shard_map/ppermute | solution.py:130
  99.2 42.0 %collective-permute-start.5 = (f32[1024]{0:T(1024)S(1)}, f32[1024]{0:T(1024)S(1)}, u32[]{:S(2)}, u32[]{:S(2)}) collective-permute-start(f32[1024]{0:T(1024)S(1)} %slice_add_fusion.1), channel_id=1, source_target_pairs={{0,2},{1,3},{2,0},{3,1},{4,6},{5,7},{6,4},{7,5},{8,10},{9,11},{10,... | collective-permute-start | bytes 12296 | tf_op jit(solution)/shard_map/ppermute | solution.py:152
  110.3 22.9 %collective-permute-start.35 = (bf16[512,512]{1,0:T(8,128)(2,1)}, bf16[512,512]{1,0:T(8,128)(2,1)S(1)}, u32[]{:S(2)}, u32[]{:S(2)}) collective-permute-start(bf16[512,512]{1,0:T(8,128)(2,1)} %collective-permute-done.34.refs_2_), channel_id=1, source_target_pairs={{0,64},{1,193},{2,66},{3,195},{64,128},{65,1},{66,130},{67,3},{128... | collective-permute-start | bytes 1572872 | tf_op jit(solution)/shard_map/ppermute | solution.py:130
  113.6 11.3 %copy-start.6 = (bf16[512,512]{1,0:T(8,128)(2,1)S(1)}, bf16[512,512]{1,0:T(8,128)(2,1)}, u32[]{:S(2)}) copy-start(bf16[512,512]{1,0:T(8,128)(2,1)} %copy-done.5) | copy-start | bytes 1572868
  113.6 11.3 %copy-start.10 = (bf16[512,512]{1,0:T(8,128)(2,1)S(1)}, bf16[512,512]{1,0:T(8,128)(2,1)}, u32[]{:S(2)}) copy-start(bf16[512,512]{1,0:T(8,128)(2,1)} %copy-done.9) | copy-start | bytes 1572868
  117.8 19.8 %collective-permute-start.21 = (bf16[1024,256]{1,0:T(8,128)(2,1)S(1)}, bf16[1024,256]{1,0:T(8,128)(2,1)S(1)}, u32[]{:S(2)}, u32[]{:S(2)}) collective-permute-start(bf16[1024,256]{1,0:T(8,128)(2,1)S(1)} %get-tuple-element.20), channel_id=1, source_target_pairs={{0,1},{1,0},{2,3},{3,2},{4,5},{5,4},{6,7},{7,6},{8,9},{9,8},{10,11... | collective-permute-start | bytes 1572872 | tf_op jit(solution)/shard_map/ppermute | solution.py:161
  128.1 10.6 %collective-permute-start.26 = (bf16[1024,256]{1,0:T(8,128)(2,1)S(1)}, bf16[1024,256]{1,0:T(8,128)(2,1)S(1)}, u32[]{:S(2)}, u32[]{:S(2)}) collective-permute-start(bf16[1024,256]{1,0:T(8,128)(2,1)S(1)} %get-tuple-element.23), channel_id=1, source_target_pairs={{0,1},{1,0},{2,3},{3,2},{4,5},{5,4},{6,7},{7,6},{8,9},{9,8},{10,11... | collective-permute-start | bytes 1572872 | tf_op jit(solution)/shard_map/ppermute | solution.py:161
  132.6 6.8 %collective-permute-start.31 = (bf16[1024,256]{1,0:T(8,128)(2,1)S(1)}, bf16[1024,256]{1,0:T(8,128)(2,1)S(1)}, u32[]{:S(2)}, u32[]{:S(2)}) collective-permute-start(bf16[1024,256]{1,0:T(8,128)(2,1)S(1)} %get-tuple-element.27), channel_id=1, source_target_pairs={{0,1},{1,0},{2,3},{3,2},{4,5},{5,4},{6,7},{7,6},{8,9},{9,8},{10,11... | collective-permute-start | bytes 1572872 | tf_op jit(solution)/shard_map/ppermute | solution.py:161
  137.5 2.9 %collective-permute-start.36 = (bf16[1024,256]{1,0:T(8,128)(2,1)S(1)}, bf16[1024,256]{1,0:T(8,128)(2,1)S(1)}, u32[]{:S(2)}, u32[]{:S(2)}) collective-permute-start(bf16[1024,256]{1,0:T(8,128)(2,1)S(1)} %get-tuple-element.31), channel_id=1, source_target_pairs={{0,1},{1,0},{2,3},{3,2},{4,5},{5,4},{6,7},{7,6},{8,9},{9,8},{10,11... | collective-permute-start | bytes 1572872 | tf_op jit(solution)/shard_map/ppermute | solution.py:161
  137.7 7.5 %collective-permute-start.22 = (bf16[1024,128]{1,0:T(8,128)(2,1)S(1)}, bf16[1024,128]{1,0:T(8,128)(2,1)S(1)}, u32[]{:S(2)}, u32[]{:S(2)}) collective-permute-start(bf16[1024,128]{1,0:T(8,128)(2,1)S(1)} %add_convert_fusion.3), channel_id=1, source_target_pairs={{0,2},{1,3},{2,0},{3,1},{4,6},{5,7},{6,4},{7,5},{8,10},{9,11},{10,... | collective-permute-start | bytes 786440 | tf_op jit(solution)/shard_map/ppermute | solution.py:163
  138.7 12.1 %collective-permute-start.27 = (bf16[1024,128]{1,0:T(8,128)(2,1)S(1)}, bf16[1024,128]{1,0:T(8,128)(2,1)S(1)}, u32[]{:S(2)}, u32[]{:S(2)}) collective-permute-start(bf16[1024,128]{1,0:T(8,128)(2,1)S(1)} %add_convert_fusion.2), channel_id=1, source_target_pairs={{0,2},{1,3},{2,0},{3,1},{4,6},{5,7},{6,4},{7,5},{8,10},{9,11},{10,... | collective-permute-start | bytes 786440 | tf_op jit(solution)/shard_map/ppermute | solution.py:163
  139.5 17.0 %collective-permute-start.32 = (bf16[1024,128]{1,0:T(8,128)(2,1)S(1)}, bf16[1024,128]{1,0:T(8,128)(2,1)S(1)}, u32[]{:S(2)}, u32[]{:S(2)}) collective-permute-start(bf16[1024,128]{1,0:T(8,128)(2,1)S(1)} %add_convert_fusion.1), channel_id=1, source_target_pairs={{0,2},{1,3},{2,0},{3,1},{4,6},{5,7},{6,4},{7,5},{8,10},{9,11},{10,... | collective-permute-start | bytes 786440 | tf_op jit(solution)/shard_map/ppermute | solution.py:163
  140.5 21.6 %collective-permute-start.37 = (bf16[1024,128]{1,0:T(8,128)(2,1)S(1)}, bf16[1024,128]{1,0:T(8,128)(2,1)S(1)}, u32[]{:S(2)}, u32[]{:S(2)}) collective-permute-start(bf16[1024,128]{1,0:T(8,128)(2,1)S(1)} %add_convert_fusion), channel_id=1, source_target_pairs={{0,2},{1,3},{2,0},{3,1},{4,6},{5,7},{6,4},{7,5},{8,10},{9,11},{10,... | collective-permute-start | bytes 786440 | tf_op jit(solution)/shard_map/ppermute | solution.py:163
  (6 other events, 13.3 us)

commit v2 on v0

v2 whole, which is shorter than its diff:
```python
import functools

import jax
import jax.numpy as jnp
from jax import lax
from jax.experimental import pallas as pl
from jax.experimental.pallas import tpu as pltpu
from jax.sharding import PartitionSpec as P

TILE = 128
F32, BF16 = jnp.float32, jnp.bfloat16
TURN = (1, -1, 1, -1)
ALONG_Y = {
    h: [(4 * y + r, 4 * ((y + h * TURN[r]) % 4) + r) for y in range(4) for r in range(4)] for h in (1, 2, 3)
}
ALONG_X = {s: [(4 * x + z, 4 * ((x + s) % 4) + z) for x in range(4) for z in range(4)] for s in (1, 3)}
ALONG_Z = {s: [(4 * x + z, 4 * x + (z + s) % 4) for x in range(4) for z in range(4)] for s in (1, 3)}
SWAP = {k: [(i, i ^ k) for i in range(4)] for k in (1, 2)}
COLS = {k: [(i, i ^ k) for i in range(16)] for k in (1, 2, 4, 8)}
VMEM = 14 << 20
TINY = pl.CostEstimate(flops=1, bytes_accessed=1, transcendentals=0)


def prep_kernel(place_ref, flags_ref, b_ref, o_ref, sum_ref, *, first):
    ones = jnp.ones((8, 512), BF16)
    block = place_ref[3] ^ (first - pl.program_id(0))
    for j in range(4):
        z = (place_ref[2] - j) & 3
        rows = pl.ds(pl.multiple_of(z * TILE, TILE), TILE)
        tiles = []
        for p in range(4):
            on = flags_ref[z, block * 4 + p] != 0
            tiles.append(jnp.where(on, b_ref[rows, TILE * p:TILE * (p + 1)], jnp.zeros((TILE, TILE), BF16)))
        line = jnp.concatenate(tiles, 1)
        o_ref[TILE * j:TILE * (j + 1), :] = line
        sum_ref[0, z] = lax.dot_general(ones, line, (((1,), (1,)), ((), ())), preferred_element_type=F32)


def prep(place, flags, b, first):
    return pl.pallas_call(
        functools.partial(prep_kernel, first=first),
        grid_spec=pltpu.PrefetchScalarGridSpec(
            num_scalar_prefetch=2,
            grid=(2,),
            in_specs=[pl.BlockSpec((512, 512), lambda i, place, flags: (0, place[3] ^ (first - i)))],
            out_specs=[
                pl.BlockSpec((512, 512), lambda i, place, flags: (0, i)),
                pl.BlockSpec((1, 4, 8, TILE), lambda i, place, flags: (i, 0, 0, 0)),
            ],
        ),
        out_shape=[jax.ShapeDtypeStruct((512, 1024), BF16), jax.ShapeDtypeStruct((2, 4, 8, TILE), F32)],
        compiler_params=pltpu.CompilerParams(vmem_limit_bytes=VMEM),
        cost_estimate=TINY,
    )(place, flags, b)


def mask_kernel(flags_ref, a_ref, o_ref):
    for k in range(8):
        rows = slice(TILE * k, TILE * (k + 1))
        o_ref[rows, :] = jnp.where(flags_ref[k] != 0, a_ref[rows, :], jnp.zeros((TILE, TILE), BF16))


def mask(flags, a):
    return pl.pallas_call(
        mask_kernel,
        grid_spec=pltpu.PrefetchScalarGridSpec(
            num_scalar_prefetch=1,
            grid=(1,),
            in_specs=[pl.BlockSpec((1024, TILE), lambda i, flags: (0, 0))],
            out_specs=pl.BlockSpec((1024, TILE), lambda i, flags: (0, 0)),
        ),
        out_shape=jax.ShapeDtypeStruct((1024, TILE), BF16),
        compiler_params=pltpu.CompilerParams(vmem_limit_bytes=VMEM),
        cost_estimate=TINY,
    )(flags, a)


def slot(place_ref, s):
    return ((place_ref[1] - place_ref[0] + s) * (1 - 2 * (place_ref[3] & 1))) & 3


def scaled(place_ref, scale_ref, piece, s):
    z = place_ref[2]
    scale = [scale_ref[slot(place_ref, s), pl.ds((z - j) & 3, 1), :] for j in range(4)]
    return (piece.astype(F32) * jnp.concatenate(scale, 1)).astype(BF16)


def row_sums(piece):
    ones = jnp.ones((8, 512), BF16)
    return lax.dot_general(ones, piece, (((1,), (1,)), ((), ())), preferred_element_type=F32)


def early_kernel(place_ref, scale_ref, own_ref, r_ref, l_ref, o_ref, sum_ref):
    total = jnp.zeros((8, 256), F32)
    for s, ref in ((0, own_ref), (1, r_ref), (3, l_ref)):
        o_ref[slot(place_ref, s)] = scaled(place_ref, scale_ref, ref[...], s)
        total += row_sums(ref[...])
    sum_ref[0] = total


SCALE = pl.BlockSpec((4, 4, TILE), lambda i, *_: (0, 0, 0))
SUMS = pl.BlockSpec((1, 8, 256), lambda i, *_: (i, 0, 0))
ROWS = pl.BlockSpec((256, 512), lambda i, *_: (i, 0))
ALL = pl.BlockSpec((4, 256, 512), lambda i, *_: (0, i, 0))
UPPER = pl.BlockSpec((256, 512), lambda i, *_: (jnp.minimum(i, 1), 0))
LOWER = pl.BlockSpec((256, 512), lambda i, *_: (jnp.maximum(i - 2, 0), 0))


def early(place, scale, pieces):
    return pl.pallas_call(
        early_kernel,
        grid_spec=pltpu.PrefetchScalarGridSpec(
            num_scalar_prefetch=1,
            grid=(4,),
            in_specs=[SCALE, ROWS, ROWS, ROWS],
            out_specs=[ALL, SUMS],
        ),
        out_shape=[jax.ShapeDtypeStruct((4, 1024, 512), BF16), jax.ShapeDtypeStruct((4, 8, 256), F32)],
        compiler_params=pltpu.CompilerParams(vmem_limit_bytes=VMEM),
        cost_estimate=TINY,
    )(place, scale, *pieces)


def multiply(a_ref, hops):
    total = jnp.dot(a_ref[0], hops[0][...], preferred_element_type=F32)
    for h in range(1, 4):
        total += jnp.dot(a_ref[h], hops[h][...], preferred_element_type=F32)
    return total


def hop_specs(q):
    return [pl.BlockSpec((512, 512), lambda i, *_: (0, q))] * 4


def opening_kernel(place_ref, scale_ref, full_ref, sums_ref, r2_ref, l2_ref, *refs):
    hops, (last_ref, o_ref, total_ref) = refs[:4], refs[4:]
    piece = jnp.where(pl.program_id(0) < 2, r2_ref[...], l2_ref[...])
    last = scaled(place_ref, scale_ref, piece, 2)
    last_ref[0] = last
    total_ref[0] = sums_ref[0] + row_sums(piece)
    missing = slot(place_ref, 2)
    lefts = [jnp.where(missing == h, last, full_ref[h]) for h in range(4)]
    o_ref[...] = multiply(lefts, hops).astype(BF16)


def opening(place, scale, full, sums, r2, l2, hops, q):
    return pl.pallas_call(
        opening_kernel,
        grid_spec=pltpu.PrefetchScalarGridSpec(
            num_scalar_prefetch=1,
            grid=(4,),
            in_specs=[SCALE, ALL, SUMS, UPPER, LOWER] + hop_specs(q),
            out_specs=[
                pl.BlockSpec((1, 256, 512), lambda i, place: (slot(place, 2), i, 0)),
                ROWS,
                SUMS,
            ],
        ),
        out_shape=[
            jax.ShapeDtypeStruct((4, 1024, 512), BF16),
            jax.ShapeDtypeStruct((1024, 512), BF16),
            jax.ShapeDtypeStruct((4, 8, 256), F32),
        ],
        input_output_aliases={2: 0},
        compiler_params=pltpu.CompilerParams(vmem_limit_bytes=VMEM),
        cost_estimate=TINY,
    )(place, scale, full, sums, r2, l2, *hops)


def product_kernel(a_ref, *refs):
    refs[4][...] = multiply(a_ref, refs[:4]).astype(refs[4].dtype)


def product(a, hops, q, dtype, start=0, steps=4):
    return pl.pallas_call(
        product_kernel,
        grid=(steps,),
        in_specs=[pl.BlockSpec((4, 256, 512), lambda i: (0, start + i, 0))] + hop_specs(q),
        out_specs=ROWS,
        out_shape=jax.ShapeDtypeStruct((256 * steps, 512), dtype),
        compiler_params=pltpu.CompilerParams(vmem_limit_bytes=VMEM),
        cost_estimate=TINY,
    )(a, *hops)


def closing_kernel(flags_ref, part_ref, upper_ref, lower_ref, chip_ref, sum_ref, more_ref, o_ref):
    core = jnp.where(pl.program_id(0) < 2, upper_ref[...], lower_ref[...])
    total = part_ref[...] + core.astype(F32)
    total += chip_ref[...].astype(F32)
    scale = jnp.float32(TILE * 256) / (1.0 + sum_ref[0] + more_ref[0])
    total *= jnp.transpose(scale)[:, 0:1]
    for k in range(2):
        rows = slice(TILE * k, TILE * (k + 1))
        for p in range(4):
            lanes = slice(TILE * p, TILE * (p + 1))
            on = flags_ref[2 * pl.program_id(0) + k, p] != 0
            o_ref[rows, lanes] = jnp.where(on, total[rows, lanes], 0.0).astype(BF16)


def closing(flags, part, upper, lower, chip, sums, more):
    return pl.pallas_call(
        closing_kernel,
        grid_spec=pltpu.PrefetchScalarGridSpec(
            num_scalar_prefetch=1,
            grid=(4,),
            in_specs=[ROWS, UPPER, LOWER, ROWS, SUMS, SUMS],
            out_specs=ROWS,
        ),
        out_shape=jax.ShapeDtypeStruct((1024, 512), BF16),
        compiler_params=pltpu.CompilerParams(vmem_limit_bytes=VMEM),
        cost_estimate=TINY,
    )(flags, part, upper, lower, chip, sums, more)


class Order:
    def __init__(self):
        self.seen = []

    def send(self, value, axes, pairs):
        others = [v for v in self.seen[-5:] if v is not value]
        if others:
            value = lax.optimization_barrier((value, *others))[0]
        return lax.ppermute(value, axes, pairs)

    def wait(self, *values):
        self.seen.extend(values)


def shards(a_weights, a_flags, b_weights, b_flags, out_flags):
    rep = lax.axis_index("rep").astype(jnp.int32)
    row = lax.axis_index("row").astype(jnp.int32)
    col = lax.axis_index("col").astype(jnp.int32)
    place = jnp.stack([col >> 2, row, col & 3, rep])
    b, bf = b_weights[0], b_flags[0]
    order = Order()

    def both(v, axis, tables):
        return order.send(v, axis, tables[1]), order.send(v, axis, tables[3])

    def onward(r, l, axis, tables):
        n = r.shape[0] // 2
        return order.send(r[:n], axis, tables[1]), order.send(l[n:], axis, tables[3])

    def send_y(v, h=1):
        return order.send(v, ("row", "rep"), ALONG_Y[h])

    a = mask(a_flags[0, :, 0], a_weights[0])
    zr, zl = both(a, "col", ALONG_Z)
    b, a = lax.optimization_barrier((b, a))
    b32, sum32 = prep(place, bf, b, 3)
    h32 = [b32, send_y(b32)]
    b10, sum10 = prep(place, bf, lax.optimization_barrier((b, sum32))[0], 1)
    h10 = [b10, send_y(b10)]
    total = (sum32[0] + sum32[1] + sum10[0] + sum10[1])[:, 0, :]
    other = order.send(total, "col", COLS[4])
    order.wait(other)
    total = total + other
    other = order.send(total, "col", COLS[8])
    order.wait(other, zr, zl)
    total = total + other
    zr2, zl2 = onward(zr, zl, "col", ALONG_Z)
    order.wait(h32[1])
    h32.append(send_y(h32[1]))
    order.wait(zr2, zl2)
    wide = jnp.concatenate([a, zr, jnp.concatenate([zr2, zl2], 0), zl], 1)
    xr, xl = both(wide, "col", ALONG_X)
    other = order.send(total, "col", COLS[1])
    order.wait(other)
    total = total + other
    other = order.send(total, "col", COLS[2])
    order.wait(other, h10[1])
    total = total + other
    walk_b = 1.0 / (1.0 + total)
    others = [send_y(walk_b, h) for h in (1, 2, 3)]
    order.wait(h32[2], *others)
    scale = jnp.stack([walk_b] + others, 0)
    h32.append(send_y(h32[2]))

    order.wait(xr, xl)
    xr2, xl2 = onward(xr, xl, "col", ALONG_X)
    h10.append(send_y(h10[1]))
    most, some = early(place, scale, (wide, xr, xl))
    full, part3, sums = opening(place, scale, most, some, xr2, xl2, h32, 0)
    order.wait(part3)
    core3 = order.send(part3, "rep", SWAP[1])
    more = order.send(sums, "rep", SWAP[1])
    order.wait(h10[2])
    part2 = product(full, [lax.optimization_barrier((h32[0], h10[2]))[0]] + h32[1:], 1, F32)
    order.wait(more, part2)
    sums = sums + more
    more = order.send(sums, "rep", SWAP[2])
    pair = (part2 + core3.astype(F32)).astype(BF16)
    chip = order.send(pair, "rep", SWAP[2])
    h10.append(send_y(h10[2]))
    h10[3] = lax.optimization_barrier((h10[3], pair))[0]
    part1 = product(full, h10, 0, BF16, 0, 2), product(full, h10, 0, BF16, 2, 2)
    part0 = product(full, h10, 1, F32)
    order.wait(part0)
    upper, lower = (order.send(v, "rep", SWAP[1]) for v in part1)
    return closing(out_flags, part0, upper, lower, chip, sums, more)


def solution(mesh):
    return jax.shard_map(
        shards,
        mesh=mesh,
        in_specs=(
            P("rep", "row", "col"),
            P("rep", "row", "col"),
            P("rep", "row", "col"),
            P("rep", "row", "col"),
            P("row", ("col", "rep")),
        ),
        out_specs=P("row", ("col", "rep")),
        check_vma=False,
    )
```

time: 379 us -> 129 us (0.34)
  blocking collectives: 162 us -> 0 us
  waiting for transfers between devices: 171 us -> 59.1 us
  starting transfers between devices: 0.09 us -> 37.2 us
  Pallas kernels: 0 us -> 26 us
  matrix products: 13.8 us -> 0 us
  between operations: 13.1 us -> 0.2 us
  other arithmetic: 12.1 us -> 1.62 us
    psum x2 -> x0, blocking collectives: 162 us -> none  [the longest x1 128 us: shards(): lax.psum(jnp.sum(a_masked, axis=(0, 2), dtype=jnp.float32), ('col', 'rep'))]
    all_gather x2 -> x0, waiting for transfers between devices: 122 us -> none  [the longest x1 86 us: shards(): lax.all_gather(walk_b, 'row', axis=1, tiled=True)[0]]
    ppermute x0 -> x27, waiting for transfers between devices: none -> 59.1 us  [send(): return lax.ppermute(value, axes, pairs)]
    reduce_scatter x1 -> x0, waiting for transfers between devices: 48.7 us -> none  [shards(): lax.psum_scatter(partial_sum.astype(jnp.bfloat16), 'rep', scatter_dimensi...]
    ppermute x0 -> x27, starting transfers between devices: none -> 37.2 us  [send(): return lax.ppermute(value, axes, pairs)]
    pallas_call x0 -> x10, Pallas kernels: none -> 26 us  [the longest x4 11.5 us: product(): pl.pallas_call(product_kernel, grid=(steps,), in_specs=[pl.BlockSpec((4,...]
    dot_general x1 -> x0, matrix products: 13.8 us -> none  [shards(): jnp.dot(left_rows, lax.all_gather(walk_b, 'row', axis=1, tiled=True)[0],...]
    convert_element_type x6 -> x1, other arithmetic: 8.61 us -> 1.39 us  [shards(): pair = (part2 + core3.astype(F32)).astype(BF16)]
  transfers between devices with their start and end apart: 3 -> 27, of which waited for: 3 -> 15; matrix products, arithmetic and copies ran while one was open for 3% -> 1% of each run, Pallas kernels for 0% -> 15%
where the time goes in v2:
time: 129 us; the launch traced here: 128 us
  waiting for transfers between devices  59.1 us (46%)
  starting transfers between devices  37.2 us (29%)
  Pallas kernels  26 us (20%)
  local copies, waits for them, and re-layouts  4.08 us (3%)
  other arithmetic  1.62 us (1%)
    ppermute x27, waiting for transfers between devices, send(): return lax.ppermute(value, axes, pairs)  59.1 us
    ppermute x27, starting transfers between devices, send(): return lax.ppermute(value, axes, pairs)  37.2 us
    pallas_call x4, Pallas kernels, product(): pl.pallas_call(product_kernel, grid=(steps,), in_specs=[pl.BlockSpec((4,...  11.5 us
    pallas_call x1, Pallas kernels, closing(): pl.pallas_call(closing_kernel, grid_spec=pltpu.PrefetchScalarGridSpec(num...  4.54 us
    pallas_call x1, Pallas kernels, opening(): pl.pallas_call(opening_kernel, grid_spec=pltpu.PrefetchScalarGridSpec(num...  4.28 us
    unnamed x11, local copies, waits for them, and re-layouts  3.97 us
    pallas_call x1, Pallas kernels, early(): pl.pallas_call(early_kernel, grid_spec=pltpu.PrefetchScalarGridSpec(num_s...  2.61 us
  transfers between devices with their start and end apart: 27, of which 15 were waited for; matrix products, arithmetic and copies ran while one was open for 1% of the time, Pallas kernels for 15%

profile of v2, /device:TPU:1, one launch (start us, length us, event | category | flops | bytes accessed | tf_op | source)
XLA Modules:
  0.0 128.3 jit_solution(1386656699329388565)
XLA Ops:
  0.0 0.9 copy-done.1
  1.0 0.7 copy-done.3
  1.6 0.6 shard_map.55
  2.3 1.6 %copy-done = bf16[1,512,2048]{2,1,0:T(8,128)(2,1)S(1)} copy-done((bf16[1,512,2048]{2,1,0:T(8,128)(2,1)S(1)}, bf16[1,512,2048]{2,1,0:T(8,128)(2,1)}, u32[]{:S(2)}) %copy-start) | copy-done | bytes 2097176
  3.9 0.7 copy-done.2
  4.6 1.2 shard_map.56
  5.8 3.6 %collective-permute-start.4 = (bf16[512,1024]{1,0:T(8,128)(2,1)S(1)}, bf16[512,1024]{1,0:T(8,128)(2,1)S(1)}, u32[]{:S(2)}, u32[]{:S(2)}) collective-permute-start(bf16[512,1024]{1,0:T(8,128)(2,1)S(1)} %get-tuple-element.63.refs_0_), channel_id=1, source_target_pairs={{0,64},{1,193},{2,66},{3,195},{64,128},{65,1},{66,130},{67,3},{128... | collective-permute-start | bytes 3145736 | tf_op jit(solution)/shard_map/ppermute | solution.py:223
  9.4 6.0 %collective-permute-start.3 = (bf16[1024,128]{1,0:T(8,128)(2,1)S(1)}, bf16[1024,128]{1,0:T(8,128)(2,1)S(1)}, u32[]{:S(2)}, u32[]{:S(2)}) collective-permute-start(bf16[1024,128]{1,0:T(8,128)(2,1)S(1)} %shard_map.55), channel_id=1, source_target_pairs={{0,12},{4,0},{8,4},{12,8},{16,28},{20,16},{24,20},{28,24},{32,44},... | collective-permute-start | bytes 786440 | tf_op jit(solution)/shard_map/ppermute | solution.py:223
  15.5 1.2 shard_map.57
  16.8 1.3 %collective-permute-start = (f32[4,128]{1,0:T(4,128)S(1)}, f32[4,128]{1,0:T(4,128)S(1)}, u32[]{:S(2)}, u32[]{:S(2)}) collective-permute-start(f32[4,128]{1,0:T(4,128)S(1)} %slice_bitcast_fusion), channel_id=1, source_target_pairs={{0,16},{4,20},{8,24},{12,28},{16,0},{20,4},{24,8},{28,12},{32,48},... | collective-permute-start | bytes 6152 | tf_op jit(solution)/shard_map/ppermute | solution.py:223
  18.1 0.5 collective-permute-start.9
  18.5 1.1 collective-permute-done
  19.6 2.7 %collective-permute-start.1 = (f32[4,128]{1,0:T(4,128)S(1)}, f32[4,128]{1,0:T(4,128)S(1)}, u32[]{:S(2)}, u32[]{:S(2)}) collective-permute-start(f32[4,128]{1,0:T(4,128)S(1)} %fusion.1), channel_id=1, source_target_pairs={{0,32},{4,36},{8,40},{12,44},{16,48},{20,52},{24,56},{28,60},{32,0... | collective-permute-start | bytes 6152 | tf_op jit(solution)/shard_map/ppermute | solution.py:223
  22.3 1.5 %collective-permute-done.1 = f32[4,128]{1,0:T(4,128)S(1)} collective-permute-done((f32[4,128]{1,0:T(4,128)S(1)}, f32[4,128]{1,0:T(4,128)S(1)}, u32[]{:S(2)}, u32[]{:S(2)}) %collective-permute-start.1) | collective-permute-done | bytes 2080 | tf_op jit(solution)/shard_map/ppermute | solution.py:223
  23.8 3.4 %collective-permute-done.3 = bf16[1024,128]{1,0:T(8,128)(2,1)S(1)} collective-permute-done((bf16[1024,128]{1,0:T(8,128)(2,1)S(1)}, bf16[1024,128]{1,0:T(8,128)(2,1)S(1)}, u32[]{:S(2)}, u32[]{:S(2)}) %collective-permute-start.3) | collective-permute-done | bytes 262176 | tf_op jit(solution)/shard_map/ppermute | solution.py:223
  27.3 4.3 %collective-permute-start.6 = (bf16[512,128]{1,0:T(8,128)(2,1)S(1)}, bf16[512,128]{1,0:T(8,128)(2,1)S(1)}, u32[]{:S(2)}, u32[]{:S(2)}) collective-permute-start(bf16[512,128]{1,0:T(8,128)(2,1)S(1)} %slice.42), channel_id=1, source_target_pairs={{0,12},{4,0},{8,4},{12,8},{16,28},{20,16},{24,20},{28,24},{32,44},... | collective-permute-start | bytes 393224 | tf_op jit(solution)/shard_map/ppermute | solution.py:223
  31.6 0.1 collective-permute-start.5
  31.7 5.5 %collective-permute-done.6 = bf16[512,128]{1,0:T(8,128)(2,1)S(1)} collective-permute-done((bf16[512,128]{1,0:T(8,128)(2,1)S(1)}, bf16[512,128]{1,0:T(8,128)(2,1)S(1)}, u32[]{:S(2)}, u32[]{:S(2)}) %collective-permute-start.6) | collective-permute-done | bytes 131104 | tf_op jit(solution)/shard_map/ppermute | solution.py:223
  37.1 3.8 %collective-permute-done.5 = bf16[512,128]{1,0:T(8,128)(2,1)S(1)} collective-permute-done((bf16[512,128]{1,0:T(8,128)(2,1)S(1)}, bf16[512,128]{1,0:T(8,128)(2,1)S(1)}, u32[]{:S(2)}, u32[]{:S(2)}) %collective-permute-start.5) | collective-permute-done | bytes 131104 | tf_op jit(solution)/shard_map/ppermute | solution.py:223
  40.9 0.1 pad_maximum_fusion.own_ref
  41.1 2.6 %collective-permute-start.14 = (bf16[1024,512]{1,0:T(8,128)(2,1)S(1)}, bf16[1024,512]{1,0:T(8,128)(2,1)S(1)}, u32[]{:S(2)}, u32[]{:S(2)}) collective-permute-start(bf16[1024,512]{1,0:T(8,128)(2,1)S(1)} %pad_maximum_fusion.own_ref), channel_id=1, source_target_pairs={{0,48},{4,52},{8,56},{12,60},{16,0},{20,4},{24,8},{28,12},{32,16},... | collective-permute-start | bytes 3145736 | tf_op jit(solution)/shard_map/ppermute | solution.py:223
  43.6 3.6 %collective-permute-done.7 = f32[4,128]{1,0:T(4,128)S(1)} collective-permute-done((f32[4,128]{1,0:T(4,128)S(1)}, f32[4,128]{1,0:T(4,128)S(1)}, u32[]{:S(2)}, u32[]{:S(2)}) %collective-permute-start.7) | collective-permute-done | bytes 2080 | tf_op jit(solution)/shard_map/ppermute | solution.py:223
  47.2 0.4 collective-permute-start.8
  47.6 5.9 %collective-permute-done.8 = f32[4,128]{1,0:T(4,128)S(1)} collective-permute-done((f32[4,128]{1,0:T(4,128)S(1)}, f32[4,128]{1,0:T(4,128)S(1)}, u32[]{:S(2)}, u32[]{:S(2)}) %collective-permute-start.8) | collective-permute-done | bytes 2080 | tf_op jit(solution)/shard_map/ppermute | solution.py:223
  53.6 0.1 collective-permute-start.10
  53.6 4.1 %collective-permute-start.11 = (f32[4,128]{1,0:T(4,128)S(1)}, f32[4,128]{1,0:T(4,128)S(1)}, u32[]{:S(2)}, u32[]{:S(2)}) collective-permute-start(f32[4,128]{1,0:T(4,128)S(1)} %add_divide_fusion), channel_id=1, source_target_pairs={{0,128},{1,129},{2,130},{3,131},{64,192},{65,193},{66,194},{67,195... | collective-permute-start | bytes 6152 | tf_op jit(solution)/shard_map/ppermute | solution.py:223
  57.7 0.9 collective-permute-start.12
  58.7 3.0 %collective-permute-done.12 = f32[4,128]{1,0:T(4,128)S(1)} collective-permute-done((f32[4,128]{1,0:T(4,128)S(1)}, f32[4,128]{1,0:T(4,128)S(1)}, u32[]{:S(2)}, u32[]{:S(2)}) %collective-permute-start.12) | collective-permute-done | bytes 2080 | tf_op jit(solution)/shard_map/ppermute | solution.py:223
  61.7 2.9 %collective-permute-done.14.l_ref = bf16[1024,512]{1,0:T(8,128)(2,1)S(1)} collective-permute-done((bf16[1024,512]{1,0:T(8,128)(2,1)S(1)}, bf16[1024,512]{1,0:T(8,128)(2,1)S(1)}, u32[]{:S(2)}, u32[]{:S(2)}) %collective-permute-start.14) | collective-permute-done | bytes 1048608 | tf_op jit(solution)/shard_map/ppermute | solution.py:223
  64.6 3.1 %collective-permute-done.13.r_ref = bf16[1024,512]{1,0:T(8,128)(2,1)S(1)} collective-permute-done((bf16[1024,512]{1,0:T(8,128)(2,1)S(1)}, bf16[1024,512]{1,0:T(8,128)(2,1)S(1)}, u32[]{:S(2)}, u32[]{:S(2)}) %collective-permute-start.13) | collective-permute-done | bytes 1048608 | tf_op jit(solution)/shard_map/ppermute | solution.py:223
  67.7 0.4 collective-permute-start.16
  68.1 1.1 collective-permute-start.15
  69.3 2.6 %shard_map.58 = (bf16[4,1024,512]{2,1,0:T(8,128)(2,1)S(1)}, f32[4,8,256]{2,1,0:T(8,128)S(1)}) custom-call(s32[4]{0:T(128)S(1)} %pad_add_fusion.place_ref, f32[4,4,128]{2,1,0:T(4,128)S(1)} %pad_maximum_fusion.1.scale_ref, bf16[1024,512]{1,0:T(8,128)(2,1)S(1)} %pad_maximum_fusion.own_ref, bf16[1024,512]{1,0:T(8,128)(2,1)S(1)} %collective-permute-done.13.r_ref, ...), custom_call_target="tpu_custom_call" | custom-call | flops 1 | bytes 1 | tf_op jit(solution)/shard_map/pallas_call | solution.py:110
  71.9 6.5 %collective-permute-done.16.l2_ref = bf16[512,512]{1,0:T(8,128)(2,1)S(1)} collective-permute-done((bf16[512,512]{1,0:T(8,128)(2,1)S(1)}, bf16[512,512]{1,0:T(8,128)(2,1)S(1)}, u32[]{:S(2)}, u32[]{:S(2)}) %collective-permute-start.16) | collective-permute-done | bytes 524320 | tf_op jit(solution)/shard_map/ppermute | solution.py:223
  78.4 1.7 %collective-permute-done.15.r2_ref = bf16[512,512]{1,0:T(8,128)(2,1)S(1)} collective-permute-done((bf16[512,512]{1,0:T(8,128)(2,1)S(1)}, bf16[512,512]{1,0:T(8,128)(2,1)S(1)}, u32[]{:S(2)}, u32[]{:S(2)}) %collective-permute-start.15) | collective-permute-done | bytes 524320 | tf_op jit(solution)/shard_map/ppermute | solution.py:223
  80.1 4.3 %shard_map.59 = (bf16[4,1024,512]{2,1,0:T(8,128)(2,1)S(1)}, bf16[1024,512]{1,0:T(8,128)(2,1)S(1)}, f32[4,8,256]{2,1,0:T(8,128)S(1)}) custom-call(s32[4]{0:T(128)S(1)} %pad_add_fusion.place_ref, f32[4,4,128]{2,1,0:T(4,128)S(1)} %pad_maximum_fusion.1.scale_ref, bf16[4,1024,512]{2,1,0:T(8,128)(2,1)S(1)} %get-tuple-element.52.full_ref, ...), custom_call_target="tpu_custom_call", output_to_operand_aliasing={{0}: (2, {})} | custom-call | flops 1 | bytes 1 | tf_op jit(solution)/shard_map/pallas_call | solution.py:147
  84.4 3.7 %collective-permute-start.22 = (bf16[1024,512]{1,0:T(8,128)(2,1)S(1)}, bf16[1024,512]{1,0:T(8,128)(2,1)S(1)}, u32[]{:S(2)}, u32[]{:S(2)}) collective-permute-start(bf16[1024,512]{1,0:T(8,128)(2,1)S(1)} %get-tuple-element.65), channel_id=1, source_target_pairs={{0,1},{1,0},{2,3},{3,2},{4,5},{5,4},{6,7},{7,6},{8,9},{9,8},{10,11... | collective-permute-start | bytes 3145736 | tf_op jit(solution)/shard_map/ppermute | solution.py:223
  88.1 0.1 collective-permute-start.20
  88.2 3.3 %shard_map.60 = f32[1024,512]{1,0:T(8,128)S(1)} custom-call(bf16[4,1024,512]{2,1,0:T(8,128)(2,1)S(1)} %get-tuple-element.58.a_ref, bf16[512,1024]{1,0:T(8,128)(2,1)S(1)} %get-tuple-element.63.refs_0_, bf16[512,1024]{1,0:T(8,128)(2,1)S(1)} %collective-permute-done.4.refs_1_, bf16[512,1024]{1,0:T(8,128)(2,1)S(1)} %collective-permute-done.17.refs_2_, ...), custom_call_target="tpu_custom_call" | custom-call | flops 1 | bytes 1 | tf_op jit(solution)/shard_map/pallas_call | solution.py:175
  91.7 1.4 %add_convert_fusion = bf16[1024,512]{1,0:T(8,128)(2,1)} fusion(f32[1024,512]{1,0:T(8,128)S(1)} %shard_map.60, bf16[1024,512]{1,0:T(8,128)(2,1)S(1)} %collective-permute-done.22), kind=kLoop, calls=%fused_computation | loop fusion | flops 1572864 | bytes 4194304 | tf_op jit(solution)/shard_map/convert_element_type | solution.py:292
  93.1 0.3 collective-permute-start.25
  93.4 14.5 %collective-permute-done.21.refs_3_ = bf16[512,1024]{1,0:T(8,128)(2,1)S(1)} collective-permute-done((bf16[512,1024]{1,0:T(8,128)(2,1)S(1)}, bf16[512,1024]{1,0:T(8,128)(2,1)S(1)}, u32[]{:S(2)}, u32[]{:S(2)}) %collective-permute-start.21) | collective-permute-done | bytes 1048608 | tf_op jit(solution)/shard_map/ppermute | solution.py:223
  107.9 2.4 %shard_map.63 = bf16[512,512]{1,0:T(8,128)(2,1)} custom-call(bf16[4,1024,512]{2,1,0:T(8,128)(2,1)S(1)} %get-tuple-element.58.a_ref, bf16[512,1024]{1,0:T(8,128)(2,1)S(1)} %get-tuple-element.48.refs_0_, bf16[512,1024]{1,0:T(8,128)(2,1)S(1)} %collective-permute-done.9.refs_1_, bf16[512,1024]{1,0:T(8,128)(2,1)S(1)} %collective-permute-done.19.refs_2_, ...), custom_call_target="tpu_custom_call" | custom-call | flops 1 | bytes 1 | tf_op jit(solution)/shard_map/pallas_call | solution.py:175
  110.3 3.3 %shard_map.61.part_ref = f32[1024,512]{1,0:T(8,128)S(1)} custom-call(bf16[4,1024,512]{2,1,0:T(8,128)(2,1)S(1)} %get-tuple-element.58.a_ref, bf16[512,1024]{1,0:T(8,128)(2,1)S(1)} %get-tuple-element.48.refs_0_, bf16[512,1024]{1,0:T(8,128)(2,1)S(1)} %collective-permute-done.9.refs_1_, bf16[512,1024]{1,0:T(8,128)(2,1)S(1)} %collective-permute-done.19.refs_2_, ...), custom_call_target="tpu_custom_call" | custom-call | flops 1 | bytes 1 | tf_op jit(solution)/shard_map/pallas_call | solution.py:175
  113.7 4.8 %collective-permute-start.24 = (bf16[512,512]{1,0:T(8,128)(2,1)}, bf16[512,512]{1,0:T(8,128)(2,1)}, u32[]{:S(2)}, u32[]{:S(2)}) collective-permute-start(bf16[512,512]{1,0:T(8,128)(2,1)} %shard_map.63), channel_id=1, source_target_pairs={{0,1},{1,0},{2,3},{3,2},{4,5},{5,4},{6,7},{7,6},{8,9},{9,8},{10,11... | collective-permute-start | bytes 1572872 | tf_op jit(solution)/shard_map/ppermute | solution.py:223
  118.4 2.4 %shard_map.62 = bf16[512,512]{1,0:T(8,128)(2,1)} custom-call(bf16[4,1024,512]{2,1,0:T(8,128)(2,1)S(1)} %get-tuple-element.58.a_ref, bf16[512,1024]{1,0:T(8,128)(2,1)S(1)} %get-tuple-element.48.refs_0_, bf16[512,1024]{1,0:T(8,128)(2,1)S(1)} %collective-permute-done.9.refs_1_, bf16[512,1024]{1,0:T(8,128)(2,1)S(1)} %collective-permute-done.19.refs_2_, ...), custom_call_target="tpu_custom_call" | custom-call | flops 1 | bytes 1 | tf_op jit(solution)/shard_map/pallas_call | solution.py:175
  121.1 2.7 %collective-permute-done.26.more_ref = f32[4,8,256]{2,1,0:T(8,128)S(1)} collective-permute-done((f32[4,8,256]{2,1,0:T(8,128)S(1)}, f32[4,8,256]{2,1,0:T(8,128)S(1)}, u32[]{:S(2)}, u32[]{:S(2)}) %collective-permute-start.26) | collective-permute-done | bytes 32800 | tf_op jit(solution)/shard_map/ppermute | solution.py:223
  123.7 4.5 %shard_map.64 = bf16[1024,512]{1,0:T(8,128)(2,1)} custom-call(s32[8,4]{1,0:T(8,128)S(1)} %copy.11.flags_ref, f32[1024,512]{1,0:T(8,128)S(1)} %shard_map.61.part_ref, bf16[512,512]{1,0:T(8,128)(2,1)} %collective-permute-done.23.upper_ref, bf16[512,512]{1,0:T(8,128)(2,1)} %collective-permute-done.24.lower_ref, ...), custom_call_target="tpu_custom_call" | custom-call | flops 1 | bytes 1 | tf_op jit(solution)/shard_map/pallas_call | solution.py:201
  (44 shorter events, 0.7 us)
Async XLA Ops:
  0.0 0.9 copy-start.1
  1.0 0.7 copy-start.3
  2.3 1.6 %copy-start = (bf16[1,512,2048]{2,1,0:T(8,128)(2,1)S(1)}, bf16[1,512,2048]{2,1,0:T(8,128)(2,1)}, u32[]{:S(2)}) copy-start(bf16[1,512,2048]{2,1,0:T(8,128)(2,1)} %param.7) | copy-start | bytes 6291460
  3.9 0.7 copy-start.2
  5.8 21.5 %collective-permute-start.4 = (bf16[512,1024]{1,0:T(8,128)(2,1)S(1)}, bf16[512,1024]{1,0:T(8,128)(2,1)S(1)}, u32[]{:S(2)}, u32[]{:S(2)}) collective-permute-start(bf16[512,1024]{1,0:T(8,128)(2,1)S(1)} %get-tuple-element.63.refs_0_), channel_id=1, source_target_pairs={{0,64},{1,193},{2,66},{3,195},{64,128},{65,1},{66,130},{67,3},{128... | collective-permute-start | bytes 3145736 | tf_op jit(solution)/shard_map/ppermute | solution.py:223
  9.4 17.8 %collective-permute-start.3 = (bf16[1024,128]{1,0:T(8,128)(2,1)S(1)}, bf16[1024,128]{1,0:T(8,128)(2,1)S(1)}, u32[]{:S(2)}, u32[]{:S(2)}) collective-permute-start(bf16[1024,128]{1,0:T(8,128)(2,1)S(1)} %shard_map.55), channel_id=1, source_target_pairs={{0,12},{4,0},{8,4},{12,8},{16,28},{20,16},{24,20},{28,24},{32,44},... | collective-permute-start | bytes 786440 | tf_op jit(solution)/shard_map/ppermute | solution.py:223
  15.5 11.8 %collective-permute-start.2 = (bf16[1024,128]{1,0:T(8,128)(2,1)S(1)}, bf16[1024,128]{1,0:T(8,128)(2,1)S(1)}, u32[]{:S(2)}, u32[]{:S(2)}) collective-permute-start(bf16[1024,128]{1,0:T(8,128)(2,1)S(1)} %shard_map.55), channel_id=1, source_target_pairs={{0,4},{4,8},{8,12},{12,0},{16,20},{20,24},{24,28},{28,16},{32,36},... | collective-permute-start | bytes 786440 | tf_op jit(solution)/shard_map/ppermute | solution.py:223
  16.8 2.8 %collective-permute-start = (f32[4,128]{1,0:T(4,128)S(1)}, f32[4,128]{1,0:T(4,128)S(1)}, u32[]{:S(2)}, u32[]{:S(2)}) collective-permute-start(f32[4,128]{1,0:T(4,128)S(1)} %slice_bitcast_fusion), channel_id=1, source_target_pairs={{0,16},{4,20},{8,24},{12,28},{16,0},{20,4},{24,8},{28,12},{32,48},... | collective-permute-start | bytes 6152 | tf_op jit(solution)/shard_map/ppermute | solution.py:223
  18.1 35.5 %collective-permute-start.9 = (bf16[512,1024]{1,0:T(8,128)(2,1)S(1)}, bf16[512,1024]{1,0:T(8,128)(2,1)S(1)}, u32[]{:S(2)}, u32[]{:S(2)}) collective-permute-start(bf16[512,1024]{1,0:T(8,128)(2,1)S(1)} %get-tuple-element.48.refs_0_), channel_id=1, source_target_pairs={{0,64},{1,193},{2,66},{3,195},{64,128},{65,1},{66,130},{67,3},{128... | collective-permute-start | bytes 3145736 | tf_op jit(solution)/shard_map/ppermute | solution.py:223
  19.6 4.2 %collective-permute-start.1 = (f32[4,128]{1,0:T(4,128)S(1)}, f32[4,128]{1,0:T(4,128)S(1)}, u32[]{:S(2)}, u32[]{:S(2)}) collective-permute-start(f32[4,128]{1,0:T(4,128)S(1)} %fusion.1), channel_id=1, source_target_pairs={{0,32},{4,36},{8,40},{12,44},{16,48},{20,52},{24,56},{28,60},{32,0... | collective-permute-start | bytes 6152 | tf_op jit(solution)/shard_map/ppermute | solution.py:223
  27.3 34.4 %collective-permute-start.17 = (bf16[512,1024]{1,0:T(8,128)(2,1)S(1)}, bf16[512,1024]{1,0:T(8,128)(2,1)S(1)}, u32[]{:S(2)}, u32[]{:S(2)}) collective-permute-start(bf16[512,1024]{1,0:T(8,128)(2,1)S(1)} %collective-permute-done.4.refs_1_), channel_id=1, source_target_pairs={{0,64},{1,193},{2,66},{3,195},{64,128},{65,1},{66,130},{67,3},{128... | collective-permute-start | bytes 3145736 | tf_op jit(solution)/shard_map/ppermute | solution.py:223
  27.3 9.8 %collective-permute-start.6 = (bf16[512,128]{1,0:T(8,128)(2,1)S(1)}, bf16[512,128]{1,0:T(8,128)(2,1)S(1)}, u32[]{:S(2)}, u32[]{:S(2)}) collective-permute-start(bf16[512,128]{1,0:T(8,128)(2,1)S(1)} %slice.42), channel_id=1, source_target_pairs={{0,12},{4,0},{8,4},{12,8},{16,28},{20,16},{24,20},{28,24},{32,44},... | collective-permute-start | bytes 393224 | tf_op jit(solution)/shard_map/ppermute | solution.py:223
  31.6 9.4 %collective-permute-start.5 = (bf16[512,128]{1,0:T(8,128)(2,1)S(1)}, bf16[512,128]{1,0:T(8,128)(2,1)S(1)}, u32[]{:S(2)}, u32[]{:S(2)}) collective-permute-start(bf16[512,128]{1,0:T(8,128)(2,1)S(1)} %slice.41), channel_id=1, source_target_pairs={{0,4},{4,8},{8,12},{12,0},{16,20},{20,24},{24,28},{28,16},{32,36},... | collective-permute-start | bytes 393224 | tf_op jit(solution)/shard_map/ppermute | solution.py:223
  41.1 23.5 %collective-permute-start.14 = (bf16[1024,512]{1,0:T(8,128)(2,1)S(1)}, bf16[1024,512]{1,0:T(8,128)(2,1)S(1)}, u32[]{:S(2)}, u32[]{:S(2)}) collective-permute-start(bf16[1024,512]{1,0:T(8,128)(2,1)S(1)} %pad_maximum_fusion.own_ref), channel_id=1, source_target_pairs={{0,48},{4,52},{8,56},{12,60},{16,0},{20,4},{24,8},{28,12},{32,16},... | collective-permute-start | bytes 3145736 | tf_op jit(solution)/shard_map/ppermute | solution.py:223
  43.6 24.1 %collective-permute-start.13 = (bf16[1024,512]{1,0:T(8,128)(2,1)S(1)}, bf16[1024,512]{1,0:T(8,128)(2,1)S(1)}, u32[]{:S(2)}, u32[]{:S(2)}) collective-permute-start(bf16[1024,512]{1,0:T(8,128)(2,1)S(1)} %pad_maximum_fusion.own_ref), channel_id=1, source_target_pairs={{0,16},{4,20},{8,24},{12,28},{16,32},{20,36},{24,40},{28,44},{32,4... | collective-permute-start | bytes 3145736 | tf_op jit(solution)/shard_map/ppermute | solution.py:223
  43.6 3.6 %collective-permute-start.7 = (f32[4,128]{1,0:T(4,128)S(1)}, f32[4,128]{1,0:T(4,128)S(1)}, u32[]{:S(2)}, u32[]{:S(2)}) collective-permute-start(f32[4,128]{1,0:T(4,128)S(1)} %add.40), channel_id=1, source_target_pairs={{0,4},{4,0},{8,12},{12,8},{16,20},{20,16},{24,28},{28,24},{32,36},... | collective-permute-start | bytes 6152 | tf_op jit(solution)/shard_map/ppermute | solution.py:223
  47.2 6.3 %collective-permute-start.8 = (f32[4,128]{1,0:T(4,128)S(1)}, f32[4,128]{1,0:T(4,128)S(1)}, u32[]{:S(2)}, u32[]{:S(2)}) collective-permute-start(f32[4,128]{1,0:T(4,128)S(1)} %add.41), channel_id=1, source_target_pairs={{0,8},{4,12},{8,0},{12,4},{16,24},{20,28},{24,16},{28,20},{32,40},... | collective-permute-start | bytes 6152 | tf_op jit(solution)/shard_map/ppermute | solution.py:223
  53.6 4.2 %collective-permute-start.10 = (f32[4,128]{1,0:T(4,128)S(1)}, f32[4,128]{1,0:T(4,128)S(1)}, u32[]{:S(2)}, u32[]{:S(2)}) collective-permute-start(f32[4,128]{1,0:T(4,128)S(1)} %add_divide_fusion), channel_id=1, source_target_pairs={{0,64},{1,193},{2,66},{3,195},{64,128},{65,1},{66,130},{67,3},{128... | collective-permute-start | bytes 6152 | tf_op jit(solution)/shard_map/ppermute | solution.py:223
  53.6 5.0 %collective-permute-start.11 = (f32[4,128]{1,0:T(4,128)S(1)}, f32[4,128]{1,0:T(4,128)S(1)}, u32[]{:S(2)}, u32[]{:S(2)}) collective-permute-start(f32[4,128]{1,0:T(4,128)S(1)} %add_divide_fusion), channel_id=1, source_target_pairs={{0,128},{1,129},{2,130},{3,131},{64,192},{65,193},{66,194},{67,195... | collective-permute-start | bytes 6152 | tf_op jit(solution)/shard_map/ppermute | solution.py:223
  57.7 3.9 %collective-permute-start.12 = (f32[4,128]{1,0:T(4,128)S(1)}, f32[4,128]{1,0:T(4,128)S(1)}, u32[]{:S(2)}, u32[]{:S(2)}) collective-permute-start(f32[4,128]{1,0:T(4,128)S(1)} %add_divide_fusion), channel_id=1, source_target_pairs={{0,192},{1,65},{2,194},{3,67},{64,0},{65,129},{66,2},{67,131},{128... | collective-permute-start | bytes 6152 | tf_op jit(solution)/shard_map/ppermute | solution.py:223
  61.7 18.5 %collective-permute-start.18 = (bf16[512,1024]{1,0:T(8,128)(2,1)S(1)}, bf16[512,1024]{1,0:T(8,128)(2,1)S(1)}, u32[]{:S(2)}, u32[]{:S(2)}) collective-permute-start(bf16[512,1024]{1,0:T(8,128)(2,1)S(1)} %collective-permute-done.17.refs_2_), channel_id=1, source_target_pairs={{0,64},{1,193},{2,66},{3,195},{64,128},{65,1},{66,130},{67,3},{128... | collective-permute-start | bytes 3145736 | tf_op jit(solution)/shard_map/ppermute | solution.py:223
  67.7 10.7 %collective-permute-start.16 = (bf16[512,512]{1,0:T(8,128)(2,1)S(1)}, bf16[512,512]{1,0:T(8,128)(2,1)S(1)}, u32[]{:S(2)}, u32[]{:S(2)}) collective-permute-start(bf16[512,512]{1,0:T(8,128)(2,1)S(1)} %slice.44), channel_id=1, source_target_pairs={{0,48},{4,52},{8,56},{12,60},{16,0},{20,4},{24,8},{28,12},{32,16},... | collective-permute-start | bytes 1572872 | tf_op jit(solution)/shard_map/ppermute | solution.py:223
  68.1 12.0 %collective-permute-start.15 = (bf16[512,512]{1,0:T(8,128)(2,1)S(1)}, bf16[512,512]{1,0:T(8,128)(2,1)S(1)}, u32[]{:S(2)}, u32[]{:S(2)}) collective-permute-start(bf16[512,512]{1,0:T(8,128)(2,1)S(1)} %slice.43), channel_id=1, source_target_pairs={{0,16},{4,20},{8,24},{12,28},{16,32},{20,36},{24,40},{28,44},{32,4... | collective-permute-start | bytes 1572872 | tf_op jit(solution)/shard_map/ppermute | solution.py:223
  69.3 19.0 %collective-permute-start.19 = (bf16[512,1024]{1,0:T(8,128)(2,1)S(1)}, bf16[512,1024]{1,0:T(8,128)(2,1)S(1)}, u32[]{:S(2)}, u32[]{:S(2)}) collective-permute-start(bf16[512,1024]{1,0:T(8,128)(2,1)S(1)} %collective-permute-done.9.refs_1_), channel_id=1, source_target_pairs={{0,64},{1,193},{2,66},{3,195},{64,128},{65,1},{66,130},{67,3},{128... | collective-permute-start | bytes 3145736 | tf_op jit(solution)/shard_map/ppermute | solution.py:223
  84.4 7.3 %collective-permute-start.22 = (bf16[1024,512]{1,0:T(8,128)(2,1)S(1)}, bf16[1024,512]{1,0:T(8,128)(2,1)S(1)}, u32[]{:S(2)}, u32[]{:S(2)}) collective-permute-start(bf16[1024,512]{1,0:T(8,128)(2,1)S(1)} %get-tuple-element.65), channel_id=1, source_target_pairs={{0,1},{1,0},{2,3},{3,2},{4,5},{5,4},{6,7},{7,6},{8,9},{9,8},{10,11... | collective-permute-start | bytes 3145736 | tf_op jit(solution)/shard_map/ppermute | solution.py:223
  88.1 3.4 %collective-permute-start.20 = (f32[4,8,256]{2,1,0:T(8,128)S(1)}, f32[4,8,256]{2,1,0:T(8,128)S(1)}, u32[]{:S(2)}, u32[]{:S(2)}) collective-permute-start(f32[4,8,256]{2,1,0:T(8,128)S(1)} %get-tuple-element.62), channel_id=1, source_target_pairs={{0,1},{1,0},{2,3},{3,2},{4,5},{5,4},{6,7},{7,6},{8,9},{9,8},{10,11... | collective-permute-start | bytes 98312 | tf_op jit(solution)/shard_map/ppermute | solution.py:223
  91.6 16.3 %collective-permute-start.21 = (bf16[512,1024]{1,0:T(8,128)(2,1)S(1)}, bf16[512,1024]{1,0:T(8,128)(2,1)S(1)}, u32[]{:S(2)}, u32[]{:S(2)}) collective-permute-start(bf16[512,1024]{1,0:T(8,128)(2,1)S(1)} %collective-permute-done.19.refs_2_), channel_id=1, source_target_pairs={{0,64},{1,193},{2,66},{3,195},{64,128},{65,1},{66,130},{67,3},{128... | collective-permute-start | bytes 3145736 | tf_op jit(solution)/shard_map/ppermute | solution.py:223
  93.1 30.6 %collective-permute-start.25 = (bf16[1024,512]{1,0:T(8,128)(2,1)}, bf16[1024,512]{1,0:T(8,128)(2,1)S(1)}, u32[]{:S(2)}, u32[]{:S(2)}) collective-permute-start(bf16[1024,512]{1,0:T(8,128)(2,1)} %add_convert_fusion), channel_id=1, source_target_pairs={{0,2},{1,3},{2,0},{3,1},{4,6},{5,7},{6,4},{7,5},{8,10},{9,11},{10,... | collective-permute-start | bytes 3145736 | tf_op jit(solution)/shard_map/ppermute | solution.py:223
  113.6 7.3 %copy-start.4 = (s32[8,4]{0,1:T(4,128)S(1)}, s32[8,4]{0,1:T(4,128)}, u32[]{:S(2)}) copy-start(s32[8,4]{0,1:T(4,128)} %param.9) | copy-start | bytes 388
  113.7 10.1 %collective-permute-start.24 = (bf16[512,512]{1,0:T(8,128)(2,1)}, bf16[512,512]{1,0:T(8,128)(2,1)}, u32[]{:S(2)}, u32[]{:S(2)}) collective-permute-start(bf16[512,512]{1,0:T(8,128)(2,1)} %shard_map.63), channel_id=1, source_target_pairs={{0,1},{1,0},{2,3},{3,2},{4,5},{5,4},{6,7},{7,6},{8,9},{9,8},{10,11... | collective-permute-start | bytes 1572872 | tf_op jit(solution)/shard_map/ppermute | solution.py:223
  120.9 2.9 %collective-permute-start.23 = (bf16[512,512]{1,0:T(8,128)(2,1)}, bf16[512,512]{1,0:T(8,128)(2,1)}, u32[]{:S(2)}, u32[]{:S(2)}) collective-permute-start(bf16[512,512]{1,0:T(8,128)(2,1)} %shard_map.62), channel_id=1, source_target_pairs={{0,1},{1,0},{2,3},{3,2},{4,5},{5,4},{6,7},{7,6},{8,9},{9,8},{10,11... | collective-permute-start | bytes 1572872 | tf_op jit(solution)/shard_map/ppermute | solution.py:223
  120.9 2.8 %collective-permute-start.26 = (f32[4,8,256]{2,1,0:T(8,128)S(1)}, f32[4,8,256]{2,1,0:T(8,128)S(1)}, u32[]{:S(2)}, u32[]{:S(2)}) collective-permute-start(f32[4,8,256]{2,1,0:T(8,128)S(1)} %add.45.sum_ref), channel_id=1, source_target_pairs={{0,2},{1,3},{2,0},{3,1},{4,6},{5,7},{6,4},{7,5},{8,10},{9,11},{10,... | collective-permute-start | bytes 98312 | tf_op jit(solution)/shard_map/ppermute | solution.py:223

commit v3 on v2

v3 whole, which is shorter than its diff:
```python
import functools

import jax
import jax.numpy as jnp
from jax import lax
from jax.experimental import pallas as pl
from jax.experimental.pallas import tpu as pltpu
from jax.sharding import PartitionSpec as P

TILE = 128
F32, BF16 = jnp.float32, jnp.bfloat16
TURN = (1, -1, 1, -1)
ALONG_Y = {
    h: [(4 * y + r, 4 * ((y + h * TURN[r]) % 4) + r) for y in range(4) for r in range(4)] for h in (1, 2, 3)
}
ALONG_X = {s: [(4 * x + z, 4 * ((x + s) % 4) + z) for x in range(4) for z in range(4)] for s in (1, 3)}
ALONG_Z = {s: [(4 * x + z, 4 * x + (z + s) % 4) for x in range(4) for z in range(4)] for s in (1, 3)}
SWAP = {k: [(i, i ^ k) for i in range(4)] for k in (1, 2)}
COLS = {k: [(i, i ^ k) for i in range(16)] for k in (1, 2, 4, 8)}
VMEM = 14 << 20
WAIT = 160 << 20
PAUSE = 8 << 20
TINY = pl.CostEstimate(flops=1, bytes_accessed=1, transcendentals=0)


def prep_kernel(place_ref, flags_ref, b_ref, o_ref, sum_ref, *, first):
    ones = jnp.ones((8, 512), BF16)
    block = place_ref[3] ^ (first - pl.program_id(0))
    for j in range(4):
        z = (place_ref[2] - j) & 3
        rows = pl.ds(pl.multiple_of(z * TILE, TILE), TILE)
        tiles = []
        for p in range(4):
            on = flags_ref[z, block * 4 + p] != 0
            tiles.append(jnp.where(on, b_ref[rows, TILE * p:TILE * (p + 1)], jnp.zeros((TILE, TILE), BF16)))
        line = jnp.concatenate(tiles, 1)
        o_ref[TILE * j:TILE * (j + 1), :] = line
        sum_ref[0, z] = lax.dot_general(ones, line, (((1,), (1,)), ((), ())), preferred_element_type=F32)


def prep(place, flags, b, first):
    return pl.pallas_call(
        functools.partial(prep_kernel, first=first),
        grid_spec=pltpu.PrefetchScalarGridSpec(
            num_scalar_prefetch=2,
            grid=(2,),
            in_specs=[pl.BlockSpec((512, 512), lambda i, place, flags: (0, place[3] ^ (first - i)))],
            out_specs=[
                pl.BlockSpec((512, 512), lambda i, place, flags: (0, i)),
                pl.BlockSpec((1, 4, 8, TILE), lambda i, place, flags: (i, 0, 0, 0)),
            ],
        ),
        out_shape=[jax.ShapeDtypeStruct((512, 1024), BF16), jax.ShapeDtypeStruct((2, 4, 8, TILE), F32)],
        compiler_params=pltpu.CompilerParams(vmem_limit_bytes=VMEM),
        cost_estimate=TINY,
    )(place, flags, b)


def mask_kernel(flags_ref, a_ref, o_ref, sum_ref):
    ones = jnp.ones((8, TILE), BF16)
    for k in range(8):
        rows = slice(TILE * k, TILE * (k + 1))
        tile = jnp.where(flags_ref[k] != 0, a_ref[rows, :], jnp.zeros((TILE, TILE), BF16))
        o_ref[rows, :] = tile
        sum_ref[k] = lax.dot_general(ones, tile, (((1,), (1,)), ((), ())), preferred_element_type=F32)


def mask(flags, a):
    return pl.pallas_call(
        mask_kernel,
        grid_spec=pltpu.PrefetchScalarGridSpec(
            num_scalar_prefetch=1,
            grid=(1,),
            in_specs=[pl.BlockSpec((1024, TILE), lambda i, flags: (0, 0))],
            out_specs=[
                pl.BlockSpec((1024, TILE), lambda i, flags: (0, 0)),
                pl.BlockSpec((8, 8, TILE), lambda i, flags: (0, 0, 0)),
            ],
        ),
        out_shape=[jax.ShapeDtypeStruct((1024, TILE), BF16), jax.ShapeDtypeStruct((8, 8, TILE), F32)],
        compiler_params=pltpu.CompilerParams(vmem_limit_bytes=VMEM),
        cost_estimate=TINY,
    )(flags, a)


def gather_kernel(own_ref, r_ref, l_ref, r2_ref, l2_ref, o_ref):
    o_ref[:, :TILE] = own_ref[...]
    o_ref[:, TILE:2 * TILE] = r_ref[...]
    o_ref[:512, 2 * TILE:3 * TILE] = r2_ref[...]
    o_ref[512:, 2 * TILE:3 * TILE] = l2_ref[...]
    o_ref[:, 3 * TILE:] = l_ref[...]


def gather(own, r, l, r2, l2):
    return pl.pallas_call(
        gather_kernel,
        out_shape=jax.ShapeDtypeStruct((1024, 512), BF16),
        compiler_params=pltpu.CompilerParams(vmem_limit_bytes=VMEM),
        cost_estimate=pl.CostEstimate(flops=1, bytes_accessed=WAIT, transcendentals=0),
    )(own, r, l, r2, l2)


def slot(place_ref, s):
    return ((place_ref[1] - place_ref[0] + s) * (1 - 2 * (place_ref[3] & 1))) & 3


def scaled(place_ref, scale_ref, piece, s):
    z = place_ref[2]
    scale = [scale_ref[slot(place_ref, s), pl.ds((z - j) & 3, 1), :] for j in range(4)]
    return (piece.astype(F32) * jnp.concatenate(scale, 1)).astype(BF16)


def early_kernel(place_ref, scale_ref, own_ref, r_ref, l_ref, o_ref):
    for s, ref in ((0, own_ref), (1, r_ref), (3, l_ref)):
        o_ref[slot(place_ref, s)] = scaled(place_ref, scale_ref, ref[...], s)


SCALE = pl.BlockSpec((4, 4, TILE), lambda i, *_: (0, 0, 0))
ROWS = pl.BlockSpec((256, 512), lambda i, *_: (i, 0))
ALL = pl.BlockSpec((4, 256, 512), lambda i, *_: (0, i, 0))
UPPER = pl.BlockSpec((256, 512), lambda i, *_: (jnp.minimum(i, 1), 0))
LOWER = pl.BlockSpec((256, 512), lambda i, *_: (jnp.maximum(i - 2, 0), 0))


def early(place, scale, pieces):
    return pl.pallas_call(
        early_kernel,
        grid_spec=pltpu.PrefetchScalarGridSpec(
            num_scalar_prefetch=1,
            grid=(4,),
            in_specs=[SCALE, ROWS, ROWS, ROWS],
            out_specs=ALL,
        ),
        out_shape=jax.ShapeDtypeStruct((4, 1024, 512), BF16),
        compiler_params=pltpu.CompilerParams(vmem_limit_bytes=VMEM),
        cost_estimate=TINY,
    )(place, scale, *pieces)


def multiply(a_ref, hops):
    total = jnp.dot(a_ref[0], hops[0][...], preferred_element_type=F32)
    for h in range(1, 4):
        total += jnp.dot(a_ref[h], hops[h][...], preferred_element_type=F32)
    return total


def hop_specs(q):
    return [pl.BlockSpec((512, 512), lambda i, *_: (0, q))] * 4


def opening_kernel(place_ref, scale_ref, full_ref, piece_ref, *refs):
    hops, (last_ref, o_ref) = refs[:4], refs[4:]
    last = scaled(place_ref, scale_ref, piece_ref[...], 2)
    last_ref[0] = last
    missing = slot(place_ref, 2)
    lefts = [jnp.where(missing == h, last, full_ref[h]) for h in range(4)]
    o_ref[...] = multiply(lefts, hops).astype(BF16)


def opening(place, scale, full, piece, hops, half):
    return pl.pallas_call(
        opening_kernel,
        grid_spec=pltpu.PrefetchScalarGridSpec(
            num_scalar_prefetch=1,
            grid=(2,),
            in_specs=[SCALE, pl.BlockSpec((4, 256, 512), lambda i, *_: (0, 2 * half + i, 0)), ROWS] + hop_specs(0),
            out_specs=[
                pl.BlockSpec((1, 256, 512), lambda i, place: (slot(place, 2), 2 * half + i, 0)),
                ROWS,
            ],
        ),
        out_shape=[
            jax.ShapeDtypeStruct((4, 1024, 512), BF16),
            jax.ShapeDtypeStruct((512, 512), BF16),
        ],
        input_output_aliases={2: 0},
        compiler_params=pltpu.CompilerParams(vmem_limit_bytes=VMEM),
        cost_estimate=TINY,
    )(place, scale, full, piece, *hops)


def middle_kernel(full_ref, core_ref, *refs):
    refs[4][...] = (multiply(full_ref, refs[:4]) + core_ref[...].astype(F32)).astype(BF16)


def middle(full, core, hops, half):
    return pl.pallas_call(
        middle_kernel,
        grid=(2,),
        in_specs=[pl.BlockSpec((4, 256, 512), lambda i: (0, 2 * half + i, 0)), ROWS] + hop_specs(1),
        out_specs=ROWS,
        out_shape=jax.ShapeDtypeStruct((512, 512), BF16),
        compiler_params=pltpu.CompilerParams(vmem_limit_bytes=VMEM),
        cost_estimate=TINY,
    )(full, core, *hops)


def multiply_split(full_ref, hops):
    total = jnp.dot(full_ref[0], hops[0][...], preferred_element_type=F32)
    for h in range(1, 3):
        total += jnp.dot(full_ref[h], hops[h][...], preferred_element_type=F32)
    total += jnp.dot(full_ref[3, :, :256], hops[3][...], preferred_element_type=F32)
    return total + jnp.dot(full_ref[3, :, 256:], hops[4][...], preferred_element_type=F32)


def split_specs(q):
    return [pl.BlockSpec((512, 512), lambda i, *_: (0, q))] * 3 + [pl.BlockSpec((256, 512), lambda i, *_: (0, q))] * 2


def pieces_kernel(full_ref, *refs):
    total = multiply_split(full_ref, refs[:5]).astype(BF16)
    for k in range(2):

        @pl.when((pl.program_id(0) >> 1) == k)
        def _():
            refs[5 + k][...] = total


def pieces(full, hops):
    return pl.pallas_call(
        pieces_kernel,
        grid=(4,),
        in_specs=[ALL] + split_specs(0),
        out_specs=[UPPER, LOWER],
        out_shape=[jax.ShapeDtypeStruct((512, 512), BF16)] * 2,
        compiler_params=pltpu.CompilerParams(vmem_limit_bytes=VMEM),
        cost_estimate=TINY,
    )(full, *hops)


def product_kernel(full_ref, *refs):
    refs[5][...] = multiply_split(full_ref, refs[:5])


def product(full, hops):
    return pl.pallas_call(
        product_kernel,
        grid=(4,),
        in_specs=[ALL] + split_specs(1),
        out_specs=ROWS,
        out_shape=jax.ShapeDtypeStruct((1024, 512), F32),
        compiler_params=pltpu.CompilerParams(vmem_limit_bytes=VMEM),
        cost_estimate=TINY,
    )(full, *hops)


def closing_kernel(flags_ref, part_ref, core0_ref, core1_ref, chip0_ref, chip1_ref, sum_ref, more_ref, o_ref):
    step = pl.program_id(0)
    core = jnp.where(step == 0, core0_ref[...], core1_ref[...])
    chip = jnp.where(step == 0, chip0_ref[...], chip1_ref[...])
    for block in range(4):
        rows = slice(TILE * block, TILE * (block + 1))
        total = part_ref[rows, :] + core[rows, :].astype(F32)
        total += chip[rows, :].astype(F32)
        line = pl.ds(4 * step + block, 1)
        scale = jnp.float32(TILE * 256) / (1.0 + sum_ref[line, :] + more_ref[line, :])
        total *= jnp.transpose(jnp.broadcast_to(scale, (8, TILE)))[:, 0:1]
        for p in range(4):
            lanes = slice(TILE * p, TILE * (p + 1))
            on = flags_ref[4 * step + block, p] != 0
            o_ref[rows, lanes] = jnp.where(on, total[:, lanes], 0.0).astype(BF16)


def closing(flags, part, core, chip, sums, more):
    rows = pl.BlockSpec((512, 512), lambda i, f: (i, 0))
    side = pl.BlockSpec((8, TILE), lambda i, f: (0, 0))
    whole = pl.BlockSpec((512, 512), lambda i, f: (0, 0))
    return pl.pallas_call(
        closing_kernel,
        grid_spec=pltpu.PrefetchScalarGridSpec(
            num_scalar_prefetch=1,
            grid=(2,),
            in_specs=[rows, whole, whole, whole, whole, side, side],
            out_specs=rows,
        ),
        out_shape=jax.ShapeDtypeStruct((1024, 512), BF16),
        compiler_params=pltpu.CompilerParams(vmem_limit_bytes=VMEM),
        cost_estimate=TINY,
    )(flags, part, *core, *chip, sums, more)


class Order:
    def __init__(self):
        self.seen = []

    def send(self, value, axes, pairs):
        others = [v for v in self.seen[-5:] if v is not value]
        if others:
            value = lax.optimization_barrier((value, *others))[0]
        return lax.ppermute(value, axes, pairs)

    def wait(self, *values):
        self.seen.extend(values)


def shards(a_weights, a_flags, b_weights, b_flags, out_flags):
    rep = lax.axis_index("rep").astype(jnp.int32)
    row = lax.axis_index("row").astype(jnp.int32)
    col = lax.axis_index("col").astype(jnp.int32)
    place = jnp.stack([col >> 2, row, col & 3, rep])
    b, bf = b_weights[0], b_flags[0]
    order = Order()

    def both(v, axis, tables):
        return order.send(v, axis, tables[1]), order.send(v, axis, tables[3])

    def onward(r, l, axis, tables):
        n = r.shape[0] // 2
        return order.send(r[:n], axis, tables[1]), order.send(l[n:], axis, tables[3])

    def send_y(v, h=1):
        return order.send(v, ("row", "rep"), ALONG_Y[h])

    a, a_sum = mask(a_flags[0, :, 0], a_weights[0])
    zr, zl = both(a, "col", ALONG_Z)
    b, a = lax.optimization_barrier((b, a))
    b32, sum32 = prep(place, bf, b, 3)
    h32 = [b32, send_y(b32)]
    b10, sum10 = prep(place, bf, lax.optimization_barrier((b, sum32))[0], 1)
    h10 = [b10, send_y(b10)]
    b_sum = sum32[0] + sum32[1] + sum10[0] + sum10[1]
    total = jnp.concatenate([a_sum[:, 0, :], b_sum[:, 0, :]], 0)
    other = order.send(total, "col", COLS[4])
    order.wait(other)
    total = total + other
    other = order.send(total, "col", COLS[8])
    order.wait(other, zr, zl)
    total = total + other
    zr2, zl2 = onward(zr, zl, "col", ALONG_Z)
    order.wait(h32[1])
    h32.append(send_y(h32[1]))
    other = order.send(total, "col", COLS[1])
    wide = gather(a, zr, zl, zr2, zl2)
    order.wait(zr2, zl2, other)
    xr, xl = both(wide, "col", ALONG_X)
    total = total + other
    other = order.send(total, "col", COLS[2])
    h10.append(send_y(h10[1]))
    order.wait(h32[2], other)
    total = total + other
    walk_b = 1.0 / (1.0 + total[8:])
    others = [send_y(walk_b, h) for h in (1, 2, 3)]
    order.wait(h10[2], *others)
    scale = jnp.stack([walk_b] + others, 0)
    h32.append(send_y(h32[2]))

    order.wait(xr, xl)
    xr2, xl2 = onward(xr, xl, "col", ALONG_X)
    upper = send_y(h10[2][:256])
    sums = total[:8]
    more = order.send(sums, "rep", SWAP[1])
    most = early(place, scale, (wide, xr, xl))
    sums = sums + more
    more = order.send(sums, "rep", SWAP[2])
    xr2 = lax.optimization_barrier((xr2, more))[0]
    full, top3 = opening(place, scale, most, xr2, h32, 0)
    order.wait(top3)
    top_core = order.send(top3, "rep", SWAP[1])
    full, low3 = opening(place, scale, full, xl2, h32, 1)
    order.wait(low3)
    low_core = order.send(low3, "rep", SWAP[1])
    top2 = middle(full, top_core, h32, 0)
    order.wait(top2)
    top_chip = order.send(top2, "rep", SWAP[2])
    low2 = middle(full, low_core, [lax.optimization_barrier((h32[0], top2, upper))[0]] + h32[1:], 1)
    order.wait(low2)
    low_chip = order.send(low2, "rep", SWAP[2])
    lower = send_y(h10[2][256:])
    hops = h10 + [upper, lax.optimization_barrier((lower, low2))[0]]
    part1 = pieces(full, hops)
    part0 = product(full, hops)
    order.wait(part0)
    core = [order.send(v, "rep", SWAP[1]) for v in part1]
    return closing(out_flags, part0, core, (top_chip, low_chip), sums, more)


def solution(mesh):
    return jax.shard_map(
        shards,
        mesh=mesh,
        in_specs=(
            P("rep", "row", "col"),
            P("rep", "row", "col"),
            P("rep", "row", "col"),
            P("rep", "row", "col"),
            P("row", ("col", "rep")),
        ),
        out_specs=P("row", ("col", "rep")),
        check_vma=False,
    )
```

time: 129 us -> 121 us (0.938)
  waiting for transfers between devices: 59.1 us -> 42.2 us
  starting transfers between devices: 37.2 us -> 49.6 us
  other arithmetic: 1.62 us -> 0.13 us
    ppermute x27 -> x30, waiting for transfers between devices: 59.1 us -> 42.2 us  [send(): return lax.ppermute(value, axes, pairs)]
    ppermute x27 -> x30, starting transfers between devices: 37.2 us -> 49.6 us  [send(): return lax.ppermute(value, axes, pairs)]
    convert_element_type x1 -> x0, other arithmetic: 1.39 us -> none  [shards(): pair = (part2 + core3.astype(F32)).astype(BF16)]
    pallas_call x4 -> x5, Pallas kernels: 11.5 us -> 12.1 us  [the longest x1 4.37 us: pieces(): pl.pallas_call(pieces_kernel, grid=(4,), in_specs=[ALL] + split_specs(0),...]
    pallas_call x1 -> x2, Pallas kernels: 4.28 us -> 4.65 us  [opening(): pl.pallas_call(opening_kernel, grid_spec=pltpu.PrefetchScalarGridSpec(num...]
  transfers between devices with their start and end apart: 27 -> 30, of which waited for: 15 -> 13; matrix products, arithmetic and copies ran while one was open for 1% -> 0% of each run, Pallas kernels for 15% -> 15%
where the time goes in v3:
time: 121 us
  starting transfers between devices  49.6 us (41%)
  waiting for transfers between devices  42.2 us (35%)
  Pallas kernels  25 us (21%)
  local copies, waits for them, and re-layouts  4.16 us (3%)
    ppermute x30, starting transfers between devices, send(): return lax.ppermute(value, axes, pairs)  49.6 us
    ppermute x30, waiting for transfers between devices, send(): return lax.ppermute(value, axes, pairs)  42.2 us
    pallas_call x2, Pallas kernels, opening(): pl.pallas_call(opening_kernel, grid_spec=pltpu.PrefetchScalarGridSpec(num...  4.65 us
    pallas_call x1, Pallas kernels, pieces(): pl.pallas_call(pieces_kernel, grid=(4,), in_specs=[ALL] + split_specs(0),...  4.37 us
    pallas_call x2, Pallas kernels, middle(): pl.pallas_call(middle_kernel, grid=(2,), in_specs=[pl.BlockSpec((4, 256,...  4.2 us
    unnamed x11, local copies, waits for them, and re-layouts  3.96 us
    pallas_call x1, Pallas kernels, closing(): pl.pallas_call(closing_kernel, grid_spec=pltpu.PrefetchScalarGridSpec(num...  3.58 us
    pallas_call x1, Pallas kernels, product(): pl.pallas_call(product_kernel, grid=(4,), in_specs=[ALL] + split_specs(1)...  3.33 us
  transfers between devices with their start and end apart: 30, of which 13 were waited for; matrix products, arithmetic and copies ran while one was open for 0% of the time, Pallas kernels for 15%

profile of v3, /device:TPU:1, one launch (start us, length us, event | category | flops | bytes accessed | tf_op | source)
XLA Modules:
  0.0 121.2 jit_solution(5217315708216601261)
XLA Ops:
  0.0 0.9 copy-done.1
  1.6 0.8 shard_map.55
  2.4 3.9 %collective-permute-start.2 = (bf16[1024,128]{1,0:T(8,128)(2,1)S(1)}, bf16[1024,128]{1,0:T(8,128)(2,1)S(1)}, u32[]{:S(2)}, u32[]{:S(2)}) collective-permute-start(bf16[1024,128]{1,0:T(8,128)(2,1)S(1)} %get-tuple-element.59.own_ref), channel_id=1, source_target_pairs={{0,4},{4,8},{8,12},{12,0},{16,20},{20,24},{24,28},{28,16},{32,36},... | collective-permute-start | bytes 786440 | tf_op jit(solution)/shard_map/ppermute | solution.py:290
  6.3 3.1 %collective-permute-start.3 = (bf16[1024,128]{1,0:T(8,128)(2,1)S(1)}, bf16[1024,128]{1,0:T(8,128)(2,1)S(1)}, u32[]{:S(2)}, u32[]{:S(2)}) collective-permute-start(bf16[1024,128]{1,0:T(8,128)(2,1)S(1)} %get-tuple-element.59.own_ref), channel_id=1, source_target_pairs={{0,12},{4,0},{8,4},{12,8},{16,28},{20,16},{24,20},{28,24},{32,44},... | collective-permute-start | bytes 786440 | tf_op jit(solution)/shard_map/ppermute | solution.py:290
  9.5 1.6 %copy-done = bf16[1,512,2048]{2,1,0:T(8,128)(2,1)S(1)} copy-done((bf16[1,512,2048]{2,1,0:T(8,128)(2,1)S(1)}, bf16[1,512,2048]{2,1,0:T(8,128)(2,1)}, u32[]{:S(2)}) %copy-start) | copy-done | bytes 2097176
  11.7 1.2 %shard_map.56 = (bf16[512,1024]{1,0:T(8,128)(2,1)S(1)}, f32[2,4,8,128]{3,2,1,0:T(8,128)S(1)}) custom-call(s32[4]{0:T(128)S(1)} %pad_add_fusion.place_ref, s32[4,16]{1,0:T(4,128)S(1)} %bitcast.22, bf16[512,2048]{1,0:T(8,128)(2,1)S(1)} %bitcast.19), custom_call_target="tpu_custom_call" | custom-call | flops 1 | bytes 1 | tf_op jit(solution)/shard_map/pallas_call | solution.py:42
  13.0 2.8 %collective-permute-start.4 = (bf16[512,1024]{1,0:T(8,128)(2,1)S(1)}, bf16[512,1024]{1,0:T(8,128)(2,1)S(1)}, u32[]{:S(2)}, u32[]{:S(2)}) collective-permute-start(bf16[512,1024]{1,0:T(8,128)(2,1)S(1)} %get-tuple-element.76.refs_0_), channel_id=1, source_target_pairs={{0,64},{1,193},{2,66},{3,195},{64,128},{65,1},{66,130},{67,3},{128... | collective-permute-start | bytes 3145736 | tf_op jit(solution)/shard_map/ppermute | solution.py:290
  15.8 1.2 %shard_map.57 = (bf16[512,1024]{1,0:T(8,128)(2,1)S(1)}, f32[2,4,8,128]{3,2,1,0:T(8,128)S(1)}) custom-call(s32[4]{0:T(128)S(1)} %pad_add_fusion.place_ref, s32[4,16]{1,0:T(4,128)S(1)} %bitcast.23, bf16[512,2048]{1,0:T(8,128)(2,1)S(1)} %bitcast.20), custom_call_target="tpu_custom_call" | custom-call | flops 1 | bytes 1 | tf_op jit(solution)/shard_map/pallas_call | solution.py:42
  17.6 1.3 %collective-permute-start = (f32[12,128]{1,0:T(8,128)S(1)}, f32[12,128]{1,0:T(8,128)S(1)}, u32[]{:S(2)}, u32[]{:S(2)}) collective-permute-start(f32[12,128]{1,0:T(8,128)S(1)} %pad_maximum_fusion), channel_id=1, source_target_pairs={{0,16},{4,20},{8,24},{12,28},{16,0},{20,4},{24,8},{28,12},{32,48},... | collective-permute-start | bytes 18440 | tf_op jit(solution)/shard_map/ppermute | solution.py:290
  18.9 1.6 %collective-permute-done = f32[12,128]{1,0:T(8,128)S(1)} collective-permute-done((f32[12,128]{1,0:T(8,128)S(1)}, f32[12,128]{1,0:T(8,128)S(1)}, u32[]{:S(2)}, u32[]{:S(2)}) %collective-permute-start) | collective-permute-done | bytes 6176 | tf_op jit(solution)/shard_map/ppermute | solution.py:290
  20.5 2.7 %collective-permute-start.1 = (f32[12,128]{1,0:T(8,128)S(1)}, f32[12,128]{1,0:T(8,128)S(1)}, u32[]{:S(2)}, u32[]{:S(2)}) collective-permute-start(f32[12,128]{1,0:T(8,128)S(1)} %fusion.2), channel_id=1, source_target_pairs={{0,32},{4,36},{8,40},{12,44},{16,48},{20,52},{24,56},{28,60},{32,0... | collective-permute-start | bytes 18440 | tf_op jit(solution)/shard_map/ppermute | solution.py:290
  23.3 1.2 %collective-permute-done.1 = f32[12,128]{1,0:T(8,128)S(1)} collective-permute-done((f32[12,128]{1,0:T(8,128)S(1)}, f32[12,128]{1,0:T(8,128)S(1)}, u32[]{:S(2)}, u32[]{:S(2)}) %collective-permute-start.1) | collective-permute-done | bytes 6176 | tf_op jit(solution)/shard_map/ppermute | solution.py:290
  24.5 1.4 %collective-permute-start.6 = (bf16[512,128]{1,0:T(8,128)(2,1)S(1)}, bf16[512,128]{1,0:T(8,128)(2,1)S(1)}, u32[]{:S(2)}, u32[]{:S(2)}) collective-permute-start(bf16[512,128]{1,0:T(8,128)(2,1)S(1)} %slice.62), channel_id=1, source_target_pairs={{0,4},{4,8},{8,12},{12,0},{16,20},{20,24},{24,28},{28,16},{32,36},... | collective-permute-start | bytes 393224 | tf_op jit(solution)/shard_map/ppermute | solution.py:290
  25.9 2.3 %collective-permute-start.7 = (bf16[512,128]{1,0:T(8,128)(2,1)S(1)}, bf16[512,128]{1,0:T(8,128)(2,1)S(1)}, u32[]{:S(2)}, u32[]{:S(2)}) collective-permute-start(bf16[512,128]{1,0:T(8,128)(2,1)S(1)} %slice.63), channel_id=1, source_target_pairs={{0,12},{4,0},{8,4},{12,8},{16,28},{20,16},{24,20},{28,24},{32,44},... | collective-permute-start | bytes 393224 | tf_op jit(solution)/shard_map/ppermute | solution.py:290
  28.2 1.2 collective-permute-start.5
  29.4 2.3 %collective-permute-start.9 = (bf16[512,1024]{1,0:T(8,128)(2,1)S(1)}, bf16[512,1024]{1,0:T(8,128)(2,1)S(1)}, u32[]{:S(2)}, u32[]{:S(2)}) collective-permute-start(bf16[512,1024]{1,0:T(8,128)(2,1)S(1)} %collective-permute-done.4.refs_1_), channel_id=1, source_target_pairs={{0,64},{1,193},{2,66},{3,195},{64,128},{65,1},{66,130},{67,3},{128... | collective-permute-start | bytes 3145736 | tf_op jit(solution)/shard_map/ppermute | solution.py:290
  31.7 1.7 %collective-permute-done.7.l2_ref = bf16[512,128]{1,0:T(8,128)(2,1)S(1)} collective-permute-done((bf16[512,128]{1,0:T(8,128)(2,1)S(1)}, bf16[512,128]{1,0:T(8,128)(2,1)S(1)}, u32[]{:S(2)}, u32[]{:S(2)}) %collective-permute-start.7) | collective-permute-done | bytes 131104 | tf_op jit(solution)/shard_map/ppermute | solution.py:290
  33.4 5.3 %collective-permute-done.18.refs_1_ = bf16[512,1024]{1,0:T(8,128)(2,1)S(1)} collective-permute-done((bf16[512,1024]{1,0:T(8,128)(2,1)S(1)}, bf16[512,1024]{1,0:T(8,128)(2,1)S(1)}, u32[]{:S(2)}, u32[]{:S(2)}) %collective-permute-start.18) | collective-permute-done | bytes 1048608 | tf_op jit(solution)/shard_map/ppermute | solution.py:290
  38.8 3.1 %collective-permute-start.19 = (bf16[512,1024]{1,0:T(8,128)(2,1)S(1)}, bf16[512,1024]{1,0:T(8,128)(2,1)S(1)}, u32[]{:S(2)}, u32[]{:S(2)}) collective-permute-start(bf16[512,1024]{1,0:T(8,128)(2,1)S(1)} %collective-permute-done.18.refs_1_), channel_id=1, source_target_pairs={{0,64},{1,193},{2,66},{3,195},{64,128},{65,1},{66,130},{67,3},{128... | collective-permute-start | bytes 3145736 | tf_op jit(solution)/shard_map/ppermute | solution.py:290
  42.1 1.3 %collective-permute-start.13 = (bf16[1024,512]{1,0:T(8,128)(2,1)S(1)}, bf16[1024,512]{1,0:T(8,128)(2,1)S(1)}, u32[]{:S(2)}, u32[]{:S(2)}) collective-permute-start(bf16[1024,512]{1,0:T(8,128)(2,1)S(1)} %shard_map.58.own_ref), channel_id=1, source_target_pairs={{0,16},{4,20},{8,24},{12,28},{16,32},{20,36},{24,40},{28,44},{32,4... | collective-permute-start | bytes 3145736 | tf_op jit(solution)/shard_map/ppermute | solution.py:290
  43.3 1.5 %collective-permute-start.14 = (bf16[1024,512]{1,0:T(8,128)(2,1)S(1)}, bf16[1024,512]{1,0:T(8,128)(2,1)S(1)}, u32[]{:S(2)}, u32[]{:S(2)}) collective-permute-start(bf16[1024,512]{1,0:T(8,128)(2,1)S(1)} %shard_map.58.own_ref), channel_id=1, source_target_pairs={{0,48},{4,52},{8,56},{12,60},{16,0},{20,4},{24,8},{28,12},{32,16},... | collective-permute-start | bytes 3145736 | tf_op jit(solution)/shard_map/ppermute | solution.py:290
  44.8 4.4 %collective-permute-start.8 = (f32[12,128]{1,0:T(8,128)S(1)}, f32[12,128]{1,0:T(8,128)S(1)}, u32[]{:S(2)}, u32[]{:S(2)}) collective-permute-start(f32[12,128]{1,0:T(8,128)S(1)} %add.38), channel_id=1, source_target_pairs={{0,8},{4,12},{8,0},{12,4},{16,24},{20,28},{24,16},{28,20},{32,40},... | collective-permute-start | bytes 18440 | tf_op jit(solution)/shard_map/ppermute | solution.py:290
  49.2 2.0 %collective-permute-done.8 = f32[12,128]{1,0:T(8,128)S(1)} collective-permute-done((f32[12,128]{1,0:T(8,128)S(1)}, f32[12,128]{1,0:T(8,128)S(1)}, u32[]{:S(2)}, u32[]{:S(2)}) %collective-permute-start.8) | collective-permute-done | bytes 6176 | tf_op jit(solution)/shard_map/ppermute | solution.py:290
  51.3 3.3 %collective-permute-start.11 = (f32[4,128]{1,0:T(4,128)S(1)}, f32[4,128]{1,0:T(4,128)S(1)}, u32[]{:S(2)}, u32[]{:S(2)}) collective-permute-start(f32[4,128]{1,0:T(4,128)S(1)} %fusion.1), channel_id=1, source_target_pairs={{0,128},{1,129},{2,130},{3,131},{64,192},{65,193},{66,194},{67,195... | collective-permute-start | bytes 6152 | tf_op jit(solution)/shard_map/ppermute | solution.py:290
  54.6 0.8 collective-permute-done.12
  55.3 0.9 collective-permute-start.10
  56.2 5.1 %collective-permute-done.10 = f32[4,128]{1,0:T(4,128)S(1)} collective-permute-done((f32[4,128]{1,0:T(4,128)S(1)}, f32[4,128]{1,0:T(4,128)S(1)}, u32[]{:S(2)}, u32[]{:S(2)}) %collective-permute-start.10) | collective-permute-done | bytes 2080 | tf_op jit(solution)/shard_map/ppermute | solution.py:290
  61.3 3.4 %collective-permute-start.20 = (bf16[512,1024]{1,0:T(8,128)(2,1)S(1)}, bf16[512,1024]{1,0:T(8,128)(2,1)S(1)}, u32[]{:S(2)}, u32[]{:S(2)}) collective-permute-start(bf16[512,1024]{1,0:T(8,128)(2,1)S(1)} %collective-permute-done.9.refs_2_), channel_id=1, source_target_pairs={{0,64},{1,193},{2,66},{3,195},{64,128},{65,1},{66,130},{67,3},{128... | collective-permute-start | bytes 3145736 | tf_op jit(solution)/shard_map/ppermute | solution.py:290
  64.7 3.6 %collective-permute-done.13.r_ref = bf16[1024,512]{1,0:T(8,128)(2,1)S(1)} collective-permute-done((bf16[1024,512]{1,0:T(8,128)(2,1)S(1)}, bf16[1024,512]{1,0:T(8,128)(2,1)S(1)}, u32[]{:S(2)}, u32[]{:S(2)}) %collective-permute-start.13) | collective-permute-done | bytes 1048608 | tf_op jit(solution)/shard_map/ppermute | solution.py:290
  68.4 1.0 collective-permute-start.15
  69.3 1.1 collective-permute-start.16
  70.4 1.7 %collective-permute-start.21 = (bf16[512,512]{1,0:T(8,128)(2,1)S(1)}, bf16[512,512]{1,0:T(8,128)(2,1)S(1)}, u32[]{:S(2)}, u32[]{:S(2)}) collective-permute-start(bf16[512,512]{1,0:T(8,128)(2,1)S(1)} %slice.67), channel_id=1, source_target_pairs={{0,48},{4,52},{8,56},{12,60},{16,0},{20,4},{24,8},{28,12},{32,16},... | collective-permute-start | bytes 1572872 | tf_op jit(solution)/shard_map/ppermute | solution.py:290
  72.1 0.8 collective-permute-start.17
  73.1 1.4 %shard_map.59.full_ref = bf16[4,1024,512]{2,1,0:T(8,128)(2,1)S(1)} custom-call(s32[4]{0:T(128)S(1)} %pad_add_fusion.place_ref, f32[4,4,128]{2,1,0:T(4,128)S(1)} %pad_maximum_fusion.1.scale_ref, bf16[1024,512]{1,0:T(8,128)(2,1)S(1)} %shard_map.58.own_ref, bf16[1024,512]{1,0:T(8,128)(2,1)S(1)} %collective-permute-done.13.r_ref, ...), custom_call_target="tpu_custom_call" | custom-call | flops 1 | bytes 1 | tf_op jit(solution)/shard_map/pallas_call | solution.py:126
  75.0 7.6 %collective-permute-done.15.piece_ref = bf16[512,512]{1,0:T(8,128)(2,1)S(1)} collective-permute-done((bf16[512,512]{1,0:T(8,128)(2,1)S(1)}, bf16[512,512]{1,0:T(8,128)(2,1)S(1)}, u32[]{:S(2)}, u32[]{:S(2)}) %collective-permute-start.15) | collective-permute-done | bytes 524320 | tf_op jit(solution)/shard_map/ppermute | solution.py:290
  82.5 2.3 %shard_map.60 = (bf16[4,1024,512]{2,1,0:T(8,128)(2,1)S(1)}, bf16[512,512]{1,0:T(8,128)(2,1)S(1)}) custom-call(s32[4]{0:T(128)S(1)} %pad_add_fusion.place_ref, f32[4,4,128]{2,1,0:T(4,128)S(1)} %pad_maximum_fusion.1.scale_ref, bf16[4,1024,512]{2,1,0:T(8,128)(2,1)S(1)} %shard_map.59.full_ref, ...), custom_call_target="tpu_custom_call", output_to_operand_aliasing={{0}: (2, {})} | custom-call | flops 1 | bytes 1 | tf_op jit(solution)/shard_map/pallas_call | solution.py:161
  84.9 1.5 %collective-permute-start.23 = (bf16[512,512]{1,0:T(8,128)(2,1)S(1)}, bf16[512,512]{1,0:T(8,128)(2,1)S(1)}, u32[]{:S(2)}, u32[]{:S(2)}) collective-permute-start(bf16[512,512]{1,0:T(8,128)(2,1)S(1)} %get-tuple-element.74), channel_id=1, source_target_pairs={{0,1},{1,0},{2,3},{3,2},{4,5},{5,4},{6,7},{7,6},{8,9},{9,8},{10,11... | collective-permute-start | bytes 1572872 | tf_op jit(solution)/shard_map/ppermute | solution.py:290
  86.4 2.3 %shard_map.61 = (bf16[4,1024,512]{2,1,0:T(8,128)(2,1)S(1)}, bf16[512,512]{1,0:T(8,128)(2,1)S(1)}) custom-call(s32[4]{0:T(128)S(1)} %pad_add_fusion.place_ref, f32[4,4,128]{2,1,0:T(4,128)S(1)} %pad_maximum_fusion.1.scale_ref, bf16[4,1024,512]{2,1,0:T(8,128)(2,1)S(1)} %get-tuple-element.68.full_ref, ...), custom_call_target="tpu_custom_call", output_to_operand_aliasing={{0}: (2, {})} | custom-call | flops 1 | bytes 1 | tf_op jit(solution)/shard_map/pallas_call | solution.py:161
  88.9 1.8 %shard_map.62 = bf16[512,512]{1,0:T(8,128)(2,1)S(1)} custom-call(bf16[4,1024,512]{2,1,0:T(8,128)(2,1)S(1)} %get-tuple-element.70.full_ref, bf16[512,512]{1,0:T(8,128)(2,1)S(1)} %collective-permute-done.23.core_ref, bf16[512,1024]{1,0:T(8,128)(2,1)S(1)} %get-tuple-element.76.refs_0_, bf16[512,1024]{1,0:T(8,128)(2,1)S(1)} %collective-permute-done.4.refs_1_, ...), custom_call_target="tpu_custom_call" | custom-call | flops 1 | bytes 1 | tf_op jit(solution)/shard_map/pallas_call | solution.py:187
  90.8 2.4 %shard_map.63 = bf16[512,512]{1,0:T(8,128)(2,1)} custom-call(bf16[4,1024,512]{2,1,0:T(8,128)(2,1)S(1)} %get-tuple-element.70.full_ref, bf16[512,512]{1,0:T(8,128)(2,1)S(1)} %collective-permute-done.24.core_ref, bf16[512,1024]{1,0:T(8,128)(2,1)S(1)} %get-tuple-element.76.refs_0_, bf16[512,1024]{1,0:T(8,128)(2,1)S(1)} %collective-permute-done.4.refs_1_, ...), custom_call_target="tpu_custom_call" | custom-call | flops 1 | bytes 1 | tf_op jit(solution)/shard_map/pallas_call | solution.py:187
  93.2 0.7 collective-permute-start.28
  93.9 0.7 collective-permute-start.29
  94.7 6.9 %collective-permute-done.25.refs_4_ = bf16[256,1024]{1,0:T(8,128)(2,1)S(1)} collective-permute-done((bf16[256,1024]{1,0:T(8,128)(2,1)S(1)}, bf16[256,1024]{1,0:T(8,128)(2,1)S(1)}, u32[]{:S(2)}, u32[]{:S(2)}) %collective-permute-start.25) | collective-permute-done | bytes 524320 | tf_op jit(solution)/shard_map/ppermute | solution.py:290
  101.5 3.3 %shard_map.64.part_ref = f32[1024,512]{1,0:T(8,128)S(1)} custom-call(bf16[4,1024,512]{2,1,0:T(8,128)(2,1)S(1)} %get-tuple-element.70.full_ref, bf16[512,1024]{1,0:T(8,128)(2,1)S(1)} %get-tuple-element.65.refs_0_, bf16[512,1024]{1,0:T(8,128)(2,1)S(1)} %collective-permute-done.18.refs_1_, bf16[512,1024]{1,0:T(8,128)(2,1)S(1)} %collective-permute-done.19.refs_2_, ...), custom_call_target="tpu_custom_call" | custom-call | flops 1 | bytes 1 | tf_op jit(solution)/shard_map/pallas_call | solution.py:236
  104.9 4.4 %shard_map.65 = (bf16[512,512]{1,0:T(8,128)(2,1)}, bf16[512,512]{1,0:T(8,128)(2,1)}) custom-call(bf16[4,1024,512]{2,1,0:T(8,128)(2,1)S(1)} %get-tuple-element.70.full_ref, bf16[512,1024]{1,0:T(8,128)(2,1)S(1)} %get-tuple-element.65.refs_0_, bf16[512,1024]{1,0:T(8,128)(2,1)S(1)} %collective-permute-done.18.refs_1_, ...), custom_call_target="tpu_custom_call" | custom-call | flops 1 | bytes 1 | tf_op jit(solution)/shard_map/pallas_call | solution.py:220
  109.2 2.5 %collective-permute-start.26 = (bf16[512,512]{1,0:T(8,128)(2,1)}, bf16[512,512]{1,0:T(8,128)(2,1)}, u32[]{:S(2)}, u32[]{:S(2)}) collective-permute-start(bf16[512,512]{1,0:T(8,128)(2,1)} %get-tuple-element.80), channel_id=1, source_target_pairs={{0,1},{1,0},{2,3},{3,2},{4,5},{5,4},{6,7},{7,6},{8,9},{9,8},{10,11... | collective-permute-start | bytes 1572872 | tf_op jit(solution)/shard_map/ppermute | solution.py:290
  111.8 5.8 %collective-permute-done.29.chip1_ref = bf16[512,512]{1,0:T(8,128)(2,1)} collective-permute-done((bf16[512,512]{1,0:T(8,128)(2,1)}, bf16[512,512]{1,0:T(8,128)(2,1)}, u32[]{:S(2)}, u32[]{:S(2)}) %collective-permute-start.29) | collective-permute-done | bytes 524320 | tf_op jit(solution)/shard_map/ppermute | solution.py:290
  117.6 3.6 %shard_map.66 = bf16[1024,512]{1,0:T(8,128)(2,1)} custom-call(s32[8,4]{1,0:T(8,128)S(1)} %copy.13.flags_ref, f32[1024,512]{1,0:T(8,128)S(1)} %shard_map.64.part_ref, bf16[512,512]{1,0:T(8,128)(2,1)} %collective-permute-done.26.core0_ref, bf16[512,512]{1,0:T(8,128)(2,1)} %collective-permute-done.27.core1_ref, ...), custom_call_target="tpu_custom_call" | custom-call | flops 1 | bytes 1 | tf_op jit(solution)/shard_map/pallas_call | solution.py:268
  (57 shorter events, 3.3 us)
Async XLA Ops:
  0.0 0.9 copy-start.1
  1.0 0.7 copy-start.3
  2.4 20.9 %collective-permute-start.2 = (bf16[1024,128]{1,0:T(8,128)(2,1)S(1)}, bf16[1024,128]{1,0:T(8,128)(2,1)S(1)}, u32[]{:S(2)}, u32[]{:S(2)}) collective-permute-start(bf16[1024,128]{1,0:T(8,128)(2,1)S(1)} %get-tuple-element.59.own_ref), channel_id=1, source_target_pairs={{0,4},{4,8},{8,12},{12,0},{16,20},{20,24},{24,28},{28,16},{32,36},... | collective-permute-start | bytes 786440 | tf_op jit(solution)/shard_map/ppermute | solution.py:290
  6.3 18.3 %collective-permute-start.3 = (bf16[1024,128]{1,0:T(8,128)(2,1)S(1)}, bf16[1024,128]{1,0:T(8,128)(2,1)S(1)}, u32[]{:S(2)}, u32[]{:S(2)}) collective-permute-start(bf16[1024,128]{1,0:T(8,128)(2,1)S(1)} %get-tuple-element.59.own_ref), channel_id=1, source_target_pairs={{0,12},{4,0},{8,4},{12,8},{16,28},{20,16},{24,20},{28,24},{32,44},... | collective-permute-start | bytes 786440 | tf_op jit(solution)/shard_map/ppermute | solution.py:290
  9.5 1.6 %copy-start = (bf16[1,512,2048]{2,1,0:T(8,128)(2,1)S(1)}, bf16[1,512,2048]{2,1,0:T(8,128)(2,1)}, u32[]{:S(2)}) copy-start(bf16[1,512,2048]{2,1,0:T(8,128)(2,1)} %param.7) | copy-start | bytes 6291460
  11.1 0.7 copy-start.2
  13.0 15.2 %collective-permute-start.4 = (bf16[512,1024]{1,0:T(8,128)(2,1)S(1)}, bf16[512,1024]{1,0:T(8,128)(2,1)S(1)}, u32[]{:S(2)}, u32[]{:S(2)}) collective-permute-start(bf16[512,1024]{1,0:T(8,128)(2,1)S(1)} %get-tuple-element.76.refs_0_), channel_id=1, source_target_pairs={{0,64},{1,193},{2,66},{3,195},{64,128},{65,1},{66,130},{67,3},{128... | collective-permute-start | bytes 3145736 | tf_op jit(solution)/shard_map/ppermute | solution.py:290
  17.0 21.7 %collective-permute-start.18 = (bf16[512,1024]{1,0:T(8,128)(2,1)S(1)}, bf16[512,1024]{1,0:T(8,128)(2,1)S(1)}, u32[]{:S(2)}, u32[]{:S(2)}) collective-permute-start(bf16[512,1024]{1,0:T(8,128)(2,1)S(1)} %get-tuple-element.65.refs_0_), channel_id=1, source_target_pairs={{0,64},{1,193},{2,66},{3,195},{64,128},{65,1},{66,130},{67,3},{128... | collective-permute-start | bytes 3145736 | tf_op jit(solution)/shard_map/ppermute | solution.py:290
  17.6 2.9 %collective-permute-start = (f32[12,128]{1,0:T(8,128)S(1)}, f32[12,128]{1,0:T(8,128)S(1)}, u32[]{:S(2)}, u32[]{:S(2)}) collective-permute-start(f32[12,128]{1,0:T(8,128)S(1)} %pad_maximum_fusion), channel_id=1, source_target_pairs={{0,16},{4,20},{8,24},{12,28},{16,0},{20,4},{24,8},{28,12},{32,48},... | collective-permute-start | bytes 18440 | tf_op jit(solution)/shard_map/ppermute | solution.py:290
  20.5 4.0 %collective-permute-start.1 = (f32[12,128]{1,0:T(8,128)S(1)}, f32[12,128]{1,0:T(8,128)S(1)}, u32[]{:S(2)}, u32[]{:S(2)}) collective-permute-start(f32[12,128]{1,0:T(8,128)S(1)} %fusion.2), channel_id=1, source_target_pairs={{0,32},{4,36},{8,40},{12,44},{16,48},{20,52},{24,56},{28,60},{32,0... | collective-permute-start | bytes 18440 | tf_op jit(solution)/shard_map/ppermute | solution.py:290
  24.5 7.2 %collective-permute-start.6 = (bf16[512,128]{1,0:T(8,128)(2,1)S(1)}, bf16[512,128]{1,0:T(8,128)(2,1)S(1)}, u32[]{:S(2)}, u32[]{:S(2)}) collective-permute-start(bf16[512,128]{1,0:T(8,128)(2,1)S(1)} %slice.62), channel_id=1, source_target_pairs={{0,4},{4,8},{8,12},{12,0},{16,20},{20,24},{24,28},{28,16},{32,36},... | collective-permute-start | bytes 393224 | tf_op jit(solution)/shard_map/ppermute | solution.py:290
  25.9 7.5 %collective-permute-start.7 = (bf16[512,128]{1,0:T(8,128)(2,1)S(1)}, bf16[512,128]{1,0:T(8,128)(2,1)S(1)}, u32[]{:S(2)}, u32[]{:S(2)}) collective-permute-start(bf16[512,128]{1,0:T(8,128)(2,1)S(1)} %slice.63), channel_id=1, source_target_pairs={{0,12},{4,0},{8,4},{12,8},{16,28},{20,16},{24,20},{28,24},{32,44},... | collective-permute-start | bytes 393224 | tf_op jit(solution)/shard_map/ppermute | solution.py:290
  28.2 10.5 %collective-permute-start.5 = (f32[12,128]{1,0:T(8,128)S(1)}, f32[12,128]{1,0:T(8,128)S(1)}, u32[]{:S(2)}, u32[]{:S(2)}) collective-permute-start(f32[12,128]{1,0:T(8,128)S(1)} %add.37), channel_id=1, source_target_pairs={{0,4},{4,0},{8,12},{12,8},{16,20},{20,16},{24,28},{28,24},{32,36},... | collective-permute-start | bytes 18440 | tf_op jit(solution)/shard_map/ppermute | solution.py:290
  29.4 21.8 %collective-permute-start.9 = (bf16[512,1024]{1,0:T(8,128)(2,1)S(1)}, bf16[512,1024]{1,0:T(8,128)(2,1)S(1)}, u32[]{:S(2)}, u32[]{:S(2)}) collective-permute-start(bf16[512,1024]{1,0:T(8,128)(2,1)S(1)} %collective-permute-done.4.refs_1_), channel_id=1, source_target_pairs={{0,64},{1,193},{2,66},{3,195},{64,128},{65,1},{66,130},{67,3},{128... | collective-permute-start | bytes 3145736 | tf_op jit(solution)/shard_map/ppermute | solution.py:290
  38.8 22.6 %collective-permute-start.19 = (bf16[512,1024]{1,0:T(8,128)(2,1)S(1)}, bf16[512,1024]{1,0:T(8,128)(2,1)S(1)}, u32[]{:S(2)}, u32[]{:S(2)}) collective-permute-start(bf16[512,1024]{1,0:T(8,128)(2,1)S(1)} %collective-permute-done.18.refs_1_), channel_id=1, source_target_pairs={{0,64},{1,193},{2,66},{3,195},{64,128},{65,1},{66,130},{67,3},{128... | collective-permute-start | bytes 3145736 | tf_op jit(solution)/shard_map/ppermute | solution.py:290
  42.1 26.3 %collective-permute-start.13 = (bf16[1024,512]{1,0:T(8,128)(2,1)S(1)}, bf16[1024,512]{1,0:T(8,128)(2,1)S(1)}, u32[]{:S(2)}, u32[]{:S(2)}) collective-permute-start(bf16[1024,512]{1,0:T(8,128)(2,1)S(1)} %shard_map.58.own_ref), channel_id=1, source_target_pairs={{0,16},{4,20},{8,24},{12,28},{16,32},{20,36},{24,40},{28,44},{32,4... | collective-permute-start | bytes 3145736 | tf_op jit(solution)/shard_map/ppermute | solution.py:290
  43.3 25.0 %collective-permute-start.14 = (bf16[1024,512]{1,0:T(8,128)(2,1)S(1)}, bf16[1024,512]{1,0:T(8,128)(2,1)S(1)}, u32[]{:S(2)}, u32[]{:S(2)}) collective-permute-start(bf16[1024,512]{1,0:T(8,128)(2,1)S(1)} %shard_map.58.own_ref), channel_id=1, source_target_pairs={{0,48},{4,52},{8,56},{12,60},{16,0},{20,4},{24,8},{28,12},{32,16},... | collective-permute-start | bytes 3145736 | tf_op jit(solution)/shard_map/ppermute | solution.py:290
  44.8 6.4 %collective-permute-start.8 = (f32[12,128]{1,0:T(8,128)S(1)}, f32[12,128]{1,0:T(8,128)S(1)}, u32[]{:S(2)}, u32[]{:S(2)}) collective-permute-start(f32[12,128]{1,0:T(8,128)S(1)} %add.38), channel_id=1, source_target_pairs={{0,8},{4,12},{8,0},{12,4},{16,24},{20,28},{24,16},{28,20},{32,40},... | collective-permute-start | bytes 18440 | tf_op jit(solution)/shard_map/ppermute | solution.py:290
  51.2 4.1 %collective-permute-start.12 = (f32[4,128]{1,0:T(4,128)S(1)}, f32[4,128]{1,0:T(4,128)S(1)}, u32[]{:S(2)}, u32[]{:S(2)}) collective-permute-start(f32[4,128]{1,0:T(4,128)S(1)} %fusion.1), channel_id=1, source_target_pairs={{0,192},{1,65},{2,194},{3,67},{64,0},{65,129},{66,2},{67,131},{128... | collective-permute-start | bytes 6152 | tf_op jit(solution)/shard_map/ppermute | solution.py:290
  51.3 4.9 %collective-permute-start.11 = (f32[4,128]{1,0:T(4,128)S(1)}, f32[4,128]{1,0:T(4,128)S(1)}, u32[]{:S(2)}, u32[]{:S(2)}) collective-permute-start(f32[4,128]{1,0:T(4,128)S(1)} %fusion.1), channel_id=1, source_target_pairs={{0,128},{1,129},{2,130},{3,131},{64,192},{65,193},{66,194},{67,195... | collective-permute-start | bytes 6152 | tf_op jit(solution)/shard_map/ppermute | solution.py:290
  55.3 6.0 %collective-permute-start.10 = (f32[4,128]{1,0:T(4,128)S(1)}, f32[4,128]{1,0:T(4,128)S(1)}, u32[]{:S(2)}, u32[]{:S(2)}) collective-permute-start(f32[4,128]{1,0:T(4,128)S(1)} %fusion.1), channel_id=1, source_target_pairs={{0,64},{1,193},{2,66},{3,195},{64,128},{65,1},{66,130},{67,3},{128... | collective-permute-start | bytes 6152 | tf_op jit(solution)/shard_map/ppermute | solution.py:290
  61.3 21.2 %collective-permute-start.20 = (bf16[512,1024]{1,0:T(8,128)(2,1)S(1)}, bf16[512,1024]{1,0:T(8,128)(2,1)S(1)}, u32[]{:S(2)}, u32[]{:S(2)}) collective-permute-start(bf16[512,1024]{1,0:T(8,128)(2,1)S(1)} %collective-permute-done.9.refs_2_), channel_id=1, source_target_pairs={{0,64},{1,193},{2,66},{3,195},{64,128},{65,1},{66,130},{67,3},{128... | collective-permute-start | bytes 3145736 | tf_op jit(solution)/shard_map/ppermute | solution.py:290
  68.4 14.2 %collective-permute-start.15 = (bf16[512,512]{1,0:T(8,128)(2,1)S(1)}, bf16[512,512]{1,0:T(8,128)(2,1)S(1)}, u32[]{:S(2)}, u32[]{:S(2)}) collective-permute-start(bf16[512,512]{1,0:T(8,128)(2,1)S(1)} %slice.65), channel_id=1, source_target_pairs={{0,16},{4,20},{8,24},{12,28},{16,32},{20,36},{24,40},{28,44},{32,4... | collective-permute-start | bytes 1572872 | tf_op jit(solution)/shard_map/ppermute | solution.py:290
  69.3 2.8 %collective-permute-start.16 = (f32[8,128]{1,0:T(8,128)S(1)}, f32[8,128]{1,0:T(8,128)S(1)}, u32[]{:S(2)}, u32[]{:S(2)}) collective-permute-start(f32[8,128]{1,0:T(8,128)S(1)} %slice.66), channel_id=1, source_target_pairs={{0,1},{1,0},{2,3},{3,2},{4,5},{5,4},{6,7},{7,6},{8,9},{9,8},{10,11... | collective-permute-start | bytes 12296 | tf_op jit(solution)/shard_map/ppermute | solution.py:290
  70.4 16.0 %collective-permute-start.21 = (bf16[512,512]{1,0:T(8,128)(2,1)S(1)}, bf16[512,512]{1,0:T(8,128)(2,1)S(1)}, u32[]{:S(2)}, u32[]{:S(2)}) collective-permute-start(bf16[512,512]{1,0:T(8,128)(2,1)S(1)} %slice.67), channel_id=1, source_target_pairs={{0,48},{4,52},{8,56},{12,60},{16,0},{20,4},{24,8},{28,12},{32,16},... | collective-permute-start | bytes 1572872 | tf_op jit(solution)/shard_map/ppermute | solution.py:290
  72.1 2.8 %collective-permute-start.17 = (f32[8,128]{1,0:T(8,128)S(1)}, f32[8,128]{1,0:T(8,128)S(1)}, u32[]{:S(2)}, u32[]{:S(2)}) collective-permute-start(f32[8,128]{1,0:T(8,128)S(1)} %slice_add_fusion.4.sum_ref), channel_id=1, source_target_pairs={{0,2},{1,3},{2,0},{3,1},{4,6},{5,7},{6,4},{7,5},{8,10},{9,11},{10,... | collective-permute-start | bytes 12296 | tf_op jit(solution)/shard_map/ppermute | solution.py:290
  73.0 17.6 %collective-permute-start.22 = (bf16[256,1024]{1,0:T(8,128)(2,1)S(1)}, bf16[256,1024]{1,0:T(8,128)(2,1)S(1)}, u32[]{:S(2)}, u32[]{:S(2)}) collective-permute-start(bf16[256,1024]{1,0:T(8,128)(2,1)S(1)} %get-tuple-element.71), channel_id=1, source_target_pairs={{0,64},{1,193},{2,66},{3,195},{64,128},{65,1},{66,130},{67,3},{128... | collective-permute-start | bytes 1572872 | tf_op jit(solution)/shard_map/ppermute | solution.py:290
  84.9 4.0 %collective-permute-start.23 = (bf16[512,512]{1,0:T(8,128)(2,1)S(1)}, bf16[512,512]{1,0:T(8,128)(2,1)S(1)}, u32[]{:S(2)}, u32[]{:S(2)}) collective-permute-start(bf16[512,512]{1,0:T(8,128)(2,1)S(1)} %get-tuple-element.74), channel_id=1, source_target_pairs={{0,1},{1,0},{2,3},{3,2},{4,5},{5,4},{6,7},{7,6},{8,9},{9,8},{10,11... | collective-permute-start | bytes 1572872 | tf_op jit(solution)/shard_map/ppermute | solution.py:290
  88.8 2.0 %collective-permute-start.24 = (bf16[512,512]{1,0:T(8,128)(2,1)S(1)}, bf16[512,512]{1,0:T(8,128)(2,1)S(1)}, u32[]{:S(2)}, u32[]{:S(2)}) collective-permute-start(bf16[512,512]{1,0:T(8,128)(2,1)S(1)} %get-tuple-element.75), channel_id=1, source_target_pairs={{0,1},{1,0},{2,3},{3,2},{4,5},{5,4},{6,7},{7,6},{8,9},{9,8},{10,11... | collective-permute-start | bytes 1572872 | tf_op jit(solution)/shard_map/ppermute | solution.py:290
  93.2 8.3 %collective-permute-start.25 = (bf16[256,1024]{1,0:T(8,128)(2,1)S(1)}, bf16[256,1024]{1,0:T(8,128)(2,1)S(1)}, u32[]{:S(2)}, u32[]{:S(2)}) collective-permute-start(bf16[256,1024]{1,0:T(8,128)(2,1)S(1)} %get-tuple-element.77), channel_id=1, source_target_pairs={{0,64},{1,193},{2,66},{3,195},{64,128},{65,1},{66,130},{67,3},{128... | collective-permute-start | bytes 1572872 | tf_op jit(solution)/shard_map/ppermute | solution.py:290
  93.2 18.6 %collective-permute-start.28 = (bf16[512,512]{1,0:T(8,128)(2,1)S(1)}, bf16[512,512]{1,0:T(8,128)(2,1)S(1)}, u32[]{:S(2)}, u32[]{:S(2)}) collective-permute-start(bf16[512,512]{1,0:T(8,128)(2,1)S(1)} %shard_map.62), channel_id=1, source_target_pairs={{0,2},{1,3},{2,0},{3,1},{4,6},{5,7},{6,4},{7,5},{8,10},{9,11},{10,... | collective-permute-start | bytes 1572872 | tf_op jit(solution)/shard_map/ppermute | solution.py:290
  93.9 23.7 %collective-permute-start.29 = (bf16[512,512]{1,0:T(8,128)(2,1)}, bf16[512,512]{1,0:T(8,128)(2,1)}, u32[]{:S(2)}, u32[]{:S(2)}) collective-permute-start(bf16[512,512]{1,0:T(8,128)(2,1)} %shard_map.63), channel_id=1, source_target_pairs={{0,2},{1,3},{2,0},{3,1},{4,6},{5,7},{6,4},{7,5},{8,10},{9,11},{10,... | collective-permute-start | bytes 1572872 | tf_op jit(solution)/shard_map/ppermute | solution.py:290
  104.9 6.9 %copy-start.4 = (s32[8,4]{0,1:T(4,128)S(1)}, s32[8,4]{0,1:T(4,128)}, u32[]{:S(2)}) copy-start(s32[8,4]{0,1:T(4,128)} %param.9) | copy-start | bytes 388
  109.2 8.4 %collective-permute-start.26 = (bf16[512,512]{1,0:T(8,128)(2,1)}, bf16[512,512]{1,0:T(8,128)(2,1)}, u32[]{:S(2)}, u32[]{:S(2)}) collective-permute-start(bf16[512,512]{1,0:T(8,128)(2,1)} %get-tuple-element.80), channel_id=1, source_target_pairs={{0,1},{1,0},{2,3},{3,2},{4,5},{5,4},{6,7},{7,6},{8,9},{9,8},{10,11... | collective-permute-start | bytes 1572872 | tf_op jit(solution)/shard_map/ppermute | solution.py:290
  111.7 5.9 %collective-permute-start.27 = (bf16[512,512]{1,0:T(8,128)(2,1)}, bf16[512,512]{1,0:T(8,128)(2,1)}, u32[]{:S(2)}, u32[]{:S(2)}) collective-permute-start(bf16[512,512]{1,0:T(8,128)(2,1)} %get-tuple-element.82), channel_id=1, source_target_pairs={{0,1},{1,0},{2,3},{3,2},{4,5},{5,4},{6,7},{7,6},{8,9},{9,8},{10,11... | collective-permute-start | bytes 1572872 | tf_op jit(solution)/shard_map/ppermute | solution.py:290

commit v4 on v3

--- a/solution.py
+++ b/solution.py
@@ -195,32 +195,20 @@
     )(full, core, *hops)
 
 
-def multiply_split(full_ref, hops):
-    total = jnp.dot(full_ref[0], hops[0][...], preferred_element_type=F32)
-    for h in range(1, 3):
-        total += jnp.dot(full_ref[h], hops[h][...], preferred_element_type=F32)
-    total += jnp.dot(full_ref[3, :, :256], hops[3][...], preferred_element_type=F32)
-    return total + jnp.dot(full_ref[3, :, 256:], hops[4][...], preferred_element_type=F32)
-
-
-def split_specs(q):
-    return [pl.BlockSpec((512, 512), lambda i, *_: (0, q))] * 3 + [pl.BlockSpec((256, 512), lambda i, *_: (0, q))] * 2
-
-
 def pieces_kernel(full_ref, *refs):
-    total = multiply_split(full_ref, refs[:5]).astype(BF16)
+    total = multiply(full_ref, refs[:4]).astype(BF16)
     for k in range(2):
 
         @pl.when((pl.program_id(0) >> 1) == k)
         def _():
-            refs[5 + k][...] = total
+            refs[4 + k][...] = total
 
 
 def pieces(full, hops):
     return pl.pallas_call(
         pieces_kernel,
         grid=(4,),
-        in_specs=[ALL] + split_specs(0),
+        in_specs=[ALL] + hop_specs(0),
         out_specs=[UPPER, LOWER],
         out_shape=[jax.ShapeDtypeStruct((512, 512), BF16)] * 2,
         compiler_params=pltpu.CompilerParams(vmem_limit_bytes=VMEM),
@@ -229,14 +217,14 @@
 
 
 def product_kernel(full_ref, *refs):
-    refs[5][...] = multiply_split(full_ref, refs[:5])
+    refs[4][...] = multiply(full_ref, refs[:4])
 
 
 def product(full, hops):
     return pl.pallas_call(
         product_kernel,
         grid=(4,),
-        in_specs=[ALL] + split_specs(1),
+        in_specs=[ALL] + hop_specs(1),
         out_specs=ROWS,
         out_shape=jax.ShapeDtypeStruct((1024, 512), F32),
         compiler_params=pltpu.CompilerParams(vmem_limit_bytes=VMEM),
@@ -327,26 +315,25 @@
     order.wait(other, zr, zl)
     total = total + other
     zr2, zl2 = onward(zr, zl, "col", ALONG_Z)
-    order.wait(h32[1])
-    h32.append(send_y(h32[1]))
     other = order.send(total, "col", COLS[1])
     wide = gather(a, zr, zl, zr2, zl2)
     order.wait(zr2, zl2, other)
     xr, xl = both(wide, "col", ALONG_X)
+    h32.append(send_y(h32[1]))
     total = total + other
+    order.wait(h10[1])
     other = order.send(total, "col", COLS[2])
-    h10.append(send_y(h10[1]))
     order.wait(h32[2], other)
     total = total + other
     walk_b = 1.0 / (1.0 + total[8:])
     others = [send_y(walk_b, h) for h in (1, 2, 3)]
-    order.wait(h10[2], *others)
+    order.wait(*others)
     scale = jnp.stack([walk_b] + others, 0)
     h32.append(send_y(h32[2]))
 
     order.wait(xr, xl)
     xr2, xl2 = onward(xr, xl, "col", ALONG_X)
-    upper = send_y(h10[2][:256])
+    h10.append(send_y(h10[1]))
     sums = total[:8]
     more = order.send(sums, "rep", SWAP[1])
     most = early(place, scale, (wide, xr, xl))
@@ -362,11 +349,11 @@
     top2 = middle(full, top_core, h32, 0)
     order.wait(top2)
     top_chip = order.send(top2, "rep", SWAP[2])
-    low2 = middle(full, low_core, [lax.optimization_barrier((h32[0], top2, upper))[0]] + h32[1:], 1)
+    low2 = middle(full, low_core, [lax.optimization_barrier((h32[0], top2))[0]] + h32[1:], 1)
     order.wait(low2)
     low_chip = order.send(low2, "rep", SWAP[2])
-    lower = send_y(h10[2][256:])
-    hops = h10 + [upper, lax.optimization_barrier((lower, low2))[0]]
+    lower = send_y(h10[2])
+    hops = h10 + [lax.optimization_barrier((lower, low2))[0]]
     part1 = pieces(full, hops)
     part0 = product(full, hops)
     order.wait(part0)

time: 121 us -> 117 us (0.967)
  waiting for transfers between devices: 42.2 us -> 36.7 us
  starting transfers between devices: 49.6 us -> 51.5 us
    ppermute x30 -> x29, waiting for transfers between devices: 42.2 us -> 36.7 us  [send(): return lax.ppermute(value, axes, pairs)]
    ppermute x30 -> x29, starting transfers between devices: 49.6 us -> 51.5 us  [send(): return lax.ppermute(value, axes, pairs)]
  transfers between devices with their start and end apart: 30 -> 29, of which waited for: 13 -> 16; matrix products, arithmetic and copies ran while one was open for 0% -> 0% of each run, Pallas kernels for 15% -> 17%
where the time goes in v4:
time: 117 us
  starting transfers between devices  51.5 us (44%)
  waiting for transfers between devices  36.7 us (31%)
  Pallas kernels  24.5 us (21%)
  local copies, waits for them, and re-layouts  4.09 us (3%)
    ppermute x29, starting transfers between devices, send(): return lax.ppermute(value, axes, pairs)  51.5 us
    ppermute x29, waiting for transfers between devices, send(): return lax.ppermute(value, axes, pairs)  36.7 us
    pallas_call x2, Pallas kernels, opening(): pl.pallas_call(opening_kernel, grid_spec=pltpu.PrefetchScalarGridSpec(num...  4.65 us
    pallas_call x1, Pallas kernels, pieces(): pl.pallas_call(pieces_kernel, grid=(4,), in_specs=[ALL] + hop_specs(0), o...  4.36 us
    unnamed x11, local copies, waits for them, and re-layouts  3.96 us
    pallas_call x1, Pallas kernels, closing(): pl.pallas_call(closing_kernel, grid_spec=pltpu.PrefetchScalarGridSpec(num...  3.74 us
    pallas_call x2, Pallas kernels, middle(): pl.pallas_call(middle_kernel, grid=(2,), in_specs=[pl.BlockSpec((4, 256,...  3.51 us
    pallas_call x1, Pallas kernels, product(): pl.pallas_call(product_kernel, grid=(4,), in_specs=[ALL] + hop_specs(1),...  3.32 us
  transfers between devices with their start and end apart: 29, of which 16 were waited for; matrix products, arithmetic and copies ran while one was open for 0% of the time, Pallas kernels for 17%

profile of v4, /device:TPU:1, one launch (start us, length us, event | category | flops | bytes accessed | tf_op | source)
XLA Modules:
  0.0 117.0 jit_solution(4443935878916308807)
XLA Ops:
  0.0 0.9 copy-done.1
  1.6 0.8 shard_map.55
  2.4 3.9 %collective-permute-start.2 = (bf16[1024,128]{1,0:T(8,128)(2,1)S(1)}, bf16[1024,128]{1,0:T(8,128)(2,1)S(1)}, u32[]{:S(2)}, u32[]{:S(2)}) collective-permute-start(bf16[1024,128]{1,0:T(8,128)(2,1)S(1)} %get-tuple-element.59.own_ref), channel_id=1, source_target_pairs={{0,4},{4,8},{8,12},{12,0},{16,20},{20,24},{24,28},{28,16},{32,36},... | collective-permute-start | bytes 786440 | tf_op jit(solution)/shard_map/ppermute | solution.py:278
  6.3 3.1 %collective-permute-start.3 = (bf16[1024,128]{1,0:T(8,128)(2,1)S(1)}, bf16[1024,128]{1,0:T(8,128)(2,1)S(1)}, u32[]{:S(2)}, u32[]{:S(2)}) collective-permute-start(bf16[1024,128]{1,0:T(8,128)(2,1)S(1)} %get-tuple-element.59.own_ref), channel_id=1, source_target_pairs={{0,12},{4,0},{8,4},{12,8},{16,28},{20,16},{24,20},{28,24},{32,44},... | collective-permute-start | bytes 786440 | tf_op jit(solution)/shard_map/ppermute | solution.py:278
  9.5 1.6 %copy-done = bf16[1,512,2048]{2,1,0:T(8,128)(2,1)S(1)} copy-done((bf16[1,512,2048]{2,1,0:T(8,128)(2,1)S(1)}, bf16[1,512,2048]{2,1,0:T(8,128)(2,1)}, u32[]{:S(2)}) %copy-start) | copy-done | bytes 2097176
  11.7 1.2 %shard_map.56 = (bf16[512,1024]{1,0:T(8,128)(2,1)S(1)}, f32[2,4,8,128]{3,2,1,0:T(8,128)S(1)}) custom-call(s32[4]{0:T(128)S(1)} %pad_add_fusion.place_ref, s32[4,16]{1,0:T(4,128)S(1)} %bitcast.22, bf16[512,2048]{1,0:T(8,128)(2,1)S(1)} %bitcast.19), custom_call_target="tpu_custom_call" | custom-call | flops 1 | bytes 1 | tf_op jit(solution)/shard_map/pallas_call | solution.py:42
  13.0 2.8 %collective-permute-start.9 = (bf16[512,1024]{1,0:T(8,128)(2,1)S(1)}, bf16[512,1024]{1,0:T(8,128)(2,1)S(1)}, u32[]{:S(2)}, u32[]{:S(2)}) collective-permute-start(bf16[512,1024]{1,0:T(8,128)(2,1)S(1)} %get-tuple-element.74.refs_0_), channel_id=1, source_target_pairs={{0,64},{1,193},{2,66},{3,195},{64,128},{65,1},{66,130},{67,3},{128... | collective-permute-start | bytes 3145736 | tf_op jit(solution)/shard_map/ppermute | solution.py:278
  15.8 1.2 %shard_map.57 = (bf16[512,1024]{1,0:T(8,128)(2,1)S(1)}, f32[2,4,8,128]{3,2,1,0:T(8,128)S(1)}) custom-call(s32[4]{0:T(128)S(1)} %pad_add_fusion.place_ref, s32[4,16]{1,0:T(4,128)S(1)} %bitcast.23, bf16[512,2048]{1,0:T(8,128)(2,1)S(1)} %bitcast.20), custom_call_target="tpu_custom_call" | custom-call | flops 1 | bytes 1 | tf_op jit(solution)/shard_map/pallas_call | solution.py:42
  17.1 1.3 %collective-permute-start = (f32[12,128]{1,0:T(8,128)S(1)}, f32[12,128]{1,0:T(8,128)S(1)}, u32[]{:S(2)}, u32[]{:S(2)}) collective-permute-start(f32[12,128]{1,0:T(8,128)S(1)} %pad_maximum_fusion), channel_id=1, source_target_pairs={{0,16},{4,20},{8,24},{12,28},{16,0},{20,4},{24,8},{28,12},{32,48},... | collective-permute-start | bytes 18440 | tf_op jit(solution)/shard_map/ppermute | solution.py:278
  18.9 1.1 collective-permute-done
  20.0 2.7 %collective-permute-start.1 = (f32[12,128]{1,0:T(8,128)S(1)}, f32[12,128]{1,0:T(8,128)S(1)}, u32[]{:S(2)}, u32[]{:S(2)}) collective-permute-start(f32[12,128]{1,0:T(8,128)S(1)} %fusion.2), channel_id=1, source_target_pairs={{0,32},{4,36},{8,40},{12,44},{16,48},{20,52},{24,56},{28,60},{32,0... | collective-permute-start | bytes 18440 | tf_op jit(solution)/shard_map/ppermute | solution.py:278
  22.8 1.2 %collective-permute-done.1 = f32[12,128]{1,0:T(8,128)S(1)} collective-permute-done((f32[12,128]{1,0:T(8,128)S(1)}, f32[12,128]{1,0:T(8,128)S(1)}, u32[]{:S(2)}, u32[]{:S(2)}) %collective-permute-start.1) | collective-permute-done | bytes 6176 | tf_op jit(solution)/shard_map/ppermute | solution.py:278
  24.0 1.5 %collective-permute-start.5 = (bf16[512,128]{1,0:T(8,128)(2,1)S(1)}, bf16[512,128]{1,0:T(8,128)(2,1)S(1)}, u32[]{:S(2)}, u32[]{:S(2)}) collective-permute-start(bf16[512,128]{1,0:T(8,128)(2,1)S(1)} %slice.54), channel_id=1, source_target_pairs={{0,4},{4,8},{8,12},{12,0},{16,20},{20,24},{24,28},{28,16},{32,36},... | collective-permute-start | bytes 393224 | tf_op jit(solution)/shard_map/ppermute | solution.py:278
  25.5 2.2 %collective-permute-start.6 = (bf16[512,128]{1,0:T(8,128)(2,1)S(1)}, bf16[512,128]{1,0:T(8,128)(2,1)S(1)}, u32[]{:S(2)}, u32[]{:S(2)}) collective-permute-start(bf16[512,128]{1,0:T(8,128)(2,1)S(1)} %slice.55), channel_id=1, source_target_pairs={{0,12},{4,0},{8,4},{12,8},{16,28},{20,16},{24,20},{28,24},{32,44},... | collective-permute-start | bytes 393224 | tf_op jit(solution)/shard_map/ppermute | solution.py:278
  27.7 1.2 %collective-permute-start.4 = (f32[12,128]{1,0:T(8,128)S(1)}, f32[12,128]{1,0:T(8,128)S(1)}, u32[]{:S(2)}, u32[]{:S(2)}) collective-permute-start(f32[12,128]{1,0:T(8,128)S(1)} %add.37), channel_id=1, source_target_pairs={{0,4},{4,0},{8,12},{12,8},{16,20},{20,16},{24,28},{28,24},{32,36},... | collective-permute-start | bytes 18440 | tf_op jit(solution)/shard_map/ppermute | solution.py:278
  28.9 4.9 %collective-permute-done.4 = f32[12,128]{1,0:T(8,128)S(1)} collective-permute-done((f32[12,128]{1,0:T(8,128)S(1)}, f32[12,128]{1,0:T(8,128)S(1)}, u32[]{:S(2)}, u32[]{:S(2)}) %collective-permute-start.4) | collective-permute-done | bytes 6176 | tf_op jit(solution)/shard_map/ppermute | solution.py:278
  34.2 2.1 %collective-permute-start.14 = (bf16[1024,512]{1,0:T(8,128)(2,1)S(1)}, bf16[1024,512]{1,0:T(8,128)(2,1)S(1)}, u32[]{:S(2)}, u32[]{:S(2)}) collective-permute-start(bf16[1024,512]{1,0:T(8,128)(2,1)S(1)} %shard_map.58.own_ref), channel_id=1, source_target_pairs={{0,16},{4,20},{8,24},{12,28},{16,32},{20,36},{24,40},{28,44},{32,4... | collective-permute-start | bytes 3145736 | tf_op jit(solution)/shard_map/ppermute | solution.py:278
  37.0 1.8 %collective-permute-done.7.refs_1_ = bf16[512,1024]{1,0:T(8,128)(2,1)S(1)} collective-permute-done((bf16[512,1024]{1,0:T(8,128)(2,1)S(1)}, bf16[512,1024]{1,0:T(8,128)(2,1)S(1)}, u32[]{:S(2)}, u32[]{:S(2)}) %collective-permute-start.7) | collective-permute-done | bytes 1048608 | tf_op jit(solution)/shard_map/ppermute | solution.py:278
  38.7 4.4 %collective-permute-start.8 = (f32[12,128]{1,0:T(8,128)S(1)}, f32[12,128]{1,0:T(8,128)S(1)}, u32[]{:S(2)}, u32[]{:S(2)}) collective-permute-start(f32[12,128]{1,0:T(8,128)S(1)} %add.38), channel_id=1, source_target_pairs={{0,8},{4,12},{8,0},{12,4},{16,24},{20,28},{24,16},{28,20},{32,40},... | collective-permute-start | bytes 18440 | tf_op jit(solution)/shard_map/ppermute | solution.py:278
  43.1 2.0 %collective-permute-done.8 = f32[12,128]{1,0:T(8,128)S(1)} collective-permute-done((f32[12,128]{1,0:T(8,128)S(1)}, f32[12,128]{1,0:T(8,128)S(1)}, u32[]{:S(2)}, u32[]{:S(2)}) %collective-permute-start.8) | collective-permute-done | bytes 6176 | tf_op jit(solution)/shard_map/ppermute | solution.py:278
  45.2 4.8 %collective-permute-done.10.refs_2_ = bf16[512,1024]{1,0:T(8,128)(2,1)S(1)} collective-permute-done((bf16[512,1024]{1,0:T(8,128)(2,1)S(1)}, bf16[512,1024]{1,0:T(8,128)(2,1)S(1)}, u32[]{:S(2)}, u32[]{:S(2)}) %collective-permute-start.10) | collective-permute-done | bytes 1048608 | tf_op jit(solution)/shard_map/ppermute | solution.py:278
  50.0 0.8 collective-permute-start.13
  50.7 3.8 %collective-permute-start.12 = (f32[4,128]{1,0:T(4,128)S(1)}, f32[4,128]{1,0:T(4,128)S(1)}, u32[]{:S(2)}, u32[]{:S(2)}) collective-permute-start(f32[4,128]{1,0:T(4,128)S(1)} %fusion.1), channel_id=1, source_target_pairs={{0,128},{1,129},{2,130},{3,131},{64,192},{65,193},{66,194},{67,195... | collective-permute-start | bytes 6152 | tf_op jit(solution)/shard_map/ppermute | solution.py:278
  54.7 0.9 collective-permute-done.12
  55.6 1.7 %collective-permute-done.11 = f32[4,128]{1,0:T(4,128)S(1)} collective-permute-done((f32[4,128]{1,0:T(4,128)S(1)}, f32[4,128]{1,0:T(4,128)S(1)}, u32[]{:S(2)}, u32[]{:S(2)}) %collective-permute-start.11) | collective-permute-done | bytes 2080 | tf_op jit(solution)/shard_map/ppermute | solution.py:278
  57.3 1.2 %collective-permute-start.19 = (bf16[512,1024]{1,0:T(8,128)(2,1)S(1)}, bf16[512,1024]{1,0:T(8,128)(2,1)S(1)}, u32[]{:S(2)}, u32[]{:S(2)}) collective-permute-start(bf16[512,1024]{1,0:T(8,128)(2,1)S(1)} %collective-permute-done.10.refs_2_), channel_id=1, source_target_pairs={{0,64},{1,193},{2,66},{3,195},{64,128},{65,1},{66,130},{67,3},{128... | collective-permute-start | bytes 3145736 | tf_op jit(solution)/shard_map/ppermute | solution.py:278
  58.6 0.8 collective-permute-start.16
  59.5 4.0 %collective-permute-start.17 = (f32[8,128]{1,0:T(8,128)S(1)}, f32[8,128]{1,0:T(8,128)S(1)}, u32[]{:S(2)}, u32[]{:S(2)}) collective-permute-start(f32[8,128]{1,0:T(8,128)S(1)} %slice.58), channel_id=1, source_target_pairs={{0,1},{1,0},{2,3},{3,2},{4,5},{5,4},{6,7},{7,6},{8,9},{9,8},{10,11... | collective-permute-start | bytes 12296 | tf_op jit(solution)/shard_map/ppermute | solution.py:278
  63.5 1.5 %collective-permute-start.20 = (bf16[512,512]{1,0:T(8,128)(2,1)S(1)}, bf16[512,512]{1,0:T(8,128)(2,1)S(1)}, u32[]{:S(2)}, u32[]{:S(2)}) collective-permute-start(bf16[512,512]{1,0:T(8,128)(2,1)S(1)} %slice.59), channel_id=1, source_target_pairs={{0,48},{4,52},{8,56},{12,60},{16,0},{20,4},{24,8},{28,12},{32,16},... | collective-permute-start | bytes 1572872 | tf_op jit(solution)/shard_map/ppermute | solution.py:278
  64.9 0.8 collective-permute-start.21
  65.8 0.8 collective-permute-start.18
  66.6 1.4 %shard_map.59.full_ref = bf16[4,1024,512]{2,1,0:T(8,128)(2,1)S(1)} custom-call(s32[4]{0:T(128)S(1)} %pad_add_fusion.place_ref, f32[4,4,128]{2,1,0:T(4,128)S(1)} %pad_maximum_fusion.1.scale_ref, bf16[1024,512]{1,0:T(8,128)(2,1)S(1)} %shard_map.58.own_ref, bf16[1024,512]{1,0:T(8,128)(2,1)S(1)} %collective-permute-done.14.r_ref, ...), custom_call_target="tpu_custom_call" | custom-call | flops 1 | bytes 1 | tf_op jit(solution)/shard_map/pallas_call | solution.py:126
  68.6 1.4 %collective-permute-done.16.piece_ref = bf16[512,512]{1,0:T(8,128)(2,1)S(1)} collective-permute-done((bf16[512,512]{1,0:T(8,128)(2,1)S(1)}, bf16[512,512]{1,0:T(8,128)(2,1)S(1)}, u32[]{:S(2)}, u32[]{:S(2)}) %collective-permute-start.16) | collective-permute-done | bytes 524320 | tf_op jit(solution)/shard_map/ppermute | solution.py:278
  70.0 1.2 %collective-permute-done.19.refs_3_ = bf16[512,1024]{1,0:T(8,128)(2,1)S(1)} collective-permute-done((bf16[512,1024]{1,0:T(8,128)(2,1)S(1)}, bf16[512,1024]{1,0:T(8,128)(2,1)S(1)}, u32[]{:S(2)}, u32[]{:S(2)}) %collective-permute-start.19) | collective-permute-done | bytes 1048608 | tf_op jit(solution)/shard_map/ppermute | solution.py:278
  71.3 2.3 %shard_map.60 = (bf16[4,1024,512]{2,1,0:T(8,128)(2,1)S(1)}, bf16[512,512]{1,0:T(8,128)(2,1)S(1)}) custom-call(s32[4]{0:T(128)S(1)} %pad_add_fusion.place_ref, f32[4,4,128]{2,1,0:T(4,128)S(1)} %pad_maximum_fusion.1.scale_ref, bf16[4,1024,512]{2,1,0:T(8,128)(2,1)S(1)} %shard_map.59.full_ref, ...), custom_call_target="tpu_custom_call", output_to_operand_aliasing={{0}: (2, {})} | custom-call | flops 1 | bytes 1 | tf_op jit(solution)/shard_map/pallas_call | solution.py:161
  73.6 4.6 %collective-permute-start.22 = (bf16[512,512]{1,0:T(8,128)(2,1)S(1)}, bf16[512,512]{1,0:T(8,128)(2,1)S(1)}, u32[]{:S(2)}, u32[]{:S(2)}) collective-permute-start(bf16[512,512]{1,0:T(8,128)(2,1)S(1)} %get-tuple-element.72), channel_id=1, source_target_pairs={{0,1},{1,0},{2,3},{3,2},{4,5},{5,4},{6,7},{7,6},{8,9},{9,8},{10,11... | collective-permute-start | bytes 1572872 | tf_op jit(solution)/shard_map/ppermute | solution.py:278
  78.1 2.3 %shard_map.61 = (bf16[4,1024,512]{2,1,0:T(8,128)(2,1)S(1)}, bf16[512,512]{1,0:T(8,128)(2,1)S(1)}) custom-call(s32[4]{0:T(128)S(1)} %pad_add_fusion.place_ref, f32[4,4,128]{2,1,0:T(4,128)S(1)} %pad_maximum_fusion.1.scale_ref, bf16[4,1024,512]{2,1,0:T(8,128)(2,1)S(1)} %get-tuple-element.66.full_ref, ...), custom_call_target="tpu_custom_call", output_to_operand_aliasing={{0}: (2, {})} | custom-call | flops 1 | bytes 1 | tf_op jit(solution)/shard_map/pallas_call | solution.py:161
  80.6 1.8 %shard_map.62 = bf16[512,512]{1,0:T(8,128)(2,1)S(1)} custom-call(bf16[4,1024,512]{2,1,0:T(8,128)(2,1)S(1)} %get-tuple-element.68.full_ref, bf16[512,512]{1,0:T(8,128)(2,1)S(1)} %collective-permute-done.22.core_ref, bf16[512,1024]{1,0:T(8,128)(2,1)S(1)} %get-tuple-element.74.refs_0_, bf16[512,1024]{1,0:T(8,128)(2,1)S(1)} %collective-permute-done.9.refs_1_, ...), custom_call_target="tpu_custom_call" | custom-call | flops 1 | bytes 1 | tf_op jit(solution)/shard_map/pallas_call | solution.py:187
  82.5 1.7 %shard_map.63 = bf16[512,512]{1,0:T(8,128)(2,1)S(1)} custom-call(bf16[4,1024,512]{2,1,0:T(8,128)(2,1)S(1)} %get-tuple-element.68.full_ref, bf16[512,512]{1,0:T(8,128)(2,1)S(1)} %collective-permute-done.23.core_ref, bf16[512,1024]{1,0:T(8,128)(2,1)S(1)} %get-tuple-element.74.refs_0_, bf16[512,1024]{1,0:T(8,128)(2,1)S(1)} %collective-permute-done.9.refs_1_, ...), custom_call_target="tpu_custom_call" | custom-call | flops 1 | bytes 1 | tf_op jit(solution)/shard_map/pallas_call | solution.py:187
  84.7 0.7 collective-permute-start.27
  85.5 0.7 collective-permute-start.28
  86.2 12.2 %collective-permute-done.24.refs_3_ = bf16[512,1024]{1,0:T(8,128)(2,1)S(1)} collective-permute-done((bf16[512,1024]{1,0:T(8,128)(2,1)S(1)}, bf16[512,1024]{1,0:T(8,128)(2,1)S(1)}, u32[]{:S(2)}, u32[]{:S(2)}) %collective-permute-start.24) | collective-permute-done | bytes 1048608 | tf_op jit(solution)/shard_map/ppermute | solution.py:278
  98.4 3.3 %shard_map.64.part_ref = f32[1024,512]{1,0:T(8,128)S(1)} custom-call(bf16[4,1024,512]{2,1,0:T(8,128)(2,1)S(1)} %get-tuple-element.68.full_ref, bf16[512,1024]{1,0:T(8,128)(2,1)S(1)} %get-tuple-element.54.refs_0_, bf16[512,1024]{1,0:T(8,128)(2,1)S(1)} %collective-permute-done.7.refs_1_, bf16[512,1024]{1,0:T(8,128)(2,1)S(1)} %collective-permute-done.21.refs_2_, ...), custom_call_target="tpu_custom_call" | custom-call | flops 1 | bytes 1 | tf_op jit(solution)/shard_map/pallas_call | solution.py:224
  101.7 4.4 %shard_map.65 = (bf16[512,512]{1,0:T(8,128)(2,1)}, bf16[512,512]{1,0:T(8,128)(2,1)}) custom-call(bf16[4,1024,512]{2,1,0:T(8,128)(2,1)S(1)} %get-tuple-element.68.full_ref, bf16[512,1024]{1,0:T(8,128)(2,1)S(1)} %get-tuple-element.54.refs_0_, bf16[512,1024]{1,0:T(8,128)(2,1)S(1)} %collective-permute-done.7.refs_1_, ...), custom_call_target="tpu_custom_call" | custom-call | flops 1 | bytes 1 | tf_op jit(solution)/shard_map/pallas_call | solution.py:208
  106.1 4.6 %collective-permute-start.25 = (bf16[512,512]{1,0:T(8,128)(2,1)}, bf16[512,512]{1,0:T(8,128)(2,1)}, u32[]{:S(2)}, u32[]{:S(2)}) collective-permute-start(bf16[512,512]{1,0:T(8,128)(2,1)} %get-tuple-element.78), channel_id=1, source_target_pairs={{0,1},{1,0},{2,3},{3,2},{4,5},{5,4},{6,7},{7,6},{8,9},{9,8},{10,11... | collective-permute-start | bytes 1572872 | tf_op jit(solution)/shard_map/ppermute | solution.py:278
  110.8 1.8 %collective-permute-done.25.core0_ref = bf16[512,512]{1,0:T(8,128)(2,1)} collective-permute-done((bf16[512,512]{1,0:T(8,128)(2,1)}, bf16[512,512]{1,0:T(8,128)(2,1)}, u32[]{:S(2)}, u32[]{:S(2)}) %collective-permute-start.25) | collective-permute-done | bytes 524320 | tf_op jit(solution)/shard_map/ppermute | solution.py:278
  112.5 0.7 collective-permute-done.26.core1_ref
  113.3 3.7 %shard_map.66 = bf16[1024,512]{1,0:T(8,128)(2,1)} custom-call(s32[8,4]{1,0:T(8,128)S(1)} %copy.13.flags_ref, f32[1024,512]{1,0:T(8,128)S(1)} %shard_map.64.part_ref, bf16[512,512]{1,0:T(8,128)(2,1)} %collective-permute-done.25.core0_ref, bf16[512,512]{1,0:T(8,128)(2,1)} %collective-permute-done.26.core1_ref, ...), custom_call_target="tpu_custom_call" | custom-call | flops 1 | bytes 1 | tf_op jit(solution)/shard_map/pallas_call | solution.py:256
  (54 shorter events, 4.6 us)
Async XLA Ops:
  0.0 0.9 copy-start.1
  1.0 0.7 copy-start.3
  2.4 20.4 %collective-permute-start.2 = (bf16[1024,128]{1,0:T(8,128)(2,1)S(1)}, bf16[1024,128]{1,0:T(8,128)(2,1)S(1)}, u32[]{:S(2)}, u32[]{:S(2)}) collective-permute-start(bf16[1024,128]{1,0:T(8,128)(2,1)S(1)} %get-tuple-element.59.own_ref), channel_id=1, source_target_pairs={{0,4},{4,8},{8,12},{12,0},{16,20},{20,24},{24,28},{28,16},{32,36},... | collective-permute-start | bytes 786440 | tf_op jit(solution)/shard_map/ppermute | solution.py:278
  6.3 17.8 %collective-permute-start.3 = (bf16[1024,128]{1,0:T(8,128)(2,1)S(1)}, bf16[1024,128]{1,0:T(8,128)(2,1)S(1)}, u32[]{:S(2)}, u32[]{:S(2)}) collective-permute-start(bf16[1024,128]{1,0:T(8,128)(2,1)S(1)} %get-tuple-element.59.own_ref), channel_id=1, source_target_pairs={{0,12},{4,0},{8,4},{12,8},{16,28},{20,16},{24,20},{28,24},{32,44},... | collective-permute-start | bytes 786440 | tf_op jit(solution)/shard_map/ppermute | solution.py:278
  9.5 1.6 %copy-start = (bf16[1,512,2048]{2,1,0:T(8,128)(2,1)S(1)}, bf16[1,512,2048]{2,1,0:T(8,128)(2,1)}, u32[]{:S(2)}) copy-start(bf16[1,512,2048]{2,1,0:T(8,128)(2,1)} %param.7) | copy-start | bytes 6291460
  11.1 0.7 copy-start.2
  13.0 20.8 %collective-permute-start.9 = (bf16[512,1024]{1,0:T(8,128)(2,1)S(1)}, bf16[512,1024]{1,0:T(8,128)(2,1)S(1)}, u32[]{:S(2)}, u32[]{:S(2)}) collective-permute-start(bf16[512,1024]{1,0:T(8,128)(2,1)S(1)} %get-tuple-element.74.refs_0_), channel_id=1, source_target_pairs={{0,64},{1,193},{2,66},{3,195},{64,128},{65,1},{66,130},{67,3},{128... | collective-permute-start | bytes 3145736 | tf_op jit(solution)/shard_map/ppermute | solution.py:278
  17.1 2.9 %collective-permute-start = (f32[12,128]{1,0:T(8,128)S(1)}, f32[12,128]{1,0:T(8,128)S(1)}, u32[]{:S(2)}, u32[]{:S(2)}) collective-permute-start(f32[12,128]{1,0:T(8,128)S(1)} %pad_maximum_fusion), channel_id=1, source_target_pairs={{0,16},{4,20},{8,24},{12,28},{16,0},{20,4},{24,8},{28,12},{32,48},... | collective-permute-start | bytes 18440 | tf_op jit(solution)/shard_map/ppermute | solution.py:278
  18.4 20.3 %collective-permute-start.7 = (bf16[512,1024]{1,0:T(8,128)(2,1)S(1)}, bf16[512,1024]{1,0:T(8,128)(2,1)S(1)}, u32[]{:S(2)}, u32[]{:S(2)}) collective-permute-start(bf16[512,1024]{1,0:T(8,128)(2,1)S(1)} %get-tuple-element.54.refs_0_), channel_id=1, source_target_pairs={{0,64},{1,193},{2,66},{3,195},{64,128},{65,1},{66,130},{67,3},{128... | collective-permute-start | bytes 3145736 | tf_op jit(solution)/shard_map/ppermute | solution.py:278
  20.0 4.0 %collective-permute-start.1 = (f32[12,128]{1,0:T(8,128)S(1)}, f32[12,128]{1,0:T(8,128)S(1)}, u32[]{:S(2)}, u32[]{:S(2)}) collective-permute-start(f32[12,128]{1,0:T(8,128)S(1)} %fusion.2), channel_id=1, source_target_pairs={{0,32},{4,36},{8,40},{12,44},{16,48},{20,52},{24,56},{28,60},{32,0... | collective-permute-start | bytes 18440 | tf_op jit(solution)/shard_map/ppermute | solution.py:278
  24.0 9.8 %collective-permute-start.5 = (bf16[512,128]{1,0:T(8,128)(2,1)S(1)}, bf16[512,128]{1,0:T(8,128)(2,1)S(1)}, u32[]{:S(2)}, u32[]{:S(2)}) collective-permute-start(bf16[512,128]{1,0:T(8,128)(2,1)S(1)} %slice.54), channel_id=1, source_target_pairs={{0,4},{4,8},{8,12},{12,0},{16,20},{20,24},{24,28},{28,16},{32,36},... | collective-permute-start | bytes 393224 | tf_op jit(solution)/shard_map/ppermute | solution.py:278
  25.5 8.3 %collective-permute-start.6 = (bf16[512,128]{1,0:T(8,128)(2,1)S(1)}, bf16[512,128]{1,0:T(8,128)(2,1)S(1)}, u32[]{:S(2)}, u32[]{:S(2)}) collective-permute-start(bf16[512,128]{1,0:T(8,128)(2,1)S(1)} %slice.55), channel_id=1, source_target_pairs={{0,12},{4,0},{8,4},{12,8},{16,28},{20,16},{24,20},{28,24},{32,44},... | collective-permute-start | bytes 393224 | tf_op jit(solution)/shard_map/ppermute | solution.py:278
  27.7 6.1 %collective-permute-start.4 = (f32[12,128]{1,0:T(8,128)S(1)}, f32[12,128]{1,0:T(8,128)S(1)}, u32[]{:S(2)}, u32[]{:S(2)}) collective-permute-start(f32[12,128]{1,0:T(8,128)S(1)} %add.37), channel_id=1, source_target_pairs={{0,4},{4,0},{8,12},{12,8},{16,20},{20,16},{24,28},{28,24},{32,36},... | collective-permute-start | bytes 18440 | tf_op jit(solution)/shard_map/ppermute | solution.py:278
  33.8 16.2 %collective-permute-start.10 = (bf16[512,1024]{1,0:T(8,128)(2,1)S(1)}, bf16[512,1024]{1,0:T(8,128)(2,1)S(1)}, u32[]{:S(2)}, u32[]{:S(2)}) collective-permute-start(bf16[512,1024]{1,0:T(8,128)(2,1)S(1)} %collective-permute-done.9.refs_1_), channel_id=1, source_target_pairs={{0,64},{1,193},{2,66},{3,195},{64,128},{65,1},{66,130},{67,3},{128... | collective-permute-start | bytes 3145736 | tf_op jit(solution)/shard_map/ppermute | solution.py:278
  34.2 24.3 %collective-permute-start.14 = (bf16[1024,512]{1,0:T(8,128)(2,1)S(1)}, bf16[1024,512]{1,0:T(8,128)(2,1)S(1)}, u32[]{:S(2)}, u32[]{:S(2)}) collective-permute-start(bf16[1024,512]{1,0:T(8,128)(2,1)S(1)} %shard_map.58.own_ref), channel_id=1, source_target_pairs={{0,16},{4,20},{8,24},{12,28},{16,32},{20,36},{24,40},{28,44},{32,4... | collective-permute-start | bytes 3145736 | tf_op jit(solution)/shard_map/ppermute | solution.py:278
  36.3 22.3 %collective-permute-start.15 = (bf16[1024,512]{1,0:T(8,128)(2,1)S(1)}, bf16[1024,512]{1,0:T(8,128)(2,1)S(1)}, u32[]{:S(2)}, u32[]{:S(2)}) collective-permute-start(bf16[1024,512]{1,0:T(8,128)(2,1)S(1)} %shard_map.58.own_ref), channel_id=1, source_target_pairs={{0,48},{4,52},{8,56},{12,60},{16,0},{20,4},{24,8},{28,12},{32,16},... | collective-permute-start | bytes 3145736 | tf_op jit(solution)/shard_map/ppermute | solution.py:278
  38.7 6.4 %collective-permute-start.8 = (f32[12,128]{1,0:T(8,128)S(1)}, f32[12,128]{1,0:T(8,128)S(1)}, u32[]{:S(2)}, u32[]{:S(2)}) collective-permute-start(f32[12,128]{1,0:T(8,128)S(1)} %add.38), channel_id=1, source_target_pairs={{0,8},{4,12},{8,0},{12,4},{16,24},{20,28},{24,16},{28,20},{32,40},... | collective-permute-start | bytes 18440 | tf_op jit(solution)/shard_map/ppermute | solution.py:278
  50.0 4.7 %collective-permute-start.13 = (f32[4,128]{1,0:T(4,128)S(1)}, f32[4,128]{1,0:T(4,128)S(1)}, u32[]{:S(2)}, u32[]{:S(2)}) collective-permute-start(f32[4,128]{1,0:T(4,128)S(1)} %fusion.1), channel_id=1, source_target_pairs={{0,192},{1,65},{2,194},{3,67},{64,0},{65,129},{66,2},{67,131},{128... | collective-permute-start | bytes 6152 | tf_op jit(solution)/shard_map/ppermute | solution.py:278
  50.7 4.8 %collective-permute-start.12 = (f32[4,128]{1,0:T(4,128)S(1)}, f32[4,128]{1,0:T(4,128)S(1)}, u32[]{:S(2)}, u32[]{:S(2)}) collective-permute-start(f32[4,128]{1,0:T(4,128)S(1)} %fusion.1), channel_id=1, source_target_pairs={{0,128},{1,129},{2,130},{3,131},{64,192},{65,193},{66,194},{67,195... | collective-permute-start | bytes 6152 | tf_op jit(solution)/shard_map/ppermute | solution.py:278
  54.6 2.7 %collective-permute-start.11 = (f32[4,128]{1,0:T(4,128)S(1)}, f32[4,128]{1,0:T(4,128)S(1)}, u32[]{:S(2)}, u32[]{:S(2)}) collective-permute-start(f32[4,128]{1,0:T(4,128)S(1)} %fusion.1), channel_id=1, source_target_pairs={{0,64},{1,193},{2,66},{3,195},{64,128},{65,1},{66,130},{67,3},{128... | collective-permute-start | bytes 6152 | tf_op jit(solution)/shard_map/ppermute | solution.py:278
  57.3 13.9 %collective-permute-start.19 = (bf16[512,1024]{1,0:T(8,128)(2,1)S(1)}, bf16[512,1024]{1,0:T(8,128)(2,1)S(1)}, u32[]{:S(2)}, u32[]{:S(2)}) collective-permute-start(bf16[512,1024]{1,0:T(8,128)(2,1)S(1)} %collective-permute-done.10.refs_2_), channel_id=1, source_target_pairs={{0,64},{1,193},{2,66},{3,195},{64,128},{65,1},{66,130},{67,3},{128... | collective-permute-start | bytes 3145736 | tf_op jit(solution)/shard_map/ppermute | solution.py:278
  58.6 11.4 %collective-permute-start.16 = (bf16[512,512]{1,0:T(8,128)(2,1)S(1)}, bf16[512,512]{1,0:T(8,128)(2,1)S(1)}, u32[]{:S(2)}, u32[]{:S(2)}) collective-permute-start(bf16[512,512]{1,0:T(8,128)(2,1)S(1)} %slice.57), channel_id=1, source_target_pairs={{0,16},{4,20},{8,24},{12,28},{16,32},{20,36},{24,40},{28,44},{32,4... | collective-permute-start | bytes 1572872 | tf_op jit(solution)/shard_map/ppermute | solution.py:278
  59.5 6.3 %collective-permute-start.17 = (f32[8,128]{1,0:T(8,128)S(1)}, f32[8,128]{1,0:T(8,128)S(1)}, u32[]{:S(2)}, u32[]{:S(2)}) collective-permute-start(f32[8,128]{1,0:T(8,128)S(1)} %slice.58), channel_id=1, source_target_pairs={{0,1},{1,0},{2,3},{3,2},{4,5},{5,4},{6,7},{7,6},{8,9},{9,8},{10,11... | collective-permute-start | bytes 12296 | tf_op jit(solution)/shard_map/ppermute | solution.py:278
  63.5 14.7 %collective-permute-start.20 = (bf16[512,512]{1,0:T(8,128)(2,1)S(1)}, bf16[512,512]{1,0:T(8,128)(2,1)S(1)}, u32[]{:S(2)}, u32[]{:S(2)}) collective-permute-start(bf16[512,512]{1,0:T(8,128)(2,1)S(1)} %slice.59), channel_id=1, source_target_pairs={{0,48},{4,52},{8,56},{12,60},{16,0},{20,4},{24,8},{28,12},{32,16},... | collective-permute-start | bytes 1572872 | tf_op jit(solution)/shard_map/ppermute | solution.py:278
  64.9 19.3 %collective-permute-start.21 = (bf16[512,1024]{1,0:T(8,128)(2,1)S(1)}, bf16[512,1024]{1,0:T(8,128)(2,1)S(1)}, u32[]{:S(2)}, u32[]{:S(2)}) collective-permute-start(bf16[512,1024]{1,0:T(8,128)(2,1)S(1)} %collective-permute-done.7.refs_1_), channel_id=1, source_target_pairs={{0,64},{1,193},{2,66},{3,195},{64,128},{65,1},{66,130},{67,3},{128... | collective-permute-start | bytes 3145736 | tf_op jit(solution)/shard_map/ppermute | solution.py:278
  65.8 2.8 %collective-permute-start.18 = (f32[8,128]{1,0:T(8,128)S(1)}, f32[8,128]{1,0:T(8,128)S(1)}, u32[]{:S(2)}, u32[]{:S(2)}) collective-permute-start(f32[8,128]{1,0:T(8,128)S(1)} %slice_add_fusion.4.sum_ref), channel_id=1, source_target_pairs={{0,2},{1,3},{2,0},{3,1},{4,6},{5,7},{6,4},{7,5},{8,10},{9,11},{10,... | collective-permute-start | bytes 12296 | tf_op jit(solution)/shard_map/ppermute | solution.py:278
  73.6 7.0 %collective-permute-start.22 = (bf16[512,512]{1,0:T(8,128)(2,1)S(1)}, bf16[512,512]{1,0:T(8,128)(2,1)S(1)}, u32[]{:S(2)}, u32[]{:S(2)}) collective-permute-start(bf16[512,512]{1,0:T(8,128)(2,1)S(1)} %get-tuple-element.72), channel_id=1, source_target_pairs={{0,1},{1,0},{2,3},{3,2},{4,5},{5,4},{6,7},{7,6},{8,9},{9,8},{10,11... | collective-permute-start | bytes 1572872 | tf_op jit(solution)/shard_map/ppermute | solution.py:278
  80.5 2.0 %collective-permute-start.23 = (bf16[512,512]{1,0:T(8,128)(2,1)S(1)}, bf16[512,512]{1,0:T(8,128)(2,1)S(1)}, u32[]{:S(2)}, u32[]{:S(2)}) collective-permute-start(bf16[512,512]{1,0:T(8,128)(2,1)S(1)} %get-tuple-element.73), channel_id=1, source_target_pairs={{0,1},{1,0},{2,3},{3,2},{4,5},{5,4},{6,7},{7,6},{8,9},{9,8},{10,11... | collective-permute-start | bytes 1572872 | tf_op jit(solution)/shard_map/ppermute | solution.py:278
  84.2 14.1 %collective-permute-start.24 = (bf16[512,1024]{1,0:T(8,128)(2,1)S(1)}, bf16[512,1024]{1,0:T(8,128)(2,1)S(1)}, u32[]{:S(2)}, u32[]{:S(2)}) collective-permute-start(bf16[512,1024]{1,0:T(8,128)(2,1)S(1)} %collective-permute-done.21.refs_2_), channel_id=1, source_target_pairs={{0,64},{1,193},{2,66},{3,195},{64,128},{65,1},{66,130},{67,3},{128... | collective-permute-start | bytes 3145736 | tf_op jit(solution)/shard_map/ppermute | solution.py:278
  84.7 26.0 %collective-permute-start.27 = (bf16[512,512]{1,0:T(8,128)(2,1)S(1)}, bf16[512,512]{1,0:T(8,128)(2,1)}, u32[]{:S(2)}, u32[]{:S(2)}) collective-permute-start(bf16[512,512]{1,0:T(8,128)(2,1)S(1)} %shard_map.62), channel_id=1, source_target_pairs={{0,2},{1,3},{2,0},{3,1},{4,6},{5,7},{6,4},{7,5},{8,10},{9,11},{10,... | collective-permute-start | bytes 1572872 | tf_op jit(solution)/shard_map/ppermute | solution.py:278
  85.5 25.3 %collective-permute-start.28 = (bf16[512,512]{1,0:T(8,128)(2,1)S(1)}, bf16[512,512]{1,0:T(8,128)(2,1)}, u32[]{:S(2)}, u32[]{:S(2)}) collective-permute-start(bf16[512,512]{1,0:T(8,128)(2,1)S(1)} %shard_map.63), channel_id=1, source_target_pairs={{0,2},{1,3},{2,0},{3,1},{4,6},{5,7},{6,4},{7,5},{8,10},{9,11},{10,... | collective-permute-start | bytes 1572872 | tf_op jit(solution)/shard_map/ppermute | solution.py:278
  101.7 9.0 %copy-start.4 = (s32[8,4]{0,1:T(4,128)S(1)}, s32[8,4]{0,1:T(4,128)}, u32[]{:S(2)}) copy-start(s32[8,4]{0,1:T(4,128)} %param.9) | copy-start | bytes 388
  106.1 6.5 %collective-permute-start.25 = (bf16[512,512]{1,0:T(8,128)(2,1)}, bf16[512,512]{1,0:T(8,128)(2,1)}, u32[]{:S(2)}, u32[]{:S(2)}) collective-permute-start(bf16[512,512]{1,0:T(8,128)(2,1)} %get-tuple-element.78), channel_id=1, source_target_pairs={{0,1},{1,0},{2,3},{3,2},{4,5},{5,4},{6,7},{7,6},{8,9},{9,8},{10,11... | collective-permute-start | bytes 1572872 | tf_op jit(solution)/shard_map/ppermute | solution.py:278
  110.7 2.6 %collective-permute-start.26 = (bf16[512,512]{1,0:T(8,128)(2,1)}, bf16[512,512]{1,0:T(8,128)(2,1)}, u32[]{:S(2)}, u32[]{:S(2)}) collective-permute-start(bf16[512,512]{1,0:T(8,128)(2,1)} %get-tuple-element.80), channel_id=1, source_target_pairs={{0,1},{1,0},{2,3},{3,2},{4,5},{5,4},{6,7},{7,6},{8,9},{9,8},{10,11... | collective-permute-start | bytes 1572872 | tf_op jit(solution)/shard_map/ppermute | solution.py:278

commit v5 on v4

--- a/solution.py
+++ b/solution.py
@@ -195,39 +195,26 @@
     )(full, core, *hops)
 
 
-def pieces_kernel(full_ref, *refs):
-    total = multiply(full_ref, refs[:4]).astype(BF16)
-    for k in range(2):
+def pair_kernel(full_ref, *refs):
+    hops, (upper_ref, lower_ref, part_ref) = refs[:4], refs[4:]
+    swapped = multiply(full_ref, [hop[:, :512] for hop in hops]).astype(BF16)
+    for k, ref in enumerate((upper_ref, lower_ref)):
 
         @pl.when((pl.program_id(0) >> 1) == k)
         def _():
-            refs[4 + k][...] = total
-
-
-def pieces(full, hops):
-    return pl.pallas_call(
-        pieces_kernel,
+            ref[...] = swapped
+
+    part_ref[...] = multiply(full_ref, [hop[:, 512:] for hop in hops])
+
+
+def pair(full, hops):
+    return pl.pallas_call(
+        pair_kernel,
         grid=(4,),
-        in_specs=[ALL] + hop_specs(0),
-        out_specs=[UPPER, LOWER],
-        out_shape=[jax.ShapeDtypeStruct((512, 512), BF16)] * 2,
-        compiler_params=pltpu.CompilerParams(vmem_limit_bytes=VMEM),
-        cost_estimate=TINY,
-    )(full, *hops)
-
-
-def product_kernel(full_ref, *refs):
-    refs[4][...] = multiply(full_ref, refs[:4])
-
-
-def product(full, hops):
-    return pl.pallas_call(
-        product_kernel,
-        grid=(4,),
-        in_specs=[ALL] + hop_specs(1),
-        out_specs=ROWS,
-        out_shape=jax.ShapeDtypeStruct((1024, 512), F32),
-        compiler_params=pltpu.CompilerParams(vmem_limit_bytes=VMEM),
+        in_specs=[ALL] + [pl.BlockSpec((512, 1024), lambda i: (0, 0))] * 4,
+        out_specs=[UPPER, LOWER, ROWS],
+        out_shape=[jax.ShapeDtypeStruct((512, 512), BF16)] * 2 + [jax.ShapeDtypeStruct((1024, 512), F32)],
+        compiler_params=pltpu.CompilerParams(vmem_limit_bytes=20 << 20),
         cost_estimate=TINY,
     )(full, *hops)
 
@@ -354,9 +341,7 @@
     low_chip = order.send(low2, "rep", SWAP[2])
     lower = send_y(h10[2])
     hops = h10 + [lax.optimization_barrier((lower, low2))[0]]
-    part1 = pieces(full, hops)
-    part0 = product(full, hops)
-    order.wait(part0)
+    *part1, part0 = pair(full, hops)
     core = [order.send(v, "rep", SWAP[1]) for v in part1]
     return closing(out_flags, part0, core, (top_chip, low_chip), sums, more)
 

time: 117 us -> 116 us (level)
    pallas_call x2 -> x1, Pallas kernels: 7.68 us -> 6.62 us  [pair(): pl.pallas_call(pair_kernel, grid=(4,), in_specs=[ALL] + [pl.BlockSpec((51...]
  transfers between devices with their start and end apart: 29 -> 29, of which waited for: 16 -> 16; matrix products, arithmetic and copies ran while one was open for 0% -> 0% of each run, Pallas kernels for 17% -> 16%
where the time goes in v5:
time: 116 us
  starting transfers between devices  51.4 us (44%)
  waiting for transfers between devices  36.7 us (32%)
  Pallas kernels  23.4 us (20%)
  local copies, waits for them, and re-layouts  4.09 us (4%)
    ppermute x29, starting transfers between devices, send(): return lax.ppermute(value, axes, pairs)  51.4 us
    ppermute x29, waiting for transfers between devices, send(): return lax.ppermute(value, axes, pairs)  36.7 us
    pallas_call x1, Pallas kernels, pair(): pl.pallas_call(pair_kernel, grid=(4,), in_specs=[ALL] + [pl.BlockSpec((51...  6.62 us
    pallas_call x2, Pallas kernels, opening(): pl.pallas_call(opening_kernel, grid_spec=pltpu.PrefetchScalarGridSpec(num...  4.65 us
    unnamed x11, local copies, waits for them, and re-layouts  3.96 us
    pallas_call x1, Pallas kernels, closing(): pl.pallas_call(closing_kernel, grid_spec=pltpu.PrefetchScalarGridSpec(num...  3.74 us
    pallas_call x2, Pallas kernels, middle(): pl.pallas_call(middle_kernel, grid=(2,), in_specs=[pl.BlockSpec((4, 256,...  3.51 us
    pallas_call x2, Pallas kernels, prep(): pl.pallas_call(functools.partial(prep_kernel, first=first), grid_spec=plt...  2.49 us
  transfers between devices with their start and end apart: 29, of which 16 were waited for; matrix products, arithmetic and copies ran while one was open for 0% of the time, Pallas kernels for 16%

profile of v5, /device:TPU:1, one launch (start us, length us, event | category | flops | bytes accessed | tf_op | source)
XLA Modules:
  0.0 116.0 jit_solution(12604276097622446869)
XLA Ops:
  0.0 0.9 copy-done.1
  1.6 0.8 shard_map.55
  2.4 3.9 %collective-permute-start.2 = (bf16[1024,128]{1,0:T(8,128)(2,1)S(1)}, bf16[1024,128]{1,0:T(8,128)(2,1)S(1)}, u32[]{:S(2)}, u32[]{:S(2)}) collective-permute-start(bf16[1024,128]{1,0:T(8,128)(2,1)S(1)} %get-tuple-element.60.own_ref), channel_id=1, source_target_pairs={{0,4},{4,8},{8,12},{12,0},{16,20},{20,24},{24,28},{28,16},{32,36},... | collective-permute-start | bytes 786440 | tf_op jit(solution)/shard_map/ppermute | solution.py:265
  6.3 3.1 %collective-permute-start.3 = (bf16[1024,128]{1,0:T(8,128)(2,1)S(1)}, bf16[1024,128]{1,0:T(8,128)(2,1)S(1)}, u32[]{:S(2)}, u32[]{:S(2)}) collective-permute-start(bf16[1024,128]{1,0:T(8,128)(2,1)S(1)} %get-tuple-element.60.own_ref), channel_id=1, source_target_pairs={{0,12},{4,0},{8,4},{12,8},{16,28},{20,16},{24,20},{28,24},{32,44},... | collective-permute-start | bytes 786440 | tf_op jit(solution)/shard_map/ppermute | solution.py:265
  9.5 1.6 %copy-done = bf16[1,512,2048]{2,1,0:T(8,128)(2,1)S(1)} copy-done((bf16[1,512,2048]{2,1,0:T(8,128)(2,1)S(1)}, bf16[1,512,2048]{2,1,0:T(8,128)(2,1)}, u32[]{:S(2)}) %copy-start) | copy-done | bytes 2097176
  11.1 0.7 copy-done.2
  11.7 1.2 %shard_map.56 = (bf16[512,1024]{1,0:T(8,128)(2,1)S(1)}, f32[2,4,8,128]{3,2,1,0:T(8,128)S(1)}) custom-call(s32[4]{0:T(128)S(1)} %pad_add_fusion.place_ref, s32[4,16]{1,0:T(4,128)S(1)} %bitcast.22, bf16[512,2048]{1,0:T(8,128)(2,1)S(1)} %bitcast.19), custom_call_target="tpu_custom_call" | custom-call | flops 1 | bytes 1 | tf_op jit(solution)/shard_map/pallas_call | solution.py:42
  13.0 2.8 %collective-permute-start.9 = (bf16[512,1024]{1,0:T(8,128)(2,1)S(1)}, bf16[512,1024]{1,0:T(8,128)(2,1)S(1)}, u32[]{:S(2)}, u32[]{:S(2)}) collective-permute-start(bf16[512,1024]{1,0:T(8,128)(2,1)S(1)} %get-tuple-element.75.refs_0_), channel_id=1, source_target_pairs={{0,64},{1,193},{2,66},{3,195},{64,128},{65,1},{66,130},{67,3},{128... | collective-permute-start | bytes 3145736 | tf_op jit(solution)/shard_map/ppermute | solution.py:265
  15.8 1.2 %shard_map.57 = (bf16[512,1024]{1,0:T(8,128)(2,1)S(1)}, f32[2,4,8,128]{3,2,1,0:T(8,128)S(1)}) custom-call(s32[4]{0:T(128)S(1)} %pad_add_fusion.place_ref, s32[4,16]{1,0:T(4,128)S(1)} %bitcast.23, bf16[512,2048]{1,0:T(8,128)(2,1)S(1)} %bitcast.20), custom_call_target="tpu_custom_call" | custom-call | flops 1 | bytes 1 | tf_op jit(solution)/shard_map/pallas_call | solution.py:42
  17.1 1.3 %collective-permute-start = (f32[12,128]{1,0:T(8,128)S(1)}, f32[12,128]{1,0:T(8,128)S(1)}, u32[]{:S(2)}, u32[]{:S(2)}) collective-permute-start(f32[12,128]{1,0:T(8,128)S(1)} %pad_maximum_fusion), channel_id=1, source_target_pairs={{0,16},{4,20},{8,24},{12,28},{16,0},{20,4},{24,8},{28,12},{32,48},... | collective-permute-start | bytes 18440 | tf_op jit(solution)/shard_map/ppermute | solution.py:265
  18.9 1.1 collective-permute-done
  20.0 2.7 %collective-permute-start.1 = (f32[12,128]{1,0:T(8,128)S(1)}, f32[12,128]{1,0:T(8,128)S(1)}, u32[]{:S(2)}, u32[]{:S(2)}) collective-permute-start(f32[12,128]{1,0:T(8,128)S(1)} %fusion.2), channel_id=1, source_target_pairs={{0,32},{4,36},{8,40},{12,44},{16,48},{20,52},{24,56},{28,60},{32,0... | collective-permute-start | bytes 18440 | tf_op jit(solution)/shard_map/ppermute | solution.py:265
  22.8 1.2 %collective-permute-done.1 = f32[12,128]{1,0:T(8,128)S(1)} collective-permute-done((f32[12,128]{1,0:T(8,128)S(1)}, f32[12,128]{1,0:T(8,128)S(1)}, u32[]{:S(2)}, u32[]{:S(2)}) %collective-permute-start.1) | collective-permute-done | bytes 6176 | tf_op jit(solution)/shard_map/ppermute | solution.py:265
  24.0 1.5 %collective-permute-start.5 = (bf16[512,128]{1,0:T(8,128)(2,1)S(1)}, bf16[512,128]{1,0:T(8,128)(2,1)S(1)}, u32[]{:S(2)}, u32[]{:S(2)}) collective-permute-start(bf16[512,128]{1,0:T(8,128)(2,1)S(1)} %slice.54), channel_id=1, source_target_pairs={{0,4},{4,8},{8,12},{12,0},{16,20},{20,24},{24,28},{28,16},{32,36},... | collective-permute-start | bytes 393224 | tf_op jit(solution)/shard_map/ppermute | solution.py:265
  25.5 2.2 %collective-permute-start.6 = (bf16[512,128]{1,0:T(8,128)(2,1)S(1)}, bf16[512,128]{1,0:T(8,128)(2,1)S(1)}, u32[]{:S(2)}, u32[]{:S(2)}) collective-permute-start(bf16[512,128]{1,0:T(8,128)(2,1)S(1)} %slice.55), channel_id=1, source_target_pairs={{0,12},{4,0},{8,4},{12,8},{16,28},{20,16},{24,20},{28,24},{32,44},... | collective-permute-start | bytes 393224 | tf_op jit(solution)/shard_map/ppermute | solution.py:265
  27.7 1.2 %collective-permute-start.4 = (f32[12,128]{1,0:T(8,128)S(1)}, f32[12,128]{1,0:T(8,128)S(1)}, u32[]{:S(2)}, u32[]{:S(2)}) collective-permute-start(f32[12,128]{1,0:T(8,128)S(1)} %add.37), channel_id=1, source_target_pairs={{0,4},{4,0},{8,12},{12,8},{16,20},{20,16},{24,28},{28,24},{32,36},... | collective-permute-start | bytes 18440 | tf_op jit(solution)/shard_map/ppermute | solution.py:265
  28.9 4.9 %collective-permute-done.4 = f32[12,128]{1,0:T(8,128)S(1)} collective-permute-done((f32[12,128]{1,0:T(8,128)S(1)}, f32[12,128]{1,0:T(8,128)S(1)}, u32[]{:S(2)}, u32[]{:S(2)}) %collective-permute-start.4) | collective-permute-done | bytes 6176 | tf_op jit(solution)/shard_map/ppermute | solution.py:265
  34.2 2.1 %collective-permute-start.14 = (bf16[1024,512]{1,0:T(8,128)(2,1)S(1)}, bf16[1024,512]{1,0:T(8,128)(2,1)S(1)}, u32[]{:S(2)}, u32[]{:S(2)}) collective-permute-start(bf16[1024,512]{1,0:T(8,128)(2,1)S(1)} %shard_map.58.own_ref), channel_id=1, source_target_pairs={{0,16},{4,20},{8,24},{12,28},{16,32},{20,36},{24,40},{28,44},{32,4... | collective-permute-start | bytes 3145736 | tf_op jit(solution)/shard_map/ppermute | solution.py:265
  37.0 1.8 %collective-permute-done.7.refs_1_ = bf16[512,1024]{1,0:T(8,128)(2,1)S(1)} collective-permute-done((bf16[512,1024]{1,0:T(8,128)(2,1)S(1)}, bf16[512,1024]{1,0:T(8,128)(2,1)S(1)}, u32[]{:S(2)}, u32[]{:S(2)}) %collective-permute-start.7) | collective-permute-done | bytes 1048608 | tf_op jit(solution)/shard_map/ppermute | solution.py:265
  38.7 4.4 %collective-permute-start.8 = (f32[12,128]{1,0:T(8,128)S(1)}, f32[12,128]{1,0:T(8,128)S(1)}, u32[]{:S(2)}, u32[]{:S(2)}) collective-permute-start(f32[12,128]{1,0:T(8,128)S(1)} %add.38), channel_id=1, source_target_pairs={{0,8},{4,12},{8,0},{12,4},{16,24},{20,28},{24,16},{28,20},{32,40},... | collective-permute-start | bytes 18440 | tf_op jit(solution)/shard_map/ppermute | solution.py:265
  43.1 2.0 %collective-permute-done.8 = f32[12,128]{1,0:T(8,128)S(1)} collective-permute-done((f32[12,128]{1,0:T(8,128)S(1)}, f32[12,128]{1,0:T(8,128)S(1)}, u32[]{:S(2)}, u32[]{:S(2)}) %collective-permute-start.8) | collective-permute-done | bytes 6176 | tf_op jit(solution)/shard_map/ppermute | solution.py:265
  45.2 4.8 %collective-permute-done.10.refs_2_ = bf16[512,1024]{1,0:T(8,128)(2,1)S(1)} collective-permute-done((bf16[512,1024]{1,0:T(8,128)(2,1)S(1)}, bf16[512,1024]{1,0:T(8,128)(2,1)S(1)}, u32[]{:S(2)}, u32[]{:S(2)}) %collective-permute-start.10) | collective-permute-done | bytes 1048608 | tf_op jit(solution)/shard_map/ppermute | solution.py:265
  50.0 0.8 collective-permute-start.13
  50.7 3.8 %collective-permute-start.12 = (f32[4,128]{1,0:T(4,128)S(1)}, f32[4,128]{1,0:T(4,128)S(1)}, u32[]{:S(2)}, u32[]{:S(2)}) collective-permute-start(f32[4,128]{1,0:T(4,128)S(1)} %fusion.1), channel_id=1, source_target_pairs={{0,128},{1,129},{2,130},{3,131},{64,192},{65,193},{66,194},{67,195... | collective-permute-start | bytes 6152 | tf_op jit(solution)/shard_map/ppermute | solution.py:265
  54.7 0.9 collective-permute-done.12
  55.6 1.7 %collective-permute-done.11 = f32[4,128]{1,0:T(4,128)S(1)} collective-permute-done((f32[4,128]{1,0:T(4,128)S(1)}, f32[4,128]{1,0:T(4,128)S(1)}, u32[]{:S(2)}, u32[]{:S(2)}) %collective-permute-start.11) | collective-permute-done | bytes 2080 | tf_op jit(solution)/shard_map/ppermute | solution.py:265
  57.3 1.2 %collective-permute-start.19 = (bf16[512,1024]{1,0:T(8,128)(2,1)S(1)}, bf16[512,1024]{1,0:T(8,128)(2,1)S(1)}, u32[]{:S(2)}, u32[]{:S(2)}) collective-permute-start(bf16[512,1024]{1,0:T(8,128)(2,1)S(1)} %collective-permute-done.10.refs_2_), channel_id=1, source_target_pairs={{0,64},{1,193},{2,66},{3,195},{64,128},{65,1},{66,130},{67,3},{128... | collective-permute-start | bytes 3145736 | tf_op jit(solution)/shard_map/ppermute | solution.py:265
  58.6 0.8 collective-permute-start.16
  59.5 4.0 %collective-permute-start.17 = (f32[8,128]{1,0:T(8,128)S(1)}, f32[8,128]{1,0:T(8,128)S(1)}, u32[]{:S(2)}, u32[]{:S(2)}) collective-permute-start(f32[8,128]{1,0:T(8,128)S(1)} %slice.58), channel_id=1, source_target_pairs={{0,1},{1,0},{2,3},{3,2},{4,5},{5,4},{6,7},{7,6},{8,9},{9,8},{10,11... | collective-permute-start | bytes 12296 | tf_op jit(solution)/shard_map/ppermute | solution.py:265
  63.5 1.5 %collective-permute-start.20 = (bf16[512,512]{1,0:T(8,128)(2,1)S(1)}, bf16[512,512]{1,0:T(8,128)(2,1)S(1)}, u32[]{:S(2)}, u32[]{:S(2)}) collective-permute-start(bf16[512,512]{1,0:T(8,128)(2,1)S(1)} %slice.59), channel_id=1, source_target_pairs={{0,48},{4,52},{8,56},{12,60},{16,0},{20,4},{24,8},{28,12},{32,16},... | collective-permute-start | bytes 1572872 | tf_op jit(solution)/shard_map/ppermute | solution.py:265
  64.9 0.8 collective-permute-start.21
  65.8 0.8 collective-permute-start.18
  66.6 1.4 %shard_map.59.full_ref = bf16[4,1024,512]{2,1,0:T(8,128)(2,1)S(1)} custom-call(s32[4]{0:T(128)S(1)} %pad_add_fusion.place_ref, f32[4,4,128]{2,1,0:T(4,128)S(1)} %pad_maximum_fusion.1.scale_ref, bf16[1024,512]{1,0:T(8,128)(2,1)S(1)} %shard_map.58.own_ref, bf16[1024,512]{1,0:T(8,128)(2,1)S(1)} %collective-permute-done.14.r_ref, ...), custom_call_target="tpu_custom_call" | custom-call | flops 1 | bytes 1 | tf_op jit(solution)/shard_map/pallas_call | solution.py:126
  68.6 1.4 %collective-permute-done.16.piece_ref = bf16[512,512]{1,0:T(8,128)(2,1)S(1)} collective-permute-done((bf16[512,512]{1,0:T(8,128)(2,1)S(1)}, bf16[512,512]{1,0:T(8,128)(2,1)S(1)}, u32[]{:S(2)}, u32[]{:S(2)}) %collective-permute-start.16) | collective-permute-done | bytes 524320 | tf_op jit(solution)/shard_map/ppermute | solution.py:265
  70.0 1.2 %collective-permute-done.19.refs_3_ = bf16[512,1024]{1,0:T(8,128)(2,1)S(1)} collective-permute-done((bf16[512,1024]{1,0:T(8,128)(2,1)S(1)}, bf16[512,1024]{1,0:T(8,128)(2,1)S(1)}, u32[]{:S(2)}, u32[]{:S(2)}) %collective-permute-start.19) | collective-permute-done | bytes 1048608 | tf_op jit(solution)/shard_map/ppermute | solution.py:265
  71.3 2.3 %shard_map.60 = (bf16[4,1024,512]{2,1,0:T(8,128)(2,1)S(1)}, bf16[512,512]{1,0:T(8,128)(2,1)S(1)}) custom-call(s32[4]{0:T(128)S(1)} %pad_add_fusion.place_ref, f32[4,4,128]{2,1,0:T(4,128)S(1)} %pad_maximum_fusion.1.scale_ref, bf16[4,1024,512]{2,1,0:T(8,128)(2,1)S(1)} %shard_map.59.full_ref, ...), custom_call_target="tpu_custom_call", output_to_operand_aliasing={{0}: (2, {})} | custom-call | flops 1 | bytes 1 | tf_op jit(solution)/shard_map/pallas_call | solution.py:161
  73.6 4.5 %collective-permute-start.22 = (bf16[512,512]{1,0:T(8,128)(2,1)S(1)}, bf16[512,512]{1,0:T(8,128)(2,1)S(1)}, u32[]{:S(2)}, u32[]{:S(2)}) collective-permute-start(bf16[512,512]{1,0:T(8,128)(2,1)S(1)} %get-tuple-element.73), channel_id=1, source_target_pairs={{0,1},{1,0},{2,3},{3,2},{4,5},{5,4},{6,7},{7,6},{8,9},{9,8},{10,11... | collective-permute-start | bytes 1572872 | tf_op jit(solution)/shard_map/ppermute | solution.py:265
  78.1 2.3 %shard_map.61 = (bf16[4,1024,512]{2,1,0:T(8,128)(2,1)S(1)}, bf16[512,512]{1,0:T(8,128)(2,1)S(1)}) custom-call(s32[4]{0:T(128)S(1)} %pad_add_fusion.place_ref, f32[4,4,128]{2,1,0:T(4,128)S(1)} %pad_maximum_fusion.1.scale_ref, bf16[4,1024,512]{2,1,0:T(8,128)(2,1)S(1)} %get-tuple-element.67.full_ref, ...), custom_call_target="tpu_custom_call", output_to_operand_aliasing={{0}: (2, {})} | custom-call | flops 1 | bytes 1 | tf_op jit(solution)/shard_map/pallas_call | solution.py:161
  80.6 1.8 %shard_map.62 = bf16[512,512]{1,0:T(8,128)(2,1)S(1)} custom-call(bf16[4,1024,512]{2,1,0:T(8,128)(2,1)S(1)} %get-tuple-element.69.full_ref, bf16[512,512]{1,0:T(8,128)(2,1)S(1)} %collective-permute-done.22.core_ref, bf16[512,1024]{1,0:T(8,128)(2,1)S(1)} %get-tuple-element.75.refs_0_, bf16[512,1024]{1,0:T(8,128)(2,1)S(1)} %collective-permute-done.9.refs_1_, ...), custom_call_target="tpu_custom_call" | custom-call | flops 1 | bytes 1 | tf_op jit(solution)/shard_map/pallas_call | solution.py:187
  82.5 1.7 %shard_map.63 = bf16[512,512]{1,0:T(8,128)(2,1)S(1)} custom-call(bf16[4,1024,512]{2,1,0:T(8,128)(2,1)S(1)} %get-tuple-element.69.full_ref, bf16[512,512]{1,0:T(8,128)(2,1)S(1)} %collective-permute-done.23.core_ref, bf16[512,1024]{1,0:T(8,128)(2,1)S(1)} %get-tuple-element.75.refs_0_, bf16[512,1024]{1,0:T(8,128)(2,1)S(1)} %collective-permute-done.9.refs_1_, ...), custom_call_target="tpu_custom_call" | custom-call | flops 1 | bytes 1 | tf_op jit(solution)/shard_map/pallas_call | solution.py:187
  84.7 0.7 collective-permute-start.27
  85.5 0.7 collective-permute-start.28
  86.2 12.2 %collective-permute-done.24.refs_3_ = bf16[512,1024]{1,0:T(8,128)(2,1)S(1)} collective-permute-done((bf16[512,1024]{1,0:T(8,128)(2,1)S(1)}, bf16[512,1024]{1,0:T(8,128)(2,1)S(1)}, u32[]{:S(2)}, u32[]{:S(2)}) %collective-permute-start.24) | collective-permute-done | bytes 1048608 | tf_op jit(solution)/shard_map/ppermute | solution.py:265
  98.4 6.6 %shard_map.64 = (bf16[512,512]{1,0:T(8,128)(2,1)}, bf16[512,512]{1,0:T(8,128)(2,1)}, f32[1024,512]{1,0:T(8,128)S(1)}) custom-call(bf16[4,1024,512]{2,1,0:T(8,128)(2,1)S(1)} %get-tuple-element.69.full_ref, bf16[512,1024]{1,0:T(8,128)(2,1)S(1)} %get-tuple-element.55.refs_0_, bf16[512,1024]{1,0:T(8,128)(2,1)S(1)} %collective-permute-done.7.refs_1_, ...), custom_call_target="tpu_custom_call" | custom-call | flops 1 | bytes 1 | tf_op jit(solution)/shard_map/pallas_call | solution.py:211
  105.0 4.6 %collective-permute-start.25 = (bf16[512,512]{1,0:T(8,128)(2,1)}, bf16[512,512]{1,0:T(8,128)(2,1)}, u32[]{:S(2)}, u32[]{:S(2)}) collective-permute-start(bf16[512,512]{1,0:T(8,128)(2,1)} %get-tuple-element.80), channel_id=1, source_target_pairs={{0,1},{1,0},{2,3},{3,2},{4,5},{5,4},{6,7},{7,6},{8,9},{9,8},{10,11... | collective-permute-start | bytes 1572872 | tf_op jit(solution)/shard_map/ppermute | solution.py:265
  109.7 1.8 %collective-permute-done.25.core0_ref = bf16[512,512]{1,0:T(8,128)(2,1)} collective-permute-done((bf16[512,512]{1,0:T(8,128)(2,1)}, bf16[512,512]{1,0:T(8,128)(2,1)}, u32[]{:S(2)}, u32[]{:S(2)}) %collective-permute-start.25) | collective-permute-done | bytes 524320 | tf_op jit(solution)/shard_map/ppermute | solution.py:265
  111.5 0.7 collective-permute-done.26.core1_ref
  112.2 3.7 %shard_map.65 = bf16[1024,512]{1,0:T(8,128)(2,1)} custom-call(s32[8,4]{1,0:T(8,128)S(1)} %copy.13.flags_ref, f32[1024,512]{1,0:T(8,128)S(1)} %get-tuple-element.78.part_ref, bf16[512,512]{1,0:T(8,128)(2,1)} %collective-permute-done.25.core0_ref, bf16[512,512]{1,0:T(8,128)(2,1)} %collective-permute-done.26.core1_ref, ...), custom_call_target="tpu_custom_call" | custom-call | flops 1 | bytes 1 | tf_op jit(solution)/shard_map/pallas_call | solution.py:243
  (53 shorter events, 3.9 us)
Async XLA Ops:
  0.0 0.9 copy-start.1
  1.0 0.7 copy-start.3
  2.4 20.4 %collective-permute-start.2 = (bf16[1024,128]{1,0:T(8,128)(2,1)S(1)}, bf16[1024,128]{1,0:T(8,128)(2,1)S(1)}, u32[]{:S(2)}, u32[]{:S(2)}) collective-permute-start(bf16[1024,128]{1,0:T(8,128)(2,1)S(1)} %get-tuple-element.60.own_ref), channel_id=1, source_target_pairs={{0,4},{4,8},{8,12},{12,0},{16,20},{20,24},{24,28},{28,16},{32,36},... | collective-permute-start | bytes 786440 | tf_op jit(solution)/shard_map/ppermute | solution.py:265
  6.3 17.8 %collective-permute-start.3 = (bf16[1024,128]{1,0:T(8,128)(2,1)S(1)}, bf16[1024,128]{1,0:T(8,128)(2,1)S(1)}, u32[]{:S(2)}, u32[]{:S(2)}) collective-permute-start(bf16[1024,128]{1,0:T(8,128)(2,1)S(1)} %get-tuple-element.60.own_ref), channel_id=1, source_target_pairs={{0,12},{4,0},{8,4},{12,8},{16,28},{20,16},{24,20},{28,24},{32,44},... | collective-permute-start | bytes 786440 | tf_op jit(solution)/shard_map/ppermute | solution.py:265
  9.5 1.6 %copy-start = (bf16[1,512,2048]{2,1,0:T(8,128)(2,1)S(1)}, bf16[1,512,2048]{2,1,0:T(8,128)(2,1)}, u32[]{:S(2)}) copy-start(bf16[1,512,2048]{2,1,0:T(8,128)(2,1)} %param.7) | copy-start | bytes 6291460
  11.1 0.7 copy-start.2
  13.0 20.8 %collective-permute-start.9 = (bf16[512,1024]{1,0:T(8,128)(2,1)S(1)}, bf16[512,1024]{1,0:T(8,128)(2,1)S(1)}, u32[]{:S(2)}, u32[]{:S(2)}) collective-permute-start(bf16[512,1024]{1,0:T(8,128)(2,1)S(1)} %get-tuple-element.75.refs_0_), channel_id=1, source_target_pairs={{0,64},{1,193},{2,66},{3,195},{64,128},{65,1},{66,130},{67,3},{128... | collective-permute-start | bytes 3145736 | tf_op jit(solution)/shard_map/ppermute | solution.py:265
  17.1 2.9 %collective-permute-start = (f32[12,128]{1,0:T(8,128)S(1)}, f32[12,128]{1,0:T(8,128)S(1)}, u32[]{:S(2)}, u32[]{:S(2)}) collective-permute-start(f32[12,128]{1,0:T(8,128)S(1)} %pad_maximum_fusion), channel_id=1, source_target_pairs={{0,16},{4,20},{8,24},{12,28},{16,0},{20,4},{24,8},{28,12},{32,48},... | collective-permute-start | bytes 18440 | tf_op jit(solution)/shard_map/ppermute | solution.py:265
  18.4 20.3 %collective-permute-start.7 = (bf16[512,1024]{1,0:T(8,128)(2,1)S(1)}, bf16[512,1024]{1,0:T(8,128)(2,1)S(1)}, u32[]{:S(2)}, u32[]{:S(2)}) collective-permute-start(bf16[512,1024]{1,0:T(8,128)(2,1)S(1)} %get-tuple-element.55.refs_0_), channel_id=1, source_target_pairs={{0,64},{1,193},{2,66},{3,195},{64,128},{65,1},{66,130},{67,3},{128... | collective-permute-start | bytes 3145736 | tf_op jit(solution)/shard_map/ppermute | solution.py:265
  20.0 4.0 %collective-permute-start.1 = (f32[12,128]{1,0:T(8,128)S(1)}, f32[12,128]{1,0:T(8,128)S(1)}, u32[]{:S(2)}, u32[]{:S(2)}) collective-permute-start(f32[12,128]{1,0:T(8,128)S(1)} %fusion.2), channel_id=1, source_target_pairs={{0,32},{4,36},{8,40},{12,44},{16,48},{20,52},{24,56},{28,60},{32,0... | collective-permute-start | bytes 18440 | tf_op jit(solution)/shard_map/ppermute | solution.py:265
  24.0 9.8 %collective-permute-start.5 = (bf16[512,128]{1,0:T(8,128)(2,1)S(1)}, bf16[512,128]{1,0:T(8,128)(2,1)S(1)}, u32[]{:S(2)}, u32[]{:S(2)}) collective-permute-start(bf16[512,128]{1,0:T(8,128)(2,1)S(1)} %slice.54), channel_id=1, source_target_pairs={{0,4},{4,8},{8,12},{12,0},{16,20},{20,24},{24,28},{28,16},{32,36},... | collective-permute-start | bytes 393224 | tf_op jit(solution)/shard_map/ppermute | solution.py:265
  25.5 8.3 %collective-permute-start.6 = (bf16[512,128]{1,0:T(8,128)(2,1)S(1)}, bf16[512,128]{1,0:T(8,128)(2,1)S(1)}, u32[]{:S(2)}, u32[]{:S(2)}) collective-permute-start(bf16[512,128]{1,0:T(8,128)(2,1)S(1)} %slice.55), channel_id=1, source_target_pairs={{0,12},{4,0},{8,4},{12,8},{16,28},{20,16},{24,20},{28,24},{32,44},... | collective-permute-start | bytes 393224 | tf_op jit(solution)/shard_map/ppermute | solution.py:265
  27.7 6.1 %collective-permute-start.4 = (f32[12,128]{1,0:T(8,128)S(1)}, f32[12,128]{1,0:T(8,128)S(1)}, u32[]{:S(2)}, u32[]{:S(2)}) collective-permute-start(f32[12,128]{1,0:T(8,128)S(1)} %add.37), channel_id=1, source_target_pairs={{0,4},{4,0},{8,12},{12,8},{16,20},{20,16},{24,28},{28,24},{32,36},... | collective-permute-start | bytes 18440 | tf_op jit(solution)/shard_map/ppermute | solution.py:265
  33.8 16.2 %collective-permute-start.10 = (bf16[512,1024]{1,0:T(8,128)(2,1)S(1)}, bf16[512,1024]{1,0:T(8,128)(2,1)S(1)}, u32[]{:S(2)}, u32[]{:S(2)}) collective-permute-start(bf16[512,1024]{1,0:T(8,128)(2,1)S(1)} %collective-permute-done.9.refs_1_), channel_id=1, source_target_pairs={{0,64},{1,193},{2,66},{3,195},{64,128},{65,1},{66,130},{67,3},{128... | collective-permute-start | bytes 3145736 | tf_op jit(solution)/shard_map/ppermute | solution.py:265
  34.2 24.3 %collective-permute-start.14 = (bf16[1024,512]{1,0:T(8,128)(2,1)S(1)}, bf16[1024,512]{1,0:T(8,128)(2,1)S(1)}, u32[]{:S(2)}, u32[]{:S(2)}) collective-permute-start(bf16[1024,512]{1,0:T(8,128)(2,1)S(1)} %shard_map.58.own_ref), channel_id=1, source_target_pairs={{0,16},{4,20},{8,24},{12,28},{16,32},{20,36},{24,40},{28,44},{32,4... | collective-permute-start | bytes 3145736 | tf_op jit(solution)/shard_map/ppermute | solution.py:265
  36.3 22.3 %collective-permute-start.15 = (bf16[1024,512]{1,0:T(8,128)(2,1)S(1)}, bf16[1024,512]{1,0:T(8,128)(2,1)S(1)}, u32[]{:S(2)}, u32[]{:S(2)}) collective-permute-start(bf16[1024,512]{1,0:T(8,128)(2,1)S(1)} %shard_map.58.own_ref), channel_id=1, source_target_pairs={{0,48},{4,52},{8,56},{12,60},{16,0},{20,4},{24,8},{28,12},{32,16},... | collective-permute-start | bytes 3145736 | tf_op jit(solution)/shard_map/ppermute | solution.py:265
  38.7 6.4 %collective-permute-start.8 = (f32[12,128]{1,0:T(8,128)S(1)}, f32[12,128]{1,0:T(8,128)S(1)}, u32[]{:S(2)}, u32[]{:S(2)}) collective-permute-start(f32[12,128]{1,0:T(8,128)S(1)} %add.38), channel_id=1, source_target_pairs={{0,8},{4,12},{8,0},{12,4},{16,24},{20,28},{24,16},{28,20},{32,40},... | collective-permute-start | bytes 18440 | tf_op jit(solution)/shard_map/ppermute | solution.py:265
  50.0 4.7 %collective-permute-start.13 = (f32[4,128]{1,0:T(4,128)S(1)}, f32[4,128]{1,0:T(4,128)S(1)}, u32[]{:S(2)}, u32[]{:S(2)}) collective-permute-start(f32[4,128]{1,0:T(4,128)S(1)} %fusion.1), channel_id=1, source_target_pairs={{0,192},{1,65},{2,194},{3,67},{64,0},{65,129},{66,2},{67,131},{128... | collective-permute-start | bytes 6152 | tf_op jit(solution)/shard_map/ppermute | solution.py:265
  50.7 4.8 %collective-permute-start.12 = (f32[4,128]{1,0:T(4,128)S(1)}, f32[4,128]{1,0:T(4,128)S(1)}, u32[]{:S(2)}, u32[]{:S(2)}) collective-permute-start(f32[4,128]{1,0:T(4,128)S(1)} %fusion.1), channel_id=1, source_target_pairs={{0,128},{1,129},{2,130},{3,131},{64,192},{65,193},{66,194},{67,195... | collective-permute-start | bytes 6152 | tf_op jit(solution)/shard_map/ppermute | solution.py:265
  54.6 2.7 %collective-permute-start.11 = (f32[4,128]{1,0:T(4,128)S(1)}, f32[4,128]{1,0:T(4,128)S(1)}, u32[]{:S(2)}, u32[]{:S(2)}) collective-permute-start(f32[4,128]{1,0:T(4,128)S(1)} %fusion.1), channel_id=1, source_target_pairs={{0,64},{1,193},{2,66},{3,195},{64,128},{65,1},{66,130},{67,3},{128... | collective-permute-start | bytes 6152 | tf_op jit(solution)/shard_map/ppermute | solution.py:265
  57.3 13.9 %collective-permute-start.19 = (bf16[512,1024]{1,0:T(8,128)(2,1)S(1)}, bf16[512,1024]{1,0:T(8,128)(2,1)S(1)}, u32[]{:S(2)}, u32[]{:S(2)}) collective-permute-start(bf16[512,1024]{1,0:T(8,128)(2,1)S(1)} %collective-permute-done.10.refs_2_), channel_id=1, source_target_pairs={{0,64},{1,193},{2,66},{3,195},{64,128},{65,1},{66,130},{67,3},{128... | collective-permute-start | bytes 3145736 | tf_op jit(solution)/shard_map/ppermute | solution.py:265
  58.6 11.4 %collective-permute-start.16 = (bf16[512,512]{1,0:T(8,128)(2,1)S(1)}, bf16[512,512]{1,0:T(8,128)(2,1)S(1)}, u32[]{:S(2)}, u32[]{:S(2)}) collective-permute-start(bf16[512,512]{1,0:T(8,128)(2,1)S(1)} %slice.57), channel_id=1, source_target_pairs={{0,16},{4,20},{8,24},{12,28},{16,32},{20,36},{24,40},{28,44},{32,4... | collective-permute-start | bytes 1572872 | tf_op jit(solution)/shard_map/ppermute | solution.py:265
  59.5 6.3 %collective-permute-start.17 = (f32[8,128]{1,0:T(8,128)S(1)}, f32[8,128]{1,0:T(8,128)S(1)}, u32[]{:S(2)}, u32[]{:S(2)}) collective-permute-start(f32[8,128]{1,0:T(8,128)S(1)} %slice.58), channel_id=1, source_target_pairs={{0,1},{1,0},{2,3},{3,2},{4,5},{5,4},{6,7},{7,6},{8,9},{9,8},{10,11... | collective-permute-start | bytes 12296 | tf_op jit(solution)/shard_map/ppermute | solution.py:265
  63.5 14.7 %collective-permute-start.20 = (bf16[512,512]{1,0:T(8,128)(2,1)S(1)}, bf16[512,512]{1,0:T(8,128)(2,1)S(1)}, u32[]{:S(2)}, u32[]{:S(2)}) collective-permute-start(bf16[512,512]{1,0:T(8,128)(2,1)S(1)} %slice.59), channel_id=1, source_target_pairs={{0,48},{4,52},{8,56},{12,60},{16,0},{20,4},{24,8},{28,12},{32,16},... | collective-permute-start | bytes 1572872 | tf_op jit(solution)/shard_map/ppermute | solution.py:265
  64.9 19.3 %collective-permute-start.21 = (bf16[512,1024]{1,0:T(8,128)(2,1)S(1)}, bf16[512,1024]{1,0:T(8,128)(2,1)S(1)}, u32[]{:S(2)}, u32[]{:S(2)}) collective-permute-start(bf16[512,1024]{1,0:T(8,128)(2,1)S(1)} %collective-permute-done.7.refs_1_), channel_id=1, source_target_pairs={{0,64},{1,193},{2,66},{3,195},{64,128},{65,1},{66,130},{67,3},{128... | collective-permute-start | bytes 3145736 | tf_op jit(solution)/shard_map/ppermute | solution.py:265
  65.8 2.8 %collective-permute-start.18 = (f32[8,128]{1,0:T(8,128)S(1)}, f32[8,128]{1,0:T(8,128)S(1)}, u32[]{:S(2)}, u32[]{:S(2)}) collective-permute-start(f32[8,128]{1,0:T(8,128)S(1)} %slice_add_fusion.4.sum_ref), channel_id=1, source_target_pairs={{0,2},{1,3},{2,0},{3,1},{4,6},{5,7},{6,4},{7,5},{8,10},{9,11},{10,... | collective-permute-start | bytes 12296 | tf_op jit(solution)/shard_map/ppermute | solution.py:265
  73.6 7.0 %collective-permute-start.22 = (bf16[512,512]{1,0:T(8,128)(2,1)S(1)}, bf16[512,512]{1,0:T(8,128)(2,1)S(1)}, u32[]{:S(2)}, u32[]{:S(2)}) collective-permute-start(bf16[512,512]{1,0:T(8,128)(2,1)S(1)} %get-tuple-element.73), channel_id=1, source_target_pairs={{0,1},{1,0},{2,3},{3,2},{4,5},{5,4},{6,7},{7,6},{8,9},{9,8},{10,11... | collective-permute-start | bytes 1572872 | tf_op jit(solution)/shard_map/ppermute | solution.py:265
  80.5 2.0 %collective-permute-start.23 = (bf16[512,512]{1,0:T(8,128)(2,1)S(1)}, bf16[512,512]{1,0:T(8,128)(2,1)S(1)}, u32[]{:S(2)}, u32[]{:S(2)}) collective-permute-start(bf16[512,512]{1,0:T(8,128)(2,1)S(1)} %get-tuple-element.74), channel_id=1, source_target_pairs={{0,1},{1,0},{2,3},{3,2},{4,5},{5,4},{6,7},{7,6},{8,9},{9,8},{10,11... | collective-permute-start | bytes 1572872 | tf_op jit(solution)/shard_map/ppermute | solution.py:265
  84.2 25.4 %copy-start.4 = (s32[8,4]{0,1:T(4,128)S(1)}, s32[8,4]{0,1:T(4,128)}, u32[]{:S(2)}) copy-start(s32[8,4]{0,1:T(4,128)} %param.9) | copy-start | bytes 388
  84.2 14.1 %collective-permute-start.24 = (bf16[512,1024]{1,0:T(8,128)(2,1)S(1)}, bf16[512,1024]{1,0:T(8,128)(2,1)S(1)}, u32[]{:S(2)}, u32[]{:S(2)}) collective-permute-start(bf16[512,1024]{1,0:T(8,128)(2,1)S(1)} %collective-permute-done.21.refs_2_), channel_id=1, source_target_pairs={{0,64},{1,193},{2,66},{3,195},{64,128},{65,1},{66,130},{67,3},{128... | collective-permute-start | bytes 3145736 | tf_op jit(solution)/shard_map/ppermute | solution.py:265
  84.7 24.9 %collective-permute-start.27 = (bf16[512,512]{1,0:T(8,128)(2,1)S(1)}, bf16[512,512]{1,0:T(8,128)(2,1)}, u32[]{:S(2)}, u32[]{:S(2)}) collective-permute-start(bf16[512,512]{1,0:T(8,128)(2,1)S(1)} %shard_map.62), channel_id=1, source_target_pairs={{0,2},{1,3},{2,0},{3,1},{4,6},{5,7},{6,4},{7,5},{8,10},{9,11},{10,... | collective-permute-start | bytes 1572872 | tf_op jit(solution)/shard_map/ppermute | solution.py:265
  85.5 24.2 %collective-permute-start.28 = (bf16[512,512]{1,0:T(8,128)(2,1)S(1)}, bf16[512,512]{1,0:T(8,128)(2,1)}, u32[]{:S(2)}, u32[]{:S(2)}) collective-permute-start(bf16[512,512]{1,0:T(8,128)(2,1)S(1)} %shard_map.63), channel_id=1, source_target_pairs={{0,2},{1,3},{2,0},{3,1},{4,6},{5,7},{6,4},{7,5},{8,10},{9,11},{10,... | collective-permute-start | bytes 1572872 | tf_op jit(solution)/shard_map/ppermute | solution.py:265
  105.0 6.5 %collective-permute-start.25 = (bf16[512,512]{1,0:T(8,128)(2,1)}, bf16[512,512]{1,0:T(8,128)(2,1)}, u32[]{:S(2)}, u32[]{:S(2)}) collective-permute-start(bf16[512,512]{1,0:T(8,128)(2,1)} %get-tuple-element.80), channel_id=1, source_target_pairs={{0,1},{1,0},{2,3},{3,2},{4,5},{5,4},{6,7},{7,6},{8,9},{9,8},{10,11... | collective-permute-start | bytes 1572872 | tf_op jit(solution)/shard_map/ppermute | solution.py:265
  109.6 2.6 %collective-permute-start.26 = (bf16[512,512]{1,0:T(8,128)(2,1)}, bf16[512,512]{1,0:T(8,128)(2,1)}, u32[]{:S(2)}, u32[]{:S(2)}) collective-permute-start(bf16[512,512]{1,0:T(8,128)(2,1)} %get-tuple-element.82), channel_id=1, source_target_pairs={{0,1},{1,0},{2,3},{3,2},{4,5},{5,4},{6,7},{7,6},{8,9},{9,8},{10,11... | collective-permute-start | bytes 1572872 | tf_op jit(solution)/shard_map/ppermute | solution.py:265

commit v6 on v5

--- a/solution.py
+++ b/solution.py
@@ -204,7 +204,7 @@
         def _():
             ref[...] = swapped
 
-    part_ref[...] = multiply(full_ref, [hop[:, 512:] for hop in hops])
+    part_ref[...] = multiply(full_ref, [hop[:, 512:] for hop in hops]).astype(BF16)
 
 
 def pair(full, hops):
@@ -213,7 +213,7 @@
         grid=(4,),
         in_specs=[ALL] + [pl.BlockSpec((512, 1024), lambda i: (0, 0))] * 4,
         out_specs=[UPPER, LOWER, ROWS],
-        out_shape=[jax.ShapeDtypeStruct((512, 512), BF16)] * 2 + [jax.ShapeDtypeStruct((1024, 512), F32)],
+        out_shape=[jax.ShapeDtypeStruct((512, 512), BF16)] * 2 + [jax.ShapeDtypeStruct((1024, 512), BF16)],
         compiler_params=pltpu.CompilerParams(vmem_limit_bytes=20 << 20),
         cost_estimate=TINY,
     )(full, *hops)
@@ -225,7 +225,7 @@
     chip = jnp.where(step == 0, chip0_ref[...], chip1_ref[...])
     for block in range(4):
         rows = slice(TILE * block, TILE * (block + 1))
-        total = part_ref[rows, :] + core[rows, :].astype(F32)
+        total = part_ref[rows, :].astype(F32) + core[rows, :].astype(F32)
         total += chip[rows, :].astype(F32)
         line = pl.ds(4 * step + block, 1)
         scale = jnp.float32(TILE * 256) / (1.0 + sum_ref[line, :] + more_ref[line, :])

time: 116 us -> 116 us (level)
  no operation moved by 1% of the time
where the time goes in v6:
time: 116 us
  starting transfers between devices  51.5 us (44%)
  waiting for transfers between devices  36.6 us (32%)
  Pallas kernels  23.2 us (20%)
  local copies, waits for them, and re-layouts  4.09 us (4%)
    ppermute x29, starting transfers between devices, send(): return lax.ppermute(value, axes, pairs)  51.5 us
    ppermute x29, waiting for transfers between devices, send(): return lax.ppermute(value, axes, pairs)  36.6 us
    pallas_call x1, Pallas kernels, pair(): pl.pallas_call(pair_kernel, grid=(4,), in_specs=[ALL] + [pl.BlockSpec((51...  6.71 us
    pallas_call x2, Pallas kernels, opening(): pl.pallas_call(opening_kernel, grid_spec=pltpu.PrefetchScalarGridSpec(num...  4.65 us
    unnamed x11, local copies, waits for them, and re-layouts  3.96 us
    pallas_call x2, Pallas kernels, middle(): pl.pallas_call(middle_kernel, grid=(2,), in_specs=[pl.BlockSpec((4, 256,...  3.51 us
    pallas_call x1, Pallas kernels, closing(): pl.pallas_call(closing_kernel, grid_spec=pltpu.PrefetchScalarGridSpec(num...  3.48 us
    pallas_call x2, Pallas kernels, prep(): pl.pallas_call(functools.partial(prep_kernel, first=first), grid_spec=plt...  2.49 us
  transfers between devices with their start and end apart: 29, of which 16 were waited for; matrix products, arithmetic and copies ran while one was open for 0% of the time, Pallas kernels for 16%

profile of v6, /device:TPU:1, one launch (start us, length us, event | category | flops | bytes accessed | tf_op | source)
XLA Modules:
  0.0 115.8 jit_solution(3698491344721236626)
XLA Ops:
  0.0 0.9 copy-done.1
  1.6 0.8 shard_map.55
  2.4 3.9 %collective-permute-start.2 = (bf16[1024,128]{1,0:T(8,128)(2,1)S(1)}, bf16[1024,128]{1,0:T(8,128)(2,1)S(1)}, u32[]{:S(2)}, u32[]{:S(2)}) collective-permute-start(bf16[1024,128]{1,0:T(8,128)(2,1)S(1)} %get-tuple-element.60.own_ref), channel_id=1, source_target_pairs={{0,4},{4,8},{8,12},{12,0},{16,20},{20,24},{24,28},{28,16},{32,36},... | collective-permute-start | bytes 786440 | tf_op jit(solution)/shard_map/ppermute | solution.py:265
  6.3 3.1 %collective-permute-start.3 = (bf16[1024,128]{1,0:T(8,128)(2,1)S(1)}, bf16[1024,128]{1,0:T(8,128)(2,1)S(1)}, u32[]{:S(2)}, u32[]{:S(2)}) collective-permute-start(bf16[1024,128]{1,0:T(8,128)(2,1)S(1)} %get-tuple-element.60.own_ref), channel_id=1, source_target_pairs={{0,12},{4,0},{8,4},{12,8},{16,28},{20,16},{24,20},{28,24},{32,44},... | collective-permute-start | bytes 786440 | tf_op jit(solution)/shard_map/ppermute | solution.py:265
  9.5 1.6 %copy-done = bf16[1,512,2048]{2,1,0:T(8,128)(2,1)S(1)} copy-done((bf16[1,512,2048]{2,1,0:T(8,128)(2,1)S(1)}, bf16[1,512,2048]{2,1,0:T(8,128)(2,1)}, u32[]{:S(2)}) %copy-start) | copy-done | bytes 2097176
  11.1 0.7 copy-done.2
  11.7 1.2 %shard_map.56 = (bf16[512,1024]{1,0:T(8,128)(2,1)S(1)}, f32[2,4,8,128]{3,2,1,0:T(8,128)S(1)}) custom-call(s32[4]{0:T(128)S(1)} %pad_add_fusion.place_ref, s32[4,16]{1,0:T(4,128)S(1)} %bitcast.22, bf16[512,2048]{1,0:T(8,128)(2,1)S(1)} %bitcast.19), custom_call_target="tpu_custom_call" | custom-call | flops 1 | bytes 1 | tf_op jit(solution)/shard_map/pallas_call | solution.py:42
  13.0 2.8 %collective-permute-start.9 = (bf16[512,1024]{1,0:T(8,128)(2,1)S(1)}, bf16[512,1024]{1,0:T(8,128)(2,1)S(1)}, u32[]{:S(2)}, u32[]{:S(2)}) collective-permute-start(bf16[512,1024]{1,0:T(8,128)(2,1)S(1)} %get-tuple-element.75.refs_0_), channel_id=1, source_target_pairs={{0,64},{1,193},{2,66},{3,195},{64,128},{65,1},{66,130},{67,3},{128... | collective-permute-start | bytes 3145736 | tf_op jit(solution)/shard_map/ppermute | solution.py:265
  15.8 1.2 %shard_map.57 = (bf16[512,1024]{1,0:T(8,128)(2,1)S(1)}, f32[2,4,8,128]{3,2,1,0:T(8,128)S(1)}) custom-call(s32[4]{0:T(128)S(1)} %pad_add_fusion.place_ref, s32[4,16]{1,0:T(4,128)S(1)} %bitcast.23, bf16[512,2048]{1,0:T(8,128)(2,1)S(1)} %bitcast.20), custom_call_target="tpu_custom_call" | custom-call | flops 1 | bytes 1 | tf_op jit(solution)/shard_map/pallas_call | solution.py:42
  17.1 1.3 %collective-permute-start = (f32[12,128]{1,0:T(8,128)S(1)}, f32[12,128]{1,0:T(8,128)S(1)}, u32[]{:S(2)}, u32[]{:S(2)}) collective-permute-start(f32[12,128]{1,0:T(8,128)S(1)} %pad_maximum_fusion), channel_id=1, source_target_pairs={{0,16},{4,20},{8,24},{12,28},{16,0},{20,4},{24,8},{28,12},{32,48},... | collective-permute-start | bytes 18440 | tf_op jit(solution)/shard_map/ppermute | solution.py:265
  18.9 1.1 collective-permute-done
  20.0 2.7 %collective-permute-start.1 = (f32[12,128]{1,0:T(8,128)S(1)}, f32[12,128]{1,0:T(8,128)S(1)}, u32[]{:S(2)}, u32[]{:S(2)}) collective-permute-start(f32[12,128]{1,0:T(8,128)S(1)} %fusion.2), channel_id=1, source_target_pairs={{0,32},{4,36},{8,40},{12,44},{16,48},{20,52},{24,56},{28,60},{32,0... | collective-permute-start | bytes 18440 | tf_op jit(solution)/shard_map/ppermute | solution.py:265
  22.8 1.2 %collective-permute-done.1 = f32[12,128]{1,0:T(8,128)S(1)} collective-permute-done((f32[12,128]{1,0:T(8,128)S(1)}, f32[12,128]{1,0:T(8,128)S(1)}, u32[]{:S(2)}, u32[]{:S(2)}) %collective-permute-start.1) | collective-permute-done | bytes 6176 | tf_op jit(solution)/shard_map/ppermute | solution.py:265
  24.0 1.5 %collective-permute-start.5 = (bf16[512,128]{1,0:T(8,128)(2,1)S(1)}, bf16[512,128]{1,0:T(8,128)(2,1)S(1)}, u32[]{:S(2)}, u32[]{:S(2)}) collective-permute-start(bf16[512,128]{1,0:T(8,128)(2,1)S(1)} %slice.54), channel_id=1, source_target_pairs={{0,4},{4,8},{8,12},{12,0},{16,20},{20,24},{24,28},{28,16},{32,36},... | collective-permute-start | bytes 393224 | tf_op jit(solution)/shard_map/ppermute | solution.py:265
  25.5 2.2 %collective-permute-start.6 = (bf16[512,128]{1,0:T(8,128)(2,1)S(1)}, bf16[512,128]{1,0:T(8,128)(2,1)S(1)}, u32[]{:S(2)}, u32[]{:S(2)}) collective-permute-start(bf16[512,128]{1,0:T(8,128)(2,1)S(1)} %slice.55), channel_id=1, source_target_pairs={{0,12},{4,0},{8,4},{12,8},{16,28},{20,16},{24,20},{28,24},{32,44},... | collective-permute-start | bytes 393224 | tf_op jit(solution)/shard_map/ppermute | solution.py:265
  27.7 1.2 %collective-permute-start.4 = (f32[12,128]{1,0:T(8,128)S(1)}, f32[12,128]{1,0:T(8,128)S(1)}, u32[]{:S(2)}, u32[]{:S(2)}) collective-permute-start(f32[12,128]{1,0:T(8,128)S(1)} %add.37), channel_id=1, source_target_pairs={{0,4},{4,0},{8,12},{12,8},{16,20},{20,16},{24,28},{28,24},{32,36},... | collective-permute-start | bytes 18440 | tf_op jit(solution)/shard_map/ppermute | solution.py:265
  28.9 4.9 %collective-permute-done.4 = f32[12,128]{1,0:T(8,128)S(1)} collective-permute-done((f32[12,128]{1,0:T(8,128)S(1)}, f32[12,128]{1,0:T(8,128)S(1)}, u32[]{:S(2)}, u32[]{:S(2)}) %collective-permute-start.4) | collective-permute-done | bytes 6176 | tf_op jit(solution)/shard_map/ppermute | solution.py:265
  34.2 2.1 %collective-permute-start.14 = (bf16[1024,512]{1,0:T(8,128)(2,1)S(1)}, bf16[1024,512]{1,0:T(8,128)(2,1)S(1)}, u32[]{:S(2)}, u32[]{:S(2)}) collective-permute-start(bf16[1024,512]{1,0:T(8,128)(2,1)S(1)} %shard_map.58.own_ref), channel_id=1, source_target_pairs={{0,16},{4,20},{8,24},{12,28},{16,32},{20,36},{24,40},{28,44},{32,4... | collective-permute-start | bytes 3145736 | tf_op jit(solution)/shard_map/ppermute | solution.py:265
  37.0 1.8 %collective-permute-done.7.refs_1_ = bf16[512,1024]{1,0:T(8,128)(2,1)S(1)} collective-permute-done((bf16[512,1024]{1,0:T(8,128)(2,1)S(1)}, bf16[512,1024]{1,0:T(8,128)(2,1)S(1)}, u32[]{:S(2)}, u32[]{:S(2)}) %collective-permute-start.7) | collective-permute-done | bytes 1048608 | tf_op jit(solution)/shard_map/ppermute | solution.py:265
  38.7 4.4 %collective-permute-start.8 = (f32[12,128]{1,0:T(8,128)S(1)}, f32[12,128]{1,0:T(8,128)S(1)}, u32[]{:S(2)}, u32[]{:S(2)}) collective-permute-start(f32[12,128]{1,0:T(8,128)S(1)} %add.38), channel_id=1, source_target_pairs={{0,8},{4,12},{8,0},{12,4},{16,24},{20,28},{24,16},{28,20},{32,40},... | collective-permute-start | bytes 18440 | tf_op jit(solution)/shard_map/ppermute | solution.py:265
  43.1 2.0 %collective-permute-done.8 = f32[12,128]{1,0:T(8,128)S(1)} collective-permute-done((f32[12,128]{1,0:T(8,128)S(1)}, f32[12,128]{1,0:T(8,128)S(1)}, u32[]{:S(2)}, u32[]{:S(2)}) %collective-permute-start.8) | collective-permute-done | bytes 6176 | tf_op jit(solution)/shard_map/ppermute | solution.py:265
  45.2 4.8 %collective-permute-done.10.refs_2_ = bf16[512,1024]{1,0:T(8,128)(2,1)S(1)} collective-permute-done((bf16[512,1024]{1,0:T(8,128)(2,1)S(1)}, bf16[512,1024]{1,0:T(8,128)(2,1)S(1)}, u32[]{:S(2)}, u32[]{:S(2)}) %collective-permute-start.10) | collective-permute-done | bytes 1048608 | tf_op jit(solution)/shard_map/ppermute | solution.py:265
  50.0 0.8 collective-permute-start.13
  50.7 3.8 %collective-permute-start.12 = (f32[4,128]{1,0:T(4,128)S(1)}, f32[4,128]{1,0:T(4,128)S(1)}, u32[]{:S(2)}, u32[]{:S(2)}) collective-permute-start(f32[4,128]{1,0:T(4,128)S(1)} %fusion.1), channel_id=1, source_target_pairs={{0,128},{1,129},{2,130},{3,131},{64,192},{65,193},{66,194},{67,195... | collective-permute-start | bytes 6152 | tf_op jit(solution)/shard_map/ppermute | solution.py:265
  54.7 0.9 collective-permute-done.12
  55.6 1.7 %collective-permute-done.11 = f32[4,128]{1,0:T(4,128)S(1)} collective-permute-done((f32[4,128]{1,0:T(4,128)S(1)}, f32[4,128]{1,0:T(4,128)S(1)}, u32[]{:S(2)}, u32[]{:S(2)}) %collective-permute-start.11) | collective-permute-done | bytes 2080 | tf_op jit(solution)/shard_map/ppermute | solution.py:265
  57.3 1.2 %collective-permute-start.19 = (bf16[512,1024]{1,0:T(8,128)(2,1)S(1)}, bf16[512,1024]{1,0:T(8,128)(2,1)S(1)}, u32[]{:S(2)}, u32[]{:S(2)}) collective-permute-start(bf16[512,1024]{1,0:T(8,128)(2,1)S(1)} %collective-permute-done.10.refs_2_), channel_id=1, source_target_pairs={{0,64},{1,193},{2,66},{3,195},{64,128},{65,1},{66,130},{67,3},{128... | collective-permute-start | bytes 3145736 | tf_op jit(solution)/shard_map/ppermute | solution.py:265
  58.6 0.8 collective-permute-start.16
  59.5 4.0 %collective-permute-start.17 = (f32[8,128]{1,0:T(8,128)S(1)}, f32[8,128]{1,0:T(8,128)S(1)}, u32[]{:S(2)}, u32[]{:S(2)}) collective-permute-start(f32[8,128]{1,0:T(8,128)S(1)} %slice.58), channel_id=1, source_target_pairs={{0,1},{1,0},{2,3},{3,2},{4,5},{5,4},{6,7},{7,6},{8,9},{9,8},{10,11... | collective-permute-start | bytes 12296 | tf_op jit(solution)/shard_map/ppermute | solution.py:265
  63.5 1.5 %collective-permute-start.20 = (bf16[512,512]{1,0:T(8,128)(2,1)S(1)}, bf16[512,512]{1,0:T(8,128)(2,1)S(1)}, u32[]{:S(2)}, u32[]{:S(2)}) collective-permute-start(bf16[512,512]{1,0:T(8,128)(2,1)S(1)} %slice.59), channel_id=1, source_target_pairs={{0,48},{4,52},{8,56},{12,60},{16,0},{20,4},{24,8},{28,12},{32,16},... | collective-permute-start | bytes 1572872 | tf_op jit(solution)/shard_map/ppermute | solution.py:265
  64.9 0.8 collective-permute-start.21
  65.8 0.8 collective-permute-start.18
  66.6 1.4 %shard_map.59.full_ref = bf16[4,1024,512]{2,1,0:T(8,128)(2,1)S(1)} custom-call(s32[4]{0:T(128)S(1)} %pad_add_fusion.place_ref, f32[4,4,128]{2,1,0:T(4,128)S(1)} %pad_maximum_fusion.1.scale_ref, bf16[1024,512]{1,0:T(8,128)(2,1)S(1)} %shard_map.58.own_ref, bf16[1024,512]{1,0:T(8,128)(2,1)S(1)} %collective-permute-done.14.r_ref, ...), custom_call_target="tpu_custom_call" | custom-call | flops 1 | bytes 1 | tf_op jit(solution)/shard_map/pallas_call | solution.py:126
  68.6 1.4 %collective-permute-done.16.piece_ref = bf16[512,512]{1,0:T(8,128)(2,1)S(1)} collective-permute-done((bf16[512,512]{1,0:T(8,128)(2,1)S(1)}, bf16[512,512]{1,0:T(8,128)(2,1)S(1)}, u32[]{:S(2)}, u32[]{:S(2)}) %collective-permute-start.16) | collective-permute-done | bytes 524320 | tf_op jit(solution)/shard_map/ppermute | solution.py:265
  70.0 1.2 %collective-permute-done.19.refs_3_ = bf16[512,1024]{1,0:T(8,128)(2,1)S(1)} collective-permute-done((bf16[512,1024]{1,0:T(8,128)(2,1)S(1)}, bf16[512,1024]{1,0:T(8,128)(2,1)S(1)}, u32[]{:S(2)}, u32[]{:S(2)}) %collective-permute-start.19) | collective-permute-done | bytes 1048608 | tf_op jit(solution)/shard_map/ppermute | solution.py:265
  71.3 2.3 %shard_map.60 = (bf16[4,1024,512]{2,1,0:T(8,128)(2,1)S(1)}, bf16[512,512]{1,0:T(8,128)(2,1)S(1)}) custom-call(s32[4]{0:T(128)S(1)} %pad_add_fusion.place_ref, f32[4,4,128]{2,1,0:T(4,128)S(1)} %pad_maximum_fusion.1.scale_ref, bf16[4,1024,512]{2,1,0:T(8,128)(2,1)S(1)} %shard_map.59.full_ref, ...), custom_call_target="tpu_custom_call", output_to_operand_aliasing={{0}: (2, {})} | custom-call | flops 1 | bytes 1 | tf_op jit(solution)/shard_map/pallas_call | solution.py:161
  73.6 4.5 %collective-permute-start.22 = (bf16[512,512]{1,0:T(8,128)(2,1)S(1)}, bf16[512,512]{1,0:T(8,128)(2,1)S(1)}, u32[]{:S(2)}, u32[]{:S(2)}) collective-permute-start(bf16[512,512]{1,0:T(8,128)(2,1)S(1)} %get-tuple-element.73), channel_id=1, source_target_pairs={{0,1},{1,0},{2,3},{3,2},{4,5},{5,4},{6,7},{7,6},{8,9},{9,8},{10,11... | collective-permute-start | bytes 1572872 | tf_op jit(solution)/shard_map/ppermute | solution.py:265
  78.1 2.3 %shard_map.61 = (bf16[4,1024,512]{2,1,0:T(8,128)(2,1)S(1)}, bf16[512,512]{1,0:T(8,128)(2,1)S(1)}) custom-call(s32[4]{0:T(128)S(1)} %pad_add_fusion.place_ref, f32[4,4,128]{2,1,0:T(4,128)S(1)} %pad_maximum_fusion.1.scale_ref, bf16[4,1024,512]{2,1,0:T(8,128)(2,1)S(1)} %get-tuple-element.67.full_ref, ...), custom_call_target="tpu_custom_call", output_to_operand_aliasing={{0}: (2, {})} | custom-call | flops 1 | bytes 1 | tf_op jit(solution)/shard_map/pallas_call | solution.py:161
  80.6 1.8 %shard_map.62 = bf16[512,512]{1,0:T(8,128)(2,1)S(1)} custom-call(bf16[4,1024,512]{2,1,0:T(8,128)(2,1)S(1)} %get-tuple-element.69.full_ref, bf16[512,512]{1,0:T(8,128)(2,1)S(1)} %collective-permute-done.22.core_ref, bf16[512,1024]{1,0:T(8,128)(2,1)S(1)} %get-tuple-element.75.refs_0_, bf16[512,1024]{1,0:T(8,128)(2,1)S(1)} %collective-permute-done.9.refs_1_, ...), custom_call_target="tpu_custom_call" | custom-call | flops 1 | bytes 1 | tf_op jit(solution)/shard_map/pallas_call | solution.py:187
  82.5 1.7 %shard_map.63 = bf16[512,512]{1,0:T(8,128)(2,1)S(1)} custom-call(bf16[4,1024,512]{2,1,0:T(8,128)(2,1)S(1)} %get-tuple-element.69.full_ref, bf16[512,512]{1,0:T(8,128)(2,1)S(1)} %collective-permute-done.23.core_ref, bf16[512,1024]{1,0:T(8,128)(2,1)S(1)} %get-tuple-element.75.refs_0_, bf16[512,1024]{1,0:T(8,128)(2,1)S(1)} %collective-permute-done.9.refs_1_, ...), custom_call_target="tpu_custom_call" | custom-call | flops 1 | bytes 1 | tf_op jit(solution)/shard_map/pallas_call | solution.py:187
  84.7 0.7 collective-permute-start.27
  85.5 0.7 collective-permute-start.28
  86.2 12.1 %collective-permute-done.24.refs_3_ = bf16[512,1024]{1,0:T(8,128)(2,1)S(1)} collective-permute-done((bf16[512,1024]{1,0:T(8,128)(2,1)S(1)}, bf16[512,1024]{1,0:T(8,128)(2,1)S(1)}, u32[]{:S(2)}, u32[]{:S(2)}) %collective-permute-start.24) | collective-permute-done | bytes 1048608 | tf_op jit(solution)/shard_map/ppermute | solution.py:265
  98.3 6.7 %shard_map.64 = (bf16[512,512]{1,0:T(8,128)(2,1)}, bf16[512,512]{1,0:T(8,128)(2,1)}, bf16[1024,512]{1,0:T(8,128)(2,1)S(1)}) custom-call(bf16[4,1024,512]{2,1,0:T(8,128)(2,1)S(1)} %get-tuple-element.69.full_ref, bf16[512,1024]{1,0:T(8,128)(2,1)S(1)} %get-tuple-element.55.refs_0_, bf16[512,1024]{1,0:T(8,128)(2,1)S(1)} %collective-permute-done.7.refs_1_, ...), custom_call_target="tpu_custom_call" | custom-call | flops 1 | bytes 1 | tf_op jit(solution)/shard_map/pallas_call | solution.py:211
  105.0 4.7 %collective-permute-start.25 = (bf16[512,512]{1,0:T(8,128)(2,1)}, bf16[512,512]{1,0:T(8,128)(2,1)}, u32[]{:S(2)}, u32[]{:S(2)}) collective-permute-start(bf16[512,512]{1,0:T(8,128)(2,1)} %get-tuple-element.80), channel_id=1, source_target_pairs={{0,1},{1,0},{2,3},{3,2},{4,5},{5,4},{6,7},{7,6},{8,9},{9,8},{10,11... | collective-permute-start | bytes 1572872 | tf_op jit(solution)/shard_map/ppermute | solution.py:265
  109.8 1.8 %collective-permute-done.25.core0_ref = bf16[512,512]{1,0:T(8,128)(2,1)} collective-permute-done((bf16[512,512]{1,0:T(8,128)(2,1)}, bf16[512,512]{1,0:T(8,128)(2,1)}, u32[]{:S(2)}, u32[]{:S(2)}) %collective-permute-start.25) | collective-permute-done | bytes 524320 | tf_op jit(solution)/shard_map/ppermute | solution.py:265
  111.5 0.7 collective-permute-done.26.core1_ref
  112.3 3.5 %shard_map.65 = bf16[1024,512]{1,0:T(8,128)(2,1)} custom-call(s32[8,4]{1,0:T(8,128)S(1)} %copy.13.flags_ref, bf16[1024,512]{1,0:T(8,128)(2,1)S(1)} %get-tuple-element.78.part_ref, bf16[512,512]{1,0:T(8,128)(2,1)} %collective-permute-done.25.core0_ref, bf16[512,512]{1,0:T(8,128)(2,1)} %collective-permute-done.26.core1_ref, ...), custom_call_target="tpu_custom_call" | custom-call | flops 1 | bytes 1 | tf_op jit(solution)/shard_map/pallas_call | solution.py:243
  (53 shorter events, 3.9 us)
Async XLA Ops:
  0.0 0.9 copy-start.1
  1.0 0.7 copy-start.3
  2.4 20.4 %collective-permute-start.2 = (bf16[1024,128]{1,0:T(8,128)(2,1)S(1)}, bf16[1024,128]{1,0:T(8,128)(2,1)S(1)}, u32[]{:S(2)}, u32[]{:S(2)}) collective-permute-start(bf16[1024,128]{1,0:T(8,128)(2,1)S(1)} %get-tuple-element.60.own_ref), channel_id=1, source_target_pairs={{0,4},{4,8},{8,12},{12,0},{16,20},{20,24},{24,28},{28,16},{32,36},... | collective-permute-start | bytes 786440 | tf_op jit(solution)/shard_map/ppermute | solution.py:265
  6.3 17.8 %collective-permute-start.3 = (bf16[1024,128]{1,0:T(8,128)(2,1)S(1)}, bf16[1024,128]{1,0:T(8,128)(2,1)S(1)}, u32[]{:S(2)}, u32[]{:S(2)}) collective-permute-start(bf16[1024,128]{1,0:T(8,128)(2,1)S(1)} %get-tuple-element.60.own_ref), channel_id=1, source_target_pairs={{0,12},{4,0},{8,4},{12,8},{16,28},{20,16},{24,20},{28,24},{32,44},... | collective-permute-start | bytes 786440 | tf_op jit(solution)/shard_map/ppermute | solution.py:265
  9.5 1.6 %copy-start = (bf16[1,512,2048]{2,1,0:T(8,128)(2,1)S(1)}, bf16[1,512,2048]{2,1,0:T(8,128)(2,1)}, u32[]{:S(2)}) copy-start(bf16[1,512,2048]{2,1,0:T(8,128)(2,1)} %param.7) | copy-start | bytes 6291460
  11.1 0.7 copy-start.2
  13.0 20.8 %collective-permute-start.9 = (bf16[512,1024]{1,0:T(8,128)(2,1)S(1)}, bf16[512,1024]{1,0:T(8,128)(2,1)S(1)}, u32[]{:S(2)}, u32[]{:S(2)}) collective-permute-start(bf16[512,1024]{1,0:T(8,128)(2,1)S(1)} %get-tuple-element.75.refs_0_), channel_id=1, source_target_pairs={{0,64},{1,193},{2,66},{3,195},{64,128},{65,1},{66,130},{67,3},{128... | collective-permute-start | bytes 3145736 | tf_op jit(solution)/shard_map/ppermute | solution.py:265
  17.1 2.9 %collective-permute-start = (f32[12,128]{1,0:T(8,128)S(1)}, f32[12,128]{1,0:T(8,128)S(1)}, u32[]{:S(2)}, u32[]{:S(2)}) collective-permute-start(f32[12,128]{1,0:T(8,128)S(1)} %pad_maximum_fusion), channel_id=1, source_target_pairs={{0,16},{4,20},{8,24},{12,28},{16,0},{20,4},{24,8},{28,12},{32,48},... | collective-permute-start | bytes 18440 | tf_op jit(solution)/shard_map/ppermute | solution.py:265
  18.4 20.3 %collective-permute-start.7 = (bf16[512,1024]{1,0:T(8,128)(2,1)S(1)}, bf16[512,1024]{1,0:T(8,128)(2,1)S(1)}, u32[]{:S(2)}, u32[]{:S(2)}) collective-permute-start(bf16[512,1024]{1,0:T(8,128)(2,1)S(1)} %get-tuple-element.55.refs_0_), channel_id=1, source_target_pairs={{0,64},{1,193},{2,66},{3,195},{64,128},{65,1},{66,130},{67,3},{128... | collective-permute-start | bytes 3145736 | tf_op jit(solution)/shard_map/ppermute | solution.py:265
  20.0 4.0 %collective-permute-start.1 = (f32[12,128]{1,0:T(8,128)S(1)}, f32[12,128]{1,0:T(8,128)S(1)}, u32[]{:S(2)}, u32[]{:S(2)}) collective-permute-start(f32[12,128]{1,0:T(8,128)S(1)} %fusion.2), channel_id=1, source_target_pairs={{0,32},{4,36},{8,40},{12,44},{16,48},{20,52},{24,56},{28,60},{32,0... | collective-permute-start | bytes 18440 | tf_op jit(solution)/shard_map/ppermute | solution.py:265
  24.0 9.8 %collective-permute-start.5 = (bf16[512,128]{1,0:T(8,128)(2,1)S(1)}, bf16[512,128]{1,0:T(8,128)(2,1)S(1)}, u32[]{:S(2)}, u32[]{:S(2)}) collective-permute-start(bf16[512,128]{1,0:T(8,128)(2,1)S(1)} %slice.54), channel_id=1, source_target_pairs={{0,4},{4,8},{8,12},{12,0},{16,20},{20,24},{24,28},{28,16},{32,36},... | collective-permute-start | bytes 393224 | tf_op jit(solution)/shard_map/ppermute | solution.py:265
  25.5 8.3 %collective-permute-start.6 = (bf16[512,128]{1,0:T(8,128)(2,1)S(1)}, bf16[512,128]{1,0:T(8,128)(2,1)S(1)}, u32[]{:S(2)}, u32[]{:S(2)}) collective-permute-start(bf16[512,128]{1,0:T(8,128)(2,1)S(1)} %slice.55), channel_id=1, source_target_pairs={{0,12},{4,0},{8,4},{12,8},{16,28},{20,16},{24,20},{28,24},{32,44},... | collective-permute-start | bytes 393224 | tf_op jit(solution)/shard_map/ppermute | solution.py:265
  27.7 6.1 %collective-permute-start.4 = (f32[12,128]{1,0:T(8,128)S(1)}, f32[12,128]{1,0:T(8,128)S(1)}, u32[]{:S(2)}, u32[]{:S(2)}) collective-permute-start(f32[12,128]{1,0:T(8,128)S(1)} %add.37), channel_id=1, source_target_pairs={{0,4},{4,0},{8,12},{12,8},{16,20},{20,16},{24,28},{28,24},{32,36},... | collective-permute-start | bytes 18440 | tf_op jit(solution)/shard_map/ppermute | solution.py:265
  33.8 16.2 %collective-permute-start.10 = (bf16[512,1024]{1,0:T(8,128)(2,1)S(1)}, bf16[512,1024]{1,0:T(8,128)(2,1)S(1)}, u32[]{:S(2)}, u32[]{:S(2)}) collective-permute-start(bf16[512,1024]{1,0:T(8,128)(2,1)S(1)} %collective-permute-done.9.refs_1_), channel_id=1, source_target_pairs={{0,64},{1,193},{2,66},{3,195},{64,128},{65,1},{66,130},{67,3},{128... | collective-permute-start | bytes 3145736 | tf_op jit(solution)/shard_map/ppermute | solution.py:265
  34.2 24.3 %collective-permute-start.14 = (bf16[1024,512]{1,0:T(8,128)(2,1)S(1)}, bf16[1024,512]{1,0:T(8,128)(2,1)S(1)}, u32[]{:S(2)}, u32[]{:S(2)}) collective-permute-start(bf16[1024,512]{1,0:T(8,128)(2,1)S(1)} %shard_map.58.own_ref), channel_id=1, source_target_pairs={{0,16},{4,20},{8,24},{12,28},{16,32},{20,36},{24,40},{28,44},{32,4... | collective-permute-start | bytes 3145736 | tf_op jit(solution)/shard_map/ppermute | solution.py:265
  36.3 22.3 %collective-permute-start.15 = (bf16[1024,512]{1,0:T(8,128)(2,1)S(1)}, bf16[1024,512]{1,0:T(8,128)(2,1)S(1)}, u32[]{:S(2)}, u32[]{:S(2)}) collective-permute-start(bf16[1024,512]{1,0:T(8,128)(2,1)S(1)} %shard_map.58.own_ref), channel_id=1, source_target_pairs={{0,48},{4,52},{8,56},{12,60},{16,0},{20,4},{24,8},{28,12},{32,16},... | collective-permute-start | bytes 3145736 | tf_op jit(solution)/shard_map/ppermute | solution.py:265
  38.7 6.4 %collective-permute-start.8 = (f32[12,128]{1,0:T(8,128)S(1)}, f32[12,128]{1,0:T(8,128)S(1)}, u32[]{:S(2)}, u32[]{:S(2)}) collective-permute-start(f32[12,128]{1,0:T(8,128)S(1)} %add.38), channel_id=1, source_target_pairs={{0,8},{4,12},{8,0},{12,4},{16,24},{20,28},{24,16},{28,20},{32,40},... | collective-permute-start | bytes 18440 | tf_op jit(solution)/shard_map/ppermute | solution.py:265
  50.0 4.7 %collective-permute-start.13 = (f32[4,128]{1,0:T(4,128)S(1)}, f32[4,128]{1,0:T(4,128)S(1)}, u32[]{:S(2)}, u32[]{:S(2)}) collective-permute-start(f32[4,128]{1,0:T(4,128)S(1)} %fusion.1), channel_id=1, source_target_pairs={{0,192},{1,65},{2,194},{3,67},{64,0},{65,129},{66,2},{67,131},{128... | collective-permute-start | bytes 6152 | tf_op jit(solution)/shard_map/ppermute | solution.py:265
  50.7 4.8 %collective-permute-start.12 = (f32[4,128]{1,0:T(4,128)S(1)}, f32[4,128]{1,0:T(4,128)S(1)}, u32[]{:S(2)}, u32[]{:S(2)}) collective-permute-start(f32[4,128]{1,0:T(4,128)S(1)} %fusion.1), channel_id=1, source_target_pairs={{0,128},{1,129},{2,130},{3,131},{64,192},{65,193},{66,194},{67,195... | collective-permute-start | bytes 6152 | tf_op jit(solution)/shard_map/ppermute | solution.py:265
  54.6 2.7 %collective-permute-start.11 = (f32[4,128]{1,0:T(4,128)S(1)}, f32[4,128]{1,0:T(4,128)S(1)}, u32[]{:S(2)}, u32[]{:S(2)}) collective-permute-start(f32[4,128]{1,0:T(4,128)S(1)} %fusion.1), channel_id=1, source_target_pairs={{0,64},{1,193},{2,66},{3,195},{64,128},{65,1},{66,130},{67,3},{128... | collective-permute-start | bytes 6152 | tf_op jit(solution)/shard_map/ppermute | solution.py:265
  57.3 13.9 %collective-permute-start.19 = (bf16[512,1024]{1,0:T(8,128)(2,1)S(1)}, bf16[512,1024]{1,0:T(8,128)(2,1)S(1)}, u32[]{:S(2)}, u32[]{:S(2)}) collective-permute-start(bf16[512,1024]{1,0:T(8,128)(2,1)S(1)} %collective-permute-done.10.refs_2_), channel_id=1, source_target_pairs={{0,64},{1,193},{2,66},{3,195},{64,128},{65,1},{66,130},{67,3},{128... | collective-permute-start | bytes 3145736 | tf_op jit(solution)/shard_map/ppermute | solution.py:265
  58.6 11.4 %collective-permute-start.16 = (bf16[512,512]{1,0:T(8,128)(2,1)S(1)}, bf16[512,512]{1,0:T(8,128)(2,1)S(1)}, u32[]{:S(2)}, u32[]{:S(2)}) collective-permute-start(bf16[512,512]{1,0:T(8,128)(2,1)S(1)} %slice.57), channel_id=1, source_target_pairs={{0,16},{4,20},{8,24},{12,28},{16,32},{20,36},{24,40},{28,44},{32,4... | collective-permute-start | bytes 1572872 | tf_op jit(solution)/shard_map/ppermute | solution.py:265
  59.5 6.3 %collective-permute-start.17 = (f32[8,128]{1,0:T(8,128)S(1)}, f32[8,128]{1,0:T(8,128)S(1)}, u32[]{:S(2)}, u32[]{:S(2)}) collective-permute-start(f32[8,128]{1,0:T(8,128)S(1)} %slice.58), channel_id=1, source_target_pairs={{0,1},{1,0},{2,3},{3,2},{4,5},{5,4},{6,7},{7,6},{8,9},{9,8},{10,11... | collective-permute-start | bytes 12296 | tf_op jit(solution)/shard_map/ppermute | solution.py:265
  63.5 14.7 %collective-permute-start.20 = (bf16[512,512]{1,0:T(8,128)(2,1)S(1)}, bf16[512,512]{1,0:T(8,128)(2,1)S(1)}, u32[]{:S(2)}, u32[]{:S(2)}) collective-permute-start(bf16[512,512]{1,0:T(8,128)(2,1)S(1)} %slice.59), channel_id=1, source_target_pairs={{0,48},{4,52},{8,56},{12,60},{16,0},{20,4},{24,8},{28,12},{32,16},... | collective-permute-start | bytes 1572872 | tf_op jit(solution)/shard_map/ppermute | solution.py:265
  64.9 19.3 %collective-permute-start.21 = (bf16[512,1024]{1,0:T(8,128)(2,1)S(1)}, bf16[512,1024]{1,0:T(8,128)(2,1)S(1)}, u32[]{:S(2)}, u32[]{:S(2)}) collective-permute-start(bf16[512,1024]{1,0:T(8,128)(2,1)S(1)} %collective-permute-done.7.refs_1_), channel_id=1, source_target_pairs={{0,64},{1,193},{2,66},{3,195},{64,128},{65,1},{66,130},{67,3},{128... | collective-permute-start | bytes 3145736 | tf_op jit(solution)/shard_map/ppermute | solution.py:265
  65.8 2.8 %collective-permute-start.18 = (f32[8,128]{1,0:T(8,128)S(1)}, f32[8,128]{1,0:T(8,128)S(1)}, u32[]{:S(2)}, u32[]{:S(2)}) collective-permute-start(f32[8,128]{1,0:T(8,128)S(1)} %slice_add_fusion.4.sum_ref), channel_id=1, source_target_pairs={{0,2},{1,3},{2,0},{3,1},{4,6},{5,7},{6,4},{7,5},{8,10},{9,11},{10,... | collective-permute-start | bytes 12296 | tf_op jit(solution)/shard_map/ppermute | solution.py:265
  73.6 7.0 %collective-permute-start.22 = (bf16[512,512]{1,0:T(8,128)(2,1)S(1)}, bf16[512,512]{1,0:T(8,128)(2,1)S(1)}, u32[]{:S(2)}, u32[]{:S(2)}) collective-permute-start(bf16[512,512]{1,0:T(8,128)(2,1)S(1)} %get-tuple-element.73), channel_id=1, source_target_pairs={{0,1},{1,0},{2,3},{3,2},{4,5},{5,4},{6,7},{7,6},{8,9},{9,8},{10,11... | collective-permute-start | bytes 1572872 | tf_op jit(solution)/shard_map/ppermute | solution.py:265
  80.5 2.0 %collective-permute-start.23 = (bf16[512,512]{1,0:T(8,128)(2,1)S(1)}, bf16[512,512]{1,0:T(8,128)(2,1)S(1)}, u32[]{:S(2)}, u32[]{:S(2)}) collective-permute-start(bf16[512,512]{1,0:T(8,128)(2,1)S(1)} %get-tuple-element.74), channel_id=1, source_target_pairs={{0,1},{1,0},{2,3},{3,2},{4,5},{5,4},{6,7},{7,6},{8,9},{9,8},{10,11... | collective-permute-start | bytes 1572872 | tf_op jit(solution)/shard_map/ppermute | solution.py:265
  84.2 25.4 %copy-start.4 = (s32[8,4]{0,1:T(4,128)S(1)}, s32[8,4]{0,1:T(4,128)}, u32[]{:S(2)}) copy-start(s32[8,4]{0,1:T(4,128)} %param.9) | copy-start | bytes 388
  84.2 14.0 %collective-permute-start.24 = (bf16[512,1024]{1,0:T(8,128)(2,1)S(1)}, bf16[512,1024]{1,0:T(8,128)(2,1)S(1)}, u32[]{:S(2)}, u32[]{:S(2)}) collective-permute-start(bf16[512,1024]{1,0:T(8,128)(2,1)S(1)} %collective-permute-done.21.refs_2_), channel_id=1, source_target_pairs={{0,64},{1,193},{2,66},{3,195},{64,128},{65,1},{66,130},{67,3},{128... | collective-permute-start | bytes 3145736 | tf_op jit(solution)/shard_map/ppermute | solution.py:265
  84.7 25.0 %collective-permute-start.27 = (bf16[512,512]{1,0:T(8,128)(2,1)S(1)}, bf16[512,512]{1,0:T(8,128)(2,1)S(1)}, u32[]{:S(2)}, u32[]{:S(2)}) collective-permute-start(bf16[512,512]{1,0:T(8,128)(2,1)S(1)} %shard_map.62), channel_id=1, source_target_pairs={{0,2},{1,3},{2,0},{3,1},{4,6},{5,7},{6,4},{7,5},{8,10},{9,11},{10,... | collective-permute-start | bytes 1572872 | tf_op jit(solution)/shard_map/ppermute | solution.py:265
  85.5 24.3 %collective-permute-start.28 = (bf16[512,512]{1,0:T(8,128)(2,1)S(1)}, bf16[512,512]{1,0:T(8,128)(2,1)S(1)}, u32[]{:S(2)}, u32[]{:S(2)}) collective-permute-start(bf16[512,512]{1,0:T(8,128)(2,1)S(1)} %shard_map.63), channel_id=1, source_target_pairs={{0,2},{1,3},{2,0},{3,1},{4,6},{5,7},{6,4},{7,5},{8,10},{9,11},{10,... | collective-permute-start | bytes 1572872 | tf_op jit(solution)/shard_map/ppermute | solution.py:265
  105.0 6.6 %collective-permute-start.25 = (bf16[512,512]{1,0:T(8,128)(2,1)}, bf16[512,512]{1,0:T(8,128)(2,1)}, u32[]{:S(2)}, u32[]{:S(2)}) collective-permute-start(bf16[512,512]{1,0:T(8,128)(2,1)} %get-tuple-element.80), channel_id=1, source_target_pairs={{0,1},{1,0},{2,3},{3,2},{4,5},{5,4},{6,7},{7,6},{8,9},{9,8},{10,11... | collective-permute-start | bytes 1572872 | tf_op jit(solution)/shard_map/ppermute | solution.py:265
  109.7 2.6 %collective-permute-start.26 = (bf16[512,512]{1,0:T(8,128)(2,1)}, bf16[512,512]{1,0:T(8,128)(2,1)}, u32[]{:S(2)}, u32[]{:S(2)}) collective-permute-start(bf16[512,512]{1,0:T(8,128)(2,1)} %get-tuple-element.82), channel_id=1, source_target_pairs={{0,1},{1,0},{2,3},{3,2},{4,5},{5,4},{6,7},{7,6},{8,9},{9,8},{10,11... | collective-permute-start | bytes 1572872 | tf_op jit(solution)/shard_map/ppermute | solution.py:265
